TPU v7x, 256 devices: a whole 4x4x8 slice. The times are simulated.
256 devices in a mesh: ens: 8 (over y, z_hi), tile: 32 (over z_lo, x, core).
Axes of the slice: x: 4, y: 4, z: 8 (z_hi: 2, z_lo: 4; z = z_hi * 4 + z_lo), core: 2. Of those that a mesh axis runs over, the one named last changes fastest.
Arguments:
- fields: bfloat16 [8, 32, 200, 8, 128], P('ens', 'tile'), may hold values from -6 to 6
- target: bfloat16 [8, 32, 200, 8, 128], P('ens', 'tile'), may hold values from -6 to 6
- wet_levels: int32 [32, 8, 128], P('tile'), may hold values from 0 to 19, as said below
- tile_links: int32 [32, 5], replicated, may hold values from -1 to 31, as said below
- tile_owner: int32 [32], replicated, may hold values from 0 to 31, as said below
- kernel: float32 [200, 49], replicated, may hold values from -0.875 to 0.875
- norm_gain: float32 [200], replicated, may hold values from 0.5 to 1.5
- weight_in: bfloat16 [200, 800], replicated, may hold values from -0.4375 to 0.4375
- weight_out: bfloat16 [800, 200], replicated, may hold values from -0.21875 to 0.21875
- layer_scale: float32 [200], replicated, may hold values from 0.25 to 1
Outputs:
- block_out: bfloat16 [8, 32, 200, 8, 128], P('ens', 'tile')
- grad_in: float32 [200, 800], replicated
- grad_out: float32 [800, 200], replicated
- grad_kernel: float32 [200, 49], replicated
Inputs may be any that keep to these rules, and one draw needn't show every extreme that they name: `wet_levels`: 0 is land; a cell is wet at the levels below its value. `tile_links`: the kept tiles are the kept blocks of a grid 8 tiles wide, numbered row by row from the south. West and east wrap around within a grid row; the southmost row has no south neighbour; the northmost row is complete, its north neighbour is the tile of the same row in the mirrored column 7 - column, and only it has flag 1 in column 4; -1 marks a missing neighbour. Column 4 is 0 or 1. `tile_owner`: a permutation.
All inputs are finite; a program needn't handle non-finite values.
Results may differ from a plain program's by a relative error of at most 0.005.
Values may be sent and summed in bfloat16 or wider, within the bound.
No kernel may reach another device: no remote copies, remote signals or barrier semaphores. Data moves between devices by JAX's collectives and lax.ppermute only.
A program may use at most 192 MiB of HBM per device.

v0:
```python
import jax
import jax.numpy as jnp
from jax import lax
from jax.sharding import PartitionSpec as P

LEVELS = 19


root_half = 0.7071067811865476
gauss_norm = 0.3989422804014327
norm_epsilon = 1e-06


def gelu_value(values):
    return 0.5 * values * (1.0 + lax.erf(values * root_half))


def gelu_slope(values):
    return (
        0.5 * (1.0 + lax.erf(values * root_half))
        + values * jnp.exp(-0.5 * values * values) * gauss_norm
    )


def take_slot(held, pieces, slot_id):
    piece_count = pieces.shape[0]
    inside = (slot_id >= 0) & (slot_id >= 0) & (slot_id < piece_count)
    taken = lax.dynamic_index_in_dim(
        pieces, jnp.clip(slot_id, 0, piece_count - 1), 0, keepdims=False
    )
    return jnp.where(inside, taken, held)


def local(
    fields,
    target,
    wet_levels,
    tile_links,
    tile_owner,
    kernel,
    norm_gain,
    weight_in,
    weight_out,
    layer_scale,
):
    members, _, channels, row_count, col_count = fields.shape
    tile_count = tile_owner.shape[0]
    own_slot = lax.axis_index("tile")
    own_tile = jnp.sum(
        jnp.where(tile_owner == own_slot, jnp.arange(tile_count, dtype=jnp.int32), 0)
    )
    level_of = jnp.arange(channels, dtype=jnp.int32) * LEVELS // channels
    wet_mask = wet_levels[0][None, :, :] > level_of[:, None, None]
    own_input = fields[:, 0]
    masked = jnp.where(wet_mask[None], own_input, jnp.zeros_like(own_input))
    entry_total = jnp.float32(
        members * lax.axis_size("ens") * tile_count * channels * row_count * col_count
    )

    def link_of(tile_id, column):
        return jnp.where(tile_id >= 0, tile_links[jnp.clip(tile_id, 0, tile_count - 1), column], -1)

    def slot_of(tile_id):
        return jnp.where(tile_id >= 0, tile_owner[jnp.clip(tile_id, 0, tile_count - 1)], -1)

    north_slot = slot_of(link_of(own_tile, 0))
    south_slot = slot_of(link_of(own_tile, 1))
    own_fold = link_of(own_tile, 4)
    west_tile = link_of(own_tile, 2)
    east_tile = link_of(own_tile, 3)
    west_slot = slot_of(west_tile)
    east_slot = slot_of(east_tile)
    zero_rows = jnp.zeros((members, channels, 3, col_count), jnp.bfloat16)
    row_strips = jnp.stack([masked[:, :, :3, :], masked[:, :, row_count - 3 :, :]], axis=0)[None]
    held = (zero_rows, zero_rows, zero_rows)
    pieces = lax.all_gather(row_strips, "tile", axis=0, tiled=True)
    lower_rows = take_slot(held[0], pieces[:, 0], north_slot)
    upper_rows = take_slot(held[1], pieces[:, 1], north_slot)
    below_rows = take_slot(held[2], pieces[:, 1], south_slot)
    north_rows = jnp.where(own_fold == 1, jnp.flip(upper_rows, (2, 3)), lower_rows)
    center = jnp.concatenate([below_rows, masked, north_rows], axis=2)
    side_cols = jnp.swapaxes(
        jnp.stack([center[..., :3], center[..., col_count - 3 :]], axis=0), 3, 4
    )[None]
    zero_cols = jnp.zeros((members, channels, 3, row_count + 6), jnp.bfloat16)
    held = (zero_cols, zero_cols)
    pieces = lax.all_gather(side_cols, "tile", axis=0, tiled=True)
    west_part = take_slot(held[0], pieces[:, 1], west_slot)
    east_part = take_slot(held[1], pieces[:, 0], east_slot)
    west_cols = jnp.swapaxes(west_part, 2, 3)
    east_cols = jnp.swapaxes(east_part, 2, 3)
    extended = jnp.concatenate([west_cols, center, east_cols], axis=3).astype(jnp.float32)
    conv_out = jnp.zeros((members, channels, row_count, col_count), jnp.float32)
    for row_off in range(7):
        for col_off in range(7):
            conv_out = (
                conv_out
                + kernel[:, 7 * row_off + col_off][None, :, None, None]
                * extended[:, :, row_off : row_off + row_count, col_off : col_off + col_count]
            )
    chan_mean = jnp.mean(conv_out, axis=1, keepdims=True)
    chan_var = jnp.mean((conv_out - chan_mean) ** 2, axis=1, keepdims=True)
    inv_std = 1.0 / jnp.sqrt(chan_var + norm_epsilon)
    centred = (conv_out - chan_mean) * inv_std
    gain_wide = norm_gain[None, :, None, None]
    scale_wide = layer_scale[None, :, None, None]
    normed = (centred * gain_wide).astype(jnp.bfloat16)
    flat_norm = normed.reshape(members, channels, row_count * col_count)
    hidden = jnp.einsum("ch,ecp->ehp", weight_in, flat_norm, preferred_element_type=jnp.float32)
    activated = gelu_value(hidden).astype(jnp.bfloat16)
    mlp_out = jnp.einsum("hc,ehp->ecp", weight_out, activated, preferred_element_type=jnp.float32)
    mlp_out = mlp_out.reshape(members, channels, row_count, col_count)
    block_out = (masked.astype(jnp.float32) + scale_wide * mlp_out).astype(jnp.bfloat16)
    misfit = jnp.where(
        wet_mask[None], block_out.astype(jnp.float32) - target[:, 0].astype(jnp.float32), 0.0
    )
    grad_mlp = (
        (2.0 * scale_wide * misfit)
        .astype(jnp.bfloat16)
        .reshape(members, channels, row_count * col_count)
    )
    part_out = jnp.einsum("ehp,ecp->hc", activated, grad_mlp, preferred_element_type=jnp.float32)
    grad_act = jnp.einsum("hc,ecp->ehp", weight_out, grad_mlp, preferred_element_type=jnp.float32)
    grad_hidden = (grad_act * gelu_slope(hidden)).astype(jnp.bfloat16)
    part_in = jnp.einsum("ecp,ehp->ch", flat_norm, grad_hidden, preferred_element_type=jnp.float32)
    grad_normed = jnp.einsum(
        "ch,ehp->ecp", weight_in, grad_hidden, preferred_element_type=jnp.float32
    )
    grad_scaled = grad_normed.reshape(members, channels, row_count, col_count) * gain_wide
    grad_conv = (
        grad_scaled
        - jnp.mean(grad_scaled, axis=1, keepdims=True)
        - centred * jnp.mean(grad_scaled * centred, axis=1, keepdims=True)
    ) * inv_std
    kernel_terms = []
    for row_off in range(7):
        for col_off in range(7):
            kernel_terms.append(
                jnp.sum(
                    grad_conv
                    * extended[:, :, row_off : row_off + row_count, col_off : col_off + col_count],
                    axis=(0, 2, 3),
                )
            )
    part_kernel = jnp.stack(kernel_terms, axis=1)
    sum_in, sum_out, sum_kernel = lax.psum((part_in, part_out, part_kernel), ("ens", "tile"))
    return (
        block_out[:, None],
        sum_in / entry_total,
        sum_out / entry_total,
        sum_kernel / entry_total,
    )


def solution(mesh):
    placed = (
        P("ens", "tile", None, None, None),
        P("ens", "tile", None, None, None),
        P("tile", None, None),
        P(),
        P(),
        P(),
        P(),
        P(),
        P(),
        P(),
    )
    return jax.shard_map(
        local,
        mesh=mesh,
        in_specs=placed,
        out_specs=(P("ens", "tile", None, None, None), P(), P(), P()),
        check_vma=False,
    )
```

profile of v0, /device:TPU:1, one launch (start us, length us, event | category | flops | bytes accessed | tf_op | source)
XLA Modules:
  0.0 524.5 jit_solution(14262006590394135632)
XLA Ops:
  12.0 1.5 constant_dynamic-slice_fusion.3
  16.0 1.5 fusion.43
  19.4 66.7 %all-gather.5.cloned.1.call-done = bf16[64,1,200,3,128]{4,2,3,1,0:T(8,128)(2,1)} async-done(((bf16[2,1,200,3,128]{4,2,3,1,0:T(8,128)(2,1)}), bf16[64,1,200,3,128]{4,2,3,1,0:T(8,128)(2,1)}) %all-gather.5.cloned.1.call-update) | async-done | bytes 9830416 | tf_op jit(solution)/shard_map/all_gather | solution.py:76
  86.0 9.3 %fusion.39 = (bf16[32,1,1,200,3,128]{5,3,4,2,1,0:T(8,128)(2,1)}, bf16[32,1,1,200,3,128]{5,3,4,2,1,0:T(8,128)(2,1)}) fusion(bf16[32,2,1,200,3,128]{5,3,4,2,1,0:T(8,128)(2,1)} %bitcast.230), kind=kLoop, calls=%fused_computation.131 | loop fusion | bytes 19660800 | tf_op jit(solution)/shard_map/slice | solution.py:77
  106.6 52.3 %all-gather.7.cloned.1.call-done = bf16[64,1,200,3,14]{2,4,3,1,0:T(8,128)(2,1)} async-done(((bf16[2,1,200,3,14]{2,4,3,1,0:T(8,128)(2,1)}), bf16[64,1,200,3,14]{2,4,3,1,0:T(8,128)(2,1)}) %all-gather.7.cloned.1.call-update) | async-done | bytes 1075216 | tf_op jit(solution)/shard_map/all_gather | solution.py:87
  158.9 28.8 %copy.29 = bf16[64,1,200,3,14]{3,2,4,0,1:T(8,128)(2,1)} copy(bf16[64,1,200,3,14]{2,4,3,1,0:T(8,128)(2,1)} %all-gather.7.cloned.1.call-done) | data formatting | bytes 2150400 | tf_op jit(solution)/shard_map/all_gather | solution.py:87
  187.7 30.0 %fusion.38 = (bf16[32,1,1,200,3,14]{4,3,5,2,1,0:T(8,128)(2,1)}, bf16[32,1,1,200,3,14]{4,3,5,2,1,0:T(8,128)(2,1)}) fusion(bf16[32,2,1,200,3,14]{4,3,5,2,1,0:T(8,128)(2,1)} %bitcast.229), kind=kLoop, calls=%fused_computation.130 | loop fusion | bytes 2150400 | tf_op jit(solution)/shard_map/slice | solution.py:88
  217.7 1.4 select_bitcast_fusion
  219.5 1.8 maximum_convert_fusion
  221.7 11.7 %fusion.37 = (f32[8,128]{1,0:T(8,128)S(1)}, f32[1,200,8,128]{3,1,2,0:T(8,128)S(1)}) fusion(f32[1,200,14,134]{3,1,2,0:T(8,128)S(1)} %maximum_convert_fusion, f32[200]{0:T(256)S(1)} %bitcast.247, f32[200]{0:T(256)S(1)} %bitcast.248, f32[200]{0:T(256)S(1)} %bitcast.250, f32[200]{0:T(256)S(1)} %bitcast.251, f32[200]{0:T(256)S(1)} %bitcast.252, ...), kind=kLoop, calls=%fused_computation.129 | loop fusion | flops 20069376 | bytes 41003296 | tf_op jit(solution)/shard_map/reduce_sum | solution.py:101
  234.7 1.5 fusion.28
  237.4 1.7 fusion.5
  239.1 1.8 fusion.26
  240.9 1.5 fusion.17
  242.4 1.6 fusion.13
  244.0 1.6 multiply_reduce_fusion.49
  245.6 6.1 %multiply_reduce_fusion = (f32[200]{0:T(256)S(1)}, f32[200]{0:T(256)S(1)}, f32[200]{0:T(256)S(1)}, f32[200]{0:T(256)S(1)}, f32[200]{0:T(256)S(1)}, /*index=5*/f3...) fusion(f32[1,200,14,134]{3,1,2,0:T(8,128)S(1)} %maximum_convert, ...), kind=kLoop, calls=%fused_computation.30 | loop fusion | flops 8802800 | bytes 17234784 | tf_op jit(solution)/shard_map/reduce_sum | solution.py:139
  252.7 4.7 multiply_reduce_fusion.18
  257.4 4.6 multiply_reduce_fusion.36
  262.3 77.3 %psum.23 = f32[200,49]{0,1:T(8,128)S(1)} all-reduce(f32[200,49]{0,1:T(8,128)S(1)} %stack.223), channel_id=1, replica_groups=mesh['ens'=8,'tile'=32] {'ens','tile'}, use_global_device_ids=true, to_apply=%region_56.57 | all-reduce | flops 9800 | bytes 78400 | tf_op jit(solution)/shard_map/psum | solution.py:146
  340.2 2.4 add_convert_fusion
  342.6 171.3 %all-reduce.3.cloned.1.call-done = (f32[200,800]{1,0:T(8,128)}, f32[800,200]{0,1:T(8,128)}) async-done(((f32[200,800]{1,0:T(8,128)}, f32[800,200]{0,1:T(8,128)}), (f32[200,800]{1,0:T(8,128)}, f32[800,200]{0,1:T(8,128)})) %all-reduce.3.cloned.1.call-update) | async-done | bytes 1280016 | tf_op jit(solution)/shard_map/psum | solution.py:146
  513.9 2.0 broadcast_multiply_fusion
  515.9 2.0 broadcast_multiply_fusion.1
  (144 shorter events, 17.8 us)
Async XLA Ops:
  7.2 226.6 %copy-start = (bf16[200,800]{1,0:T(8,128)(2,1)S(1)}, bf16[200,800]{1,0:T(8,128)(2,1)}, u32[]{:S(2)}) copy-start(bf16[200,800]{1,0:T(8,128)(2,1)} %param.17) | copy-start | bytes 960004
  7.2 78.9 %all-gather.5.cloned.1.call-start = ((), (), s32[]{:S(2)}) async-start(), calls=%async_computation | async-start | bytes 10137600 | tf_op jit(solution)/shard_map/all_gather | solution.py:76
  8.5 89.9 %copy-start.3 = (bf16[1,200,8,128]{3,1,2,0:T(8,128)(2,1)}, bf16[1,200,8,128]{3,1,2,0:T(8,128)(2,1)S(1)}, u32[]{:S(2)}) copy-start(bf16[1,200,8,128]{3,1,2,0:T(8,128)(2,1)S(1)} %compare_select_fusion.2) | copy-start | bytes 1228804
  9.3 149.6 %all-gather.7.cloned.1.call-start = ((), (), s32[]{:S(2)}) async-start(), calls=%async_computation.1 | async-start | bytes 1622016 | tf_op jit(solution)/shard_map/all_gather | solution.py:87
  98.5 3.5 copy-start.4
  98.8 4.2 copy-start.9
  98.8 5.3 %copy-start.12 = (f32[200]{0:T(256)S(1)}, f32[200]{0:T(256)}, u32[]{:S(2)}) copy-start(f32[200]{0:T(256)} %param.19) | copy-start | bytes 2404
  98.8 5.8 %copy-start.10 = (f32[200,49]{0,1:T(8,128)S(1)}, f32[200,49]{0,1:T(8,128)}, u32[]{:S(2)}) copy-start(f32[200,49]{0,1:T(8,128)} %param.15) | copy-start | bytes 117604
  100.5 413.4 %all-reduce.3.cloned.1.call-start = ((), (), s32[]{:S(2)}) async-start(), calls=%async_computation.2 | async-start | bytes 2867200 | tf_op jit(solution)/shard_map/psum | solution.py:146
  219.1 2.2 copy-start.14
  219.1 2.2 copy-start.15
  219.1 2.2 copy-start.16
  219.1 2.2 copy-start.17
  219.1 2.2 copy-start.18
  219.1 2.2 copy-start.19
  219.2 2.2 copy-start.20
  219.2 2.2 copy-start.21
  219.2 2.2 copy-start.22
  221.7 11.9 %copy-start.13 = (f32[200]{0:T(256)S(1)}, f32[200]{0:T(256)}, u32[]{:S(2)}) copy-start(f32[200]{0:T(256)} %param.16) | copy-start | bytes 2404
  234.7 2.4 copy-start.5
  234.7 2.4 copy-start.8
  234.7 2.4 copy-start.11
  234.7 2.4 copy-start.52
  257.4 4.6 copy-start.7
  (33 other events, 67.5 us)
Sparse Core Ops, SparseCore 0:
  10.4 75.5 all-gather.4
  100.6 58.2 all-gather.6
  257.5 256.3 all-reduce.2
where the time goes:
time: 528 us; the launch traced here: 524 us
  waiting for transfers between devices  290 us (55%)
  local copies, waits for them, and re-layouts  80.3 us (15%)
  blocking collectives  77.3 us (15%)
  other arithmetic  45.9 us (9%)
  between operations  21.6 us (4%)
  matrix products  8.74 us (2%)
    psum x1, waiting for transfers between devices, local(): lax.psum((part_in, part_out, part_kernel), ('ens', 'tile'))  171 us
    psum x1, blocking collectives, local(): lax.psum((part_in, part_out, part_kernel), ('ens', 'tile'))  77.3 us
    all_gather x1, waiting for transfers between devices, local(): pieces = lax.all_gather(row_strips, 'tile', axis=0, tiled=True)  66.7 us
    all_gather x1, waiting for transfers between devices, local(): pieces = lax.all_gather(side_cols, 'tile', axis=0, tiled=True)  52.3 us
    slice x1, local copies, waits for them, and re-layouts, local(): west_part = take_slot(held[0], pieces[:, 1], west_slot)  30 us
    all_gather x1, local copies, waits for them, and re-layouts, local(): pieces = lax.all_gather(side_cols, 'tile', axis=0, tiled=True)  28.8 us
    reduce_sum x3, other arithmetic, local(): jnp.sum(grad_conv * extended[:, :, row_off:row_off + row_count, col_off:c...  15.4 us
    reduce_sum x1, other arithmetic, local(): chan_mean = jnp.mean(conv_out, axis=1, keepdims=True)  11.7 us
  transfers between devices with their start and end apart: 3, of which 3 were waited for; matrix products, arithmetic and copies ran while one was open for 3% of the time, Pallas kernels for 0%

commit v1 on v0

v1 whole, which is shorter than its diff:
```python
import jax
import jax.numpy as jnp
from jax import lax
from jax.experimental import pallas as pl
from jax.experimental.pallas import tpu as pltpu
from jax.sharding import PartitionSpec as P

LEVELS = 19
TILES = 32
CH = 200
PARTS = 7
ROWS = 8
COLS = 128
EXT = 14
TAPS = 7
HID = 800
CELLS = ROWS * COLS
CHUNKS = 32
SUB = 12

root_half = 0.7071067811865476
gauss_norm = 0.3989422804014327
norm_epsilon = 1e-06
f32 = jnp.float32
bf16 = jnp.bfloat16
AXES = ("ens", "tile")
BIG = 48 << 20


def gelu_value(values):
    return 0.5 * values * (1.0 + lax.erf(values * root_half))


def gelu_slope(values):
    return (
        0.5 * (1.0 + lax.erf(values * root_half))
        + values * jnp.exp(-0.5 * values * values) * gauss_norm
    )


def link_at(links, tile_id, column):
    return jnp.where(tile_id >= 0, links[jnp.maximum(tile_id, 0), column], -1)


def compose_kernel(links, owner, x_ref, o_ref, inverse):
    shape = (PARTS, ROWS, COLS)
    row = lax.broadcasted_iota(jnp.int32, shape, 1)
    lane = lax.broadcasted_iota(jnp.int32, shape, 2)
    edge = (lane < 3) | (lane >= COLS - 3)
    east_side = lane < 64

    def note(k, _):
        inverse[owner[k]] = k
        return 0

    lax.fori_loop(0, TILES, note, 0)

    def load(tile_id):
        slot = jnp.where(tile_id >= 0, owner[jnp.maximum(tile_id, 0)], 0)
        block = x_ref[slot].astype(f32)
        return jnp.where(tile_id >= 0, block, 0.0)

    def north_of(tile_id):
        block = load(link_at(links, tile_id, 0))
        return jnp.where(link_at(links, tile_id, 4) == 1, pltpu.roll(block, 3, 1), block)

    def body(d, _):
        own = inverse[d]
        west = link_at(links, own, 2)
        east = link_at(links, own, 3)
        north_rows = north_of(own)
        south_rows = load(link_at(links, own, 1))
        sides = jnp.where(edge, jnp.where(east_side, load(east), load(west)), 0.0)
        north_side = (lane < 64) != (link_at(links, own, 4) == 1)
        north_corner = jnp.where(north_side, north_of(east), north_of(west))
        south_corner = jnp.where(
            east_side, load(link_at(links, east, 1)), load(link_at(links, west, 1))
        )
        corners = jnp.where(row < 3, north_corner, south_corner)
        corners = jnp.where(edge & ((row < 3) | (row > 4)), corners, 0.0)
        spread = pltpu.roll(
            sides + pltpu.roll(corners, 64, 2), 24, 2, stride=8, stride_axis=1
        )
        packed = jnp.sum(spread, axis=1, keepdims=True)
        block = jnp.where(row == 3, packed, jnp.where(row < 3, north_rows, south_rows))
        o_ref[d] = block.astype(bf16)
        return 0

    lax.fori_loop(0, TILES, body, 0)


def compose(links, owner, chunks):
    smem = pl.BlockSpec(memory_space=pltpu.SMEM)
    vmem = pl.BlockSpec(memory_space=pltpu.VMEM)
    return pl.pallas_call(
        compose_kernel,
        out_shape=jax.ShapeDtypeStruct((TILES, PARTS, ROWS, COLS), bf16),
        in_specs=[smem, smem, vmem],
        out_specs=vmem,
        scratch_shapes=[pltpu.SMEM((TILES,), jnp.int32)],
        compiler_params=pltpu.CompilerParams(vmem_limit_bytes=BIG),
        name="compose",
    )(links, owner, chunks)


def shifted(center, halo, col_off, lane):
    if col_off < 3:
        k = 3 - col_off
        return pltpu.roll(jnp.where(lane >= COLS - k, halo, center), k, 1)
    if col_off > 3:
        k = col_off - 3
        return pltpu.roll(jnp.where(lane < k, halo, center), COLS - k, 1)
    return center


def conv_kernel(
    links, owner, own_slot, m_ref, r_ref, coef, cen_ref, norm_ref, inv_ref, ext, halo, flat_ref, mine, rims
):
    slot = own_slot[0]

    def find(k, best):
        return jnp.where(owner[k] == slot, k, best)

    own = lax.fori_loop(0, TILES, find, 0)
    fold = links[own, 4] == 1
    mine[...] = m_ref[0:CH].astype(f32).reshape(CH * ROWS, COLS)
    rims[...] = r_ref[0:CH].astype(f32).reshape(CH * ROWS, COLS)
    for r in range(ROWS):
        values = mine[pl.ds(r, CH, stride=ROWS), :]
        ext[3 + r] = values
        flat_ref[:, COLS * r : COLS * r + COLS] = values.astype(bf16)
    row = lax.broadcasted_iota(jnp.int32, (COLS, COLS), 0)
    col = lax.broadcasted_iota(jnp.int32, (COLS, COLS), 1)
    turn = (row == jnp.where(fold, COLS - 1 - col, col)).astype(f32).astype(bf16)
    edges = rims[pl.ds(3, CH, stride=ROWS), :]
    for r in range(11):
        halo[r] = edges if r == 0 else pltpu.roll(edges, COLS - 8 * r, 1)
    north = [rims[pl.ds(t, CH, stride=ROWS), :] for t in range(3)]
    corner = [pltpu.roll(edges, COLS - 8 * (11 + t), 1) for t in range(3)]
    for t in range(3):
        ext[t] = rims[pl.ds(5 + t, CH, stride=ROWS), :]
        for dest, source in ((ext, north), (halo, corner)):
            raw = jnp.where(fold, source[2 - t], source[t]).astype(bf16)
            dest[11 + t] = jnp.dot(raw, turn, preferred_element_type=f32)
    lane = lax.broadcasted_iota(jnp.int32, (8, COLS), 1)

    def block(i, sums):
        at = pl.ds(pl.multiple_of(8 * i, 8), 8)
        taps = coef[at, :]
        acc = [jnp.zeros((8, COLS), f32) for _ in range(ROWS)]
        for b in range(TAPS):
            moved = [shifted(ext[r, at, :], halo[r, at, :], b, lane) for r in range(EXT)]
            for a in range(TAPS):
                tap = jnp.broadcast_to(taps[:, 7 * a + b : 7 * a + b + 1], (8, COLS))
                for r in range(ROWS):
                    acc[r] = acc[r] + tap * moved[r + a]
        for r in range(ROWS):
            cen_ref[at, COLS * r : COLS * r + COLS] = acc[r]
        return tuple(s + x for s, x in zip(sums, acc))

    sums = lax.fori_loop(0, CH // 8, block, tuple(jnp.zeros((8, COLS), f32) for _ in range(ROWS)))
    gain = jnp.broadcast_to(coef[:, 49:50], (CH, COLS))
    for r in range(ROWS):
        at = slice(COLS * r, COLS * r + COLS)
        mean = jnp.sum(sums[r], axis=0, keepdims=True) * (1.0 / CH)
        off = cen_ref[:, at] - mean
        var = jnp.sum(off * off, axis=0, keepdims=True) * (1.0 / CH)
        inv = 1.0 / jnp.sqrt(var + norm_epsilon)
        centred = off * inv
        cen_ref[:, at] = centred
        norm_ref[:, at] = (centred * gain).astype(bf16)
        inv_ref[r : r + 1, :] = inv


def forward_conv(links, owner, own_slot, payload, rims, coef):
    smem = pl.BlockSpec(memory_space=pltpu.SMEM)
    vmem = pl.BlockSpec(memory_space=pltpu.VMEM)
    shapes = [
        ((CH, CELLS), f32),
        ((CH, CELLS), bf16),
        ((ROWS, COLS), f32),
        ((EXT, CH, COLS), f32),
        ((EXT, CH, COLS), f32),
        ((CH, CELLS), bf16),
    ]
    return pl.pallas_call(
        conv_kernel,
        out_shape=[jax.ShapeDtypeStruct(s, d) for s, d in shapes],
        in_specs=[smem, smem, smem, vmem, vmem, vmem],
        out_specs=[vmem] * len(shapes),
        scratch_shapes=[pltpu.VMEM((CH * ROWS, COLS), f32)] * 2,
        compiler_params=pltpu.CompilerParams(vmem_limit_bytes=BIG),
        name="forward_conv",
    )(links, owner, own_slot, payload, rims, coef)


def grad_kernel(me, gn_ref, cen_ref, inv_ref, ext, halo, coef, in_ref, out_ref, keep, send, gconv, pack):
    gain = jnp.broadcast_to(coef[:, 49:50], (CH, COLS))
    for r in range(ROWS):
        at = slice(COLS * r, COLS * r + COLS)
        scaled = gn_ref[:, at] * gain
        centred = cen_ref[:, at]
        mean = jnp.sum(scaled, axis=0, keepdims=True) * (1.0 / CH)
        along = jnp.sum(scaled * centred, axis=0, keepdims=True) * (1.0 / CH)
        gconv[:, at] = (scaled - mean - centred * along) * inv_ref[r : r + 1, :]
    lane = lax.broadcasted_iota(jnp.int32, (8, COLS), 1)

    def block(i, _):
        at = pl.ds(pl.multiple_of(8 * i, 8), 8)
        grads = [gconv[at, COLS * r : COLS * r + COLS] for r in range(ROWS)]
        found = jnp.zeros((8, COLS), f32)
        for b in range(TAPS):
            moved = [shifted(ext[r, at, :], halo[r, at, :], b, lane) for r in range(EXT)]
            for a in range(TAPS):
                terms = grads[0] * moved[a]
                for r in range(1, ROWS):
                    terms = terms + grads[r] * moved[r + a]
                total = jnp.sum(terms, axis=1, keepdims=True)
                found = jnp.where(lane == 32 + 7 * a + b, total, found)
        for t in range(6):
            pack[7 * i + t] = in_ref[at, COLS * t : COLS * t + COLS]
        tail = jnp.concatenate([in_ref[at, 6 * COLS : HID], jnp.zeros((8, 96), f32)], axis=1)
        pack[7 * i + 6] = jnp.where(lane < 32, tail, found)
        return 0

    lax.fori_loop(0, CH // 8, block, 0)

    def rows(i, _):
        at = pl.ds(pl.multiple_of(8 * i, 8), 8)
        pack[175 + 2 * i] = out_ref[at, 0:COLS]
        pack[176 + 2 * i] = jnp.concatenate(
            [out_ref[at, COLS:CH], jnp.zeros((8, 2 * COLS - CH), f32)], axis=1
        )
        return 0

    lax.fori_loop(0, HID // 8, rows, 0)
    for t in range(375, CHUNKS * SUB):
        pack[t] = jnp.zeros((8, COLS), f32)

    def split(j, _):
        for dest, offset in ((keep, 0), (send, 16)):
            source = ((j + offset) ^ me[0]) * SUB
            for t in range(SUB):
                dest[j, 8 * t : 8 * t + 8, :] = pack[source + t]
        return 0

    lax.fori_loop(0, CHUNKS // 2, split, 0)


def backward_conv(me, gn, cen, inv, ext, halo, coef, part_in, part_out):
    smem = pl.BlockSpec(memory_space=pltpu.SMEM)
    vmem = pl.BlockSpec(memory_space=pltpu.VMEM)
    half = jax.ShapeDtypeStruct((CHUNKS // 2, 8 * SUB, COLS), f32)
    return pl.pallas_call(
        grad_kernel,
        out_shape=[half, half],
        in_specs=[smem] + [vmem] * 8,
        out_specs=[vmem, vmem],
        scratch_shapes=[
            pltpu.VMEM((CH, CELLS), f32),
            pltpu.VMEM((CHUNKS * SUB, 8, COLS), f32),
        ],
        compiler_params=pltpu.CompilerParams(vmem_limit_bytes=BIG),
        name="backward_conv",
    )(me, gn, cen, inv, ext, halo, coef, part_in, part_out)


def unpack_kernel(me, x_ref, in_ref, out_ref, k_ref, pack):
    share = 1.0 / (8 * TILES * CH * CELLS)

    def order(j, _):
        dest = (j ^ me[0]) * SUB
        values = x_ref[j].astype(f32) * share
        for t in range(SUB):
            pack[dest + t] = values[8 * t : 8 * t + 8, :]
        return 0

    lax.fori_loop(0, CHUNKS, order, 0)

    def block(i, _):
        at = pl.ds(pl.multiple_of(8 * i, 8), 8)
        for t in range(6):
            in_ref[at, COLS * t : COLS * t + COLS] = pack[7 * i + t]
        tail = pack[7 * i + 6]
        in_ref[at, 6 * COLS : HID] = tail[:, 0:32]
        k_ref[at, :] = tail[:, 32:81]
        return 0

    lax.fori_loop(0, CH // 8, block, 0)

    def rows(i, _):
        at = pl.ds(pl.multiple_of(8 * i, 8), 8)
        out_ref[at, 0:COLS] = pack[175 + 2 * i]
        out_ref[at, COLS:CH] = pack[176 + 2 * i][:, 0 : CH - COLS]
        return 0

    lax.fori_loop(0, HID // 8, rows, 0)


def unpack(me, gathered):
    vmem = pl.BlockSpec(memory_space=pltpu.VMEM)
    return pl.pallas_call(
        unpack_kernel,
        out_shape=[
            jax.ShapeDtypeStruct((CH, HID), f32),
            jax.ShapeDtypeStruct((HID, CH), f32),
            jax.ShapeDtypeStruct((CH, 49), f32),
        ],
        in_specs=[pl.BlockSpec(memory_space=pltpu.SMEM), vmem],
        out_specs=[vmem] * 3,
        scratch_shapes=[pltpu.VMEM((CHUNKS * SUB, 8, COLS), f32)],
        compiler_params=pltpu.CompilerParams(vmem_limit_bytes=BIG),
        name="unpack",
    )(me, gathered)


def swap(values, bits):
    return lax.ppermute(values, AXES, [(i, i ^ bits) for i in range(256)])


def reduce_all(keep, send):
    held = keep + swap(send, 1)
    held = held.reshape(4, 4, 8 * SUB, COLS)
    held = (held[0] + swap(held[1], 2)) + (swap(held[2], 4) + swap(held[3], 6))
    held = (held[0] + swap(held[1], 64)) + (swap(held[2], 128) + swap(held[3], 192))
    for bits in (8, 16, 32):
        held = held + swap(held, bits)
    part = held.astype(bf16)
    part = jnp.stack([part] + [swap(part, k << 6) for k in (1, 2, 3)])
    part = jnp.stack([part] + [swap(part, k << 1) for k in (1, 2, 3)])
    part = jnp.stack([part, swap(part, 1)])
    return part.reshape(CHUNKS, 8 * SUB, COLS)


def local(
    fields,
    target,
    wet_levels,
    tile_links,
    tile_owner,
    kernel,
    norm_gain,
    weight_in,
    weight_out,
    layer_scale,
):
    tile_at = lax.axis_index("tile").astype(jnp.int32)
    ens_at = lax.axis_index("ens").astype(jnp.int32)
    own_slot = tile_at.reshape(1)
    me = ((tile_at & 1) * 16 + ((tile_at >> 1) & 3) * 4 + (ens_at >> 1)).reshape(1)
    level_of = jnp.arange(CH, dtype=jnp.int32) * LEVELS // CH
    wet_mask = wet_levels[0][None, :, :] > level_of[:, None, None]
    own_input = fields[0, 0]
    masked = jnp.where(wet_mask, own_input, jnp.zeros_like(own_input))
    payload = jnp.pad(masked, ((0, TILES * PARTS - CH), (0, 0), (0, 0)))
    coef = jnp.concatenate([kernel, norm_gain[:, None], layer_scale[:, None]], axis=1)

    chunks = lax.all_to_all(
        payload.reshape(TILES, PARTS, ROWS, COLS), "tile", 0, 0, tiled=True
    )
    rims = lax.all_to_all(compose(tile_links, tile_owner, chunks), "tile", 0, 0, tiled=True)
    rims = rims.reshape(TILES * PARTS, ROWS, COLS)
    centred, flat_norm, inv_std, ext, halo, flat_masked = forward_conv(
        tile_links, tile_owner, own_slot, payload, rims, coef
    )

    scale_wide = layer_scale[:, None]
    hidden = jnp.einsum("ch,cp->hp", weight_in, flat_norm, preferred_element_type=f32)
    activated = gelu_value(hidden).astype(bf16)
    mlp_out = jnp.einsum("hc,hp->cp", weight_out, activated, preferred_element_type=f32)
    block_out = (flat_masked.astype(f32) + scale_wide * mlp_out).astype(bf16)
    flat_wet = wet_levels[0].reshape(1, CELLS) > level_of[:, None]
    misfit = jnp.where(
        flat_wet, block_out.astype(f32) - target[0, 0].reshape(CH, CELLS).astype(f32), 0.0
    )
    grad_mlp = (2.0 * scale_wide * misfit).astype(bf16)
    part_out = jnp.einsum("hp,cp->hc", activated, grad_mlp, preferred_element_type=f32)
    grad_act = jnp.einsum("hc,cp->hp", weight_out, grad_mlp, preferred_element_type=f32)
    grad_hidden = (grad_act * gelu_slope(hidden)).astype(bf16)
    part_in = jnp.einsum("cp,hp->ch", flat_norm, grad_hidden, preferred_element_type=f32)
    grad_normed = jnp.einsum("ch,hp->cp", weight_in, grad_hidden, preferred_element_type=f32)

    keep, send = backward_conv(
        me, grad_normed, centred, inv_std, ext, halo, coef, part_in, part_out
    )
    grad_in, grad_out, grad_taps = unpack(me, reduce_all(keep, send))
    return block_out.reshape(1, 1, CH, ROWS, COLS), grad_in, grad_out, grad_taps


def solution(mesh):
    placed = (
        P("ens", "tile", None, None, None),
        P("ens", "tile", None, None, None),
        P("tile", None, None),
        P(),
        P(),
        P(),
        P(),
        P(),
        P(),
        P(),
    )
    return jax.shard_map(
        local,
        mesh=mesh,
        in_specs=placed,
        out_specs=(P("ens", "tile", None, None, None), P(), P(), P()),
        check_vma=False,
    )
```

time: 528 us -> 149 us (0.28)
  waiting for transfers between devices: 290 us -> 58.5 us
  blocking collectives: 77.3 us -> 0 us
  local copies, waits for them, and re-layouts: 80.3 us -> 5.35 us
  other arithmetic: 45.9 us -> 1.94 us
  starting transfers between devices: 0.3 us -> 42.5 us
  Pallas kernels: 0 us -> 33.9 us
  between operations: 21.6 us -> 0.99 us
    psum x1 -> x0, waiting for transfers between devices: 171 us -> none  [local(): lax.psum((part_in, part_out, part_kernel), ('ens', 'tile'))]
    all_gather x2 -> x0, waiting for transfers between devices: 119 us -> none  [the longest x1 66.7 us: local(): pieces = lax.all_gather(row_strips, 'tile', axis=0, tiled=True)]
    psum x1 -> x0, blocking collectives: 77.3 us -> none  [local(): lax.psum((part_in, part_out, part_kernel), ('ens', 'tile'))]
    slice x5 -> x1, local copies, waits for them, and re-layouts: 41.3 us -> 0.04 us  [reduce_all(): held = held[0] + swap(held[1], 2) + (swap(held[2], 4) + swap(held[3], 6))]
    pallas_call x0 -> x4, Pallas kernels: none -> 33.9 us  [the longest x1 13.5 us: backward_conv(): pl.pallas_call(grad_kernel, out_shape=[half, half], in_specs=[smem] + [vm...]
    reduce_sum x7 -> x0, other arithmetic: 30.1 us -> none  [the longest x3 15.4 us: local(): jnp.sum(grad_conv * extended[:, :, row_off:row_off + row_count, col_off:c...]
    ppermute x0 -> x17, waiting for transfers between devices: none -> 29.7 us  [swap(): return lax.ppermute(values, AXES, [(i, i ^ bits) for i in range(256)])]
    all_to_all x0 -> x2, waiting for transfers between devices: none -> 28.8 us  [the longest x1 14.5 us: local(): lax.all_to_all(compose(tile_links, tile_owner, chunks), 'tile', 0, 0, til...]
  transfers between devices with their start and end apart: 3 -> 19, of which waited for: 3 -> 16; matrix products, arithmetic and copies ran while one was open for 3% -> 1% of each run, Pallas kernels for 0% -> 0%
where the time goes in v1:
time: 149 us
  waiting for transfers between devices  58.5 us (39%)
  starting transfers between devices  42.5 us (29%)
  Pallas kernels  33.9 us (23%)
  matrix products  5.94 us (4%)
  local copies, waits for them, and re-layouts  5.35 us (4%)
  other arithmetic  1.94 us (1%)
    ppermute x17, waiting for transfers between devices, swap(): return lax.ppermute(values, AXES, [(i, i ^ bits) for i in range(256)])  29.7 us
    ppermute x17, starting transfers between devices, swap(): return lax.ppermute(values, AXES, [(i, i ^ bits) for i in range(256)])  28.4 us
    all_to_all x1, waiting for transfers between devices, local(): lax.all_to_all(compose(tile_links, tile_owner, chunks), 'tile', 0, 0, til...  14.5 us
    all_to_all x1, waiting for transfers between devices, local(): lax.all_to_all(payload.reshape(TILES, PARTS, ROWS, COLS), 'tile', 0, 0, t...  14.3 us
    pallas_call x1, Pallas kernels, backward_conv(): pl.pallas_call(grad_kernel, out_shape=[half, half], in_specs=[smem] + [vm...  13.5 us
    all_to_all x1, starting transfers between devices, local(): lax.all_to_all(payload.reshape(TILES, PARTS, ROWS, COLS), 'tile', 0, 0, t...  10 us
    pallas_call x1, Pallas kernels, forward_conv(): pl.pallas_call(conv_kernel, out_shape=[jax.ShapeDtypeStruct(s, d) for s,...  9.04 us
    pallas_call x1, Pallas kernels, compose(): pl.pallas_call(compose_kernel, out_shape=jax.ShapeDtypeStruct((TILES, PAR...  7.81 us
  transfers between devices with their start and end apart: 19, of which 16 were waited for; matrix products, arithmetic and copies ran while one was open for 1% of the time, Pallas kernels for 0%

profile of v1, /device:TPU:1, one launch (start us, length us, event | category | flops | bytes accessed | tf_op | source)
XLA Modules:
  0.0 149.1 jit_solution(7055010444642934313)
XLA Ops:
  0.7 1.4 compare_select_fusion
  2.9 10.0 %all-to-all-start = ((bf16[32,7,8,128]{3,2,1,0:T(8,128)(2,1)}), bf16[32,7,8,128]{3,2,1,0:T(8,128)(2,1)S(1)}, u32[]{:S(2)}, u32[]{:S(2)}) async-start(bf16[32,7,8,128]{3,2,1,0:T(8,128)(2,1)} %bitcast.3), calls=%async_computation | async-start | bytes 917504 | tf_op jit(solution)/shard_map/all_to_all | solution.py:358
  13.7 14.3 %all-to-all-done.x_ref = bf16[32,7,8,128]{3,2,1,0:T(8,128)(2,1)S(1)} async-done(((bf16[32,7,8,128]{3,2,1,0:T(8,128)(2,1)}), bf16[32,7,8,128]{3,2,1,0:T(8,128)(2,1)S(1)}, u32[]{:S(2)}, u32[]{:S(2)}) %all-to-all-start) | async-done | bytes 458784 | tf_op jit(solution)/shard_map/all_to_all | solution.py:358
  28.7 7.8 %compose.1 = bf16[32,7,8,128]{3,2,1,0:T(8,128)(2,1)} custom-call(s32[32,5]{1,0:T(8,128)S(1)} %copy.24.links, s32[32]{0:T(128)S(1)} %copy-done.3, bf16[32,7,8,128]{3,2,1,0:T(8,128)(2,1)S(1)} %all-to-all-done.x_ref), custom_call_target="tpu_custom_call" | custom-call | tf_op jit(solution)/shard_map/compose/pallas_call | solution.py:95
  36.5 4.0 %all-to-all-start.1 = ((bf16[32,7,8,128]{3,2,1,0:T(8,128)(2,1)}), bf16[32,7,8,128]{3,2,1,0:T(8,128)(2,1)S(1)}, u32[]{:S(2)}, u32[]{:S(2)}) async-start(bf16[32,7,8,128]{3,2,1,0:T(8,128)(2,1)} %compose.1), calls=%async_computation.1 | async-start | bytes 917504 | tf_op jit(solution)/shard_map/all_to_all | solution.py:361
  41.2 14.5 %all-to-all-done.1 = bf16[32,7,8,128]{3,2,1,0:T(8,128)(2,1)S(1)} async-done(((bf16[32,7,8,128]{3,2,1,0:T(8,128)(2,1)}), bf16[32,7,8,128]{3,2,1,0:T(8,128)(2,1)S(1)}, u32[]{:S(2)}, u32[]{:S(2)}) %all-to-all-start.1) | async-done | bytes 458784 | tf_op jit(solution)/shard_map/all_to_all | solution.py:361
  55.7 9.0 %forward_conv.1 = (f32[200,1024]{1,0:T(8,128)S(1)}, bf16[200,1024]{1,0:T(8,128)(2,1)S(1)}, f32[8,128]{1,0:T(8,128)S(1)}, f32[14,200,128]{2,1,0:T(8,128)S(1)}, f3...) custom-call(s32[32,5]{1,0:T(8,128)S(1)} %copy.24.links, s32[32]{0:T(128)S(1)} %copy-done.4, s32[1]{0:T(128)} %bitcast.own_slot, ...), custom_call_target="tpu_custom_call" | custom-call | tf_op jit(solution)/shard_map/forward_conv/pallas_call | solution.py:186
  64.8 1.5 %fusion.7 = (bf16[800,1024]{1,0:T(8,128)(2,1)S(1)}, f32[1024,800]{0,1:T(8,128)S(1)}) fusion(bf16[200,1024]{1,0:T(8,128)(2,1)S(1)} %get-tuple-element.16, bf16[200,800]{1,0:T(8,128)(2,1)S(1)} %copy-done), kind=kOutput, calls=%fused_computation.10 | convolution fusion | flops 331776000 | bytes 5644800 | tf_op jit(solution)/shard_map/ch,cp->hp/dot_general | solution.py:368
  67.7 1.7 %fusion.5 = bf16[800,1024]{1,0:T(8,128)(2,1)S(1)} fusion(f32[1024,800]{0,1:T(8,128)S(1)} %get-tuple-element.45, bf16[200,1024]{1,0:T(8,128)(2,1)S(1)} %get-tuple-element.46, bf16[800,200]{0,1:T(8,128)(2,1)S(1)} %copy-done.10), kind=kOutput, calls=%fused_computation.6 | convolution fusion | flops 335872000 | bytes 5644800 | tf_op jit(solution)/shard_map/hc,cp->hp/dot_general | solution.py:378
  70.8 13.5 %backward_conv.1 = (f32[16,96,128]{2,1,0:T(8,128)S(1)}, f32[16,96,128]{2,1,0:T(8,128)S(1)}) custom-call(s32[1]{0:T(128)} %bitcast.9.me, f32[200,1024]{1,0:T(8,128)S(1)} %convolution_bitcast_fusion.gn_ref, f32[200,1024]{1,0:T(8,128)S(1)} %get-tuple-element.17.cen_ref, f32[8,128]{1,0:T(8,128)S(1)} %get-tuple-element.18.inv_ref, f32[14,200,128]{2,1,0:T(8,128)} %copy-done.1, ...), custom_call_target="tpu_custom_call" | custom-call | tf_op jit(solution)/shard_map/backward_conv/pallas_call | solution.py:254
  84.4 2.3 %collective-permute-done = f32[16,96,128]{2,1,0:T(8,128)S(1)} collective-permute-done((f32[16,96,128]{2,1,0:T(8,128)S(1)}, f32[16,96,128]{2,1,0:T(8,128)S(1)}, u32[]{:S(2)}, u32[]{:S(2)}) %collective-permute-start) | collective-permute-done | bytes 786464 | tf_op jit(solution)/shard_map/ppermute | solution.py:318
  90.1 8.5 %collective-permute-done.3 = f32[4,96,128]{2,1,0:T(8,128)S(1)} collective-permute-done((f32[4,96,128]{2,1,0:T(8,128)S(1)}, f32[4,96,128]{2,1,0:T(8,128)S(1)}, u32[]{:S(2)}, u32[]{:S(2)}) %collective-permute-start.3) | collective-permute-done | bytes 196640 | tf_op jit(solution)/shard_map/ppermute | solution.py:318
  99.0 2.8 %collective-permute-start.6 = (f32[96,128]{1,0:T(8,128)S(1)}, f32[96,128]{1,0:T(8,128)S(1)}, u32[]{:S(2)}, u32[]{:S(2)}) collective-permute-start(f32[96,128]{1,0:T(8,128)S(1)} %get-tuple-element.39), channel_id=1, source_target_pairs={{0,192},{1,193},{2,194},{3,195},{4,196},{5,197},{6,198},{7,199},{8... | collective-permute-start | bytes 147464 | tf_op jit(solution)/shard_map/ppermute | solution.py:318
  103.3 3.0 %collective-permute-done.5 = f32[96,128]{1,0:T(8,128)S(1)} collective-permute-done((f32[96,128]{1,0:T(8,128)S(1)}, f32[96,128]{1,0:T(8,128)S(1)}, u32[]{:S(2)}, u32[]{:S(2)}) %collective-permute-start.5) | collective-permute-done | bytes 49184 | tf_op jit(solution)/shard_map/ppermute | solution.py:318
  107.0 2.4 %collective-permute-done.7 = f32[96,128]{1,0:T(8,128)S(1)} collective-permute-done((f32[96,128]{1,0:T(8,128)S(1)}, f32[96,128]{1,0:T(8,128)S(1)}, u32[]{:S(2)}, u32[]{:S(2)}) %collective-permute-start.7) | collective-permute-done | bytes 49184 | tf_op jit(solution)/shard_map/ppermute | solution.py:318
  110.0 4.0 %collective-permute-done.8 = f32[96,128]{1,0:T(8,128)S(1)} collective-permute-done((f32[96,128]{1,0:T(8,128)S(1)}, f32[96,128]{1,0:T(8,128)S(1)}, u32[]{:S(2)}, u32[]{:S(2)}) %collective-permute-start.8) | collective-permute-done | bytes 49184 | tf_op jit(solution)/shard_map/ppermute | solution.py:318
  114.0 4.3 %collective-permute-start.9 = (f32[96,128]{1,0:T(8,128)S(1)}, f32[96,128]{1,0:T(8,128)S(1)}, u32[]{:S(2)}, u32[]{:S(2)}) collective-permute-start(f32[96,128]{1,0:T(8,128)S(1)} %add.70), channel_id=1, source_target_pairs={{0,32},{1,33},{2,34},{3,35},{4,36},{5,37},{6,38},{7,39},{8,40},{9,... | collective-permute-start | bytes 147464 | tf_op jit(solution)/shard_map/ppermute | solution.py:318
  118.3 2.6 %collective-permute-done.9 = f32[96,128]{1,0:T(8,128)S(1)} collective-permute-done((f32[96,128]{1,0:T(8,128)S(1)}, f32[96,128]{1,0:T(8,128)S(1)}, u32[]{:S(2)}, u32[]{:S(2)}) %collective-permute-start.9) | collective-permute-done | bytes 49184 | tf_op jit(solution)/shard_map/ppermute | solution.py:318
  122.7 1.5 %collective-permute-start.10 = (bf16[96,128]{1,0:T(8,128)(2,1)S(1)}, bf16[96,128]{1,0:T(8,128)(2,1)S(1)}, u32[]{:S(2)}, u32[]{:S(2)}) collective-permute-start(bf16[96,128]{1,0:T(8,128)(2,1)S(1)} %add_convert_fusion), channel_id=1, source_target_pairs={{0,64},{1,65},{2,66},{3,67},{4,68},{5,69},{6,70},{7,71},{8,72},{9,... | collective-permute-start | bytes 73736 | tf_op jit(solution)/shard_map/ppermute | solution.py:318
  128.0 1.6 %collective-permute-start.15 = (bf16[4,96,128]{2,1,0:T(8,128)(2,1)S(1)}, bf16[4,96,128]{2,1,0:T(8,128)(2,1)S(1)}, u32[]{:S(2)}, u32[]{:S(2)}) collective-permute-start(bf16[4,96,128]{2,1,0:T(8,128)(2,1)S(1)} %get-tuple-element.43), channel_id=1, source_target_pairs={{0,6},{1,7},{2,4},{3,5},{4,2},{5,3},{6,0},{7,1},{8,14},{9,15},{10,... | collective-permute-start | bytes 294920 | tf_op jit(solution)/shard_map/ppermute | solution.py:318
  129.5 1.7 %collective-permute-done.14 = bf16[4,96,128]{2,1,0:T(8,128)(2,1)S(1)} collective-permute-done((bf16[4,96,128]{2,1,0:T(8,128)(2,1)S(1)}, bf16[4,96,128]{2,1,0:T(8,128)(2,1)S(1)}, u32[]{:S(2)}, u32[]{:S(2)}) %collective-permute-start.14) | collective-permute-done | bytes 98336 | tf_op jit(solution)/shard_map/ppermute | solution.py:318
  131.3 1.6 %collective-permute-done.15 = bf16[4,96,128]{2,1,0:T(8,128)(2,1)S(1)} collective-permute-done((bf16[4,96,128]{2,1,0:T(8,128)(2,1)S(1)}, bf16[4,96,128]{2,1,0:T(8,128)(2,1)S(1)}, u32[]{:S(2)}, u32[]{:S(2)}) %collective-permute-start.15) | collective-permute-done | bytes 98336 | tf_op jit(solution)/shard_map/ppermute | solution.py:318
  133.0 9.2 %collective-permute-start.16 = (bf16[4,4,96,128]{3,2,1,0:T(8,128)(2,1)S(1)}, bf16[4,4,96,128]{3,2,1,0:T(8,128)(2,1)S(1)}, u32[]{:S(2)}, u32[]{:S(2)}) collective-permute-start(bf16[4,4,96,128]{3,2,1,0:T(8,128)(2,1)S(1)} %get-tuple-element.38), channel_id=1, source_target_pairs={{0,1},{1,0},{2,3},{3,2},{4,5},{5,4},{6,7},{7,6},{8,9},{9,8},{10,11... | collective-permute-start | bytes 1179656 | tf_op jit(solution)/shard_map/ppermute | solution.py:318
  143.6 3.6 %unpack.1 = (f32[200,800]{1,0:T(8,128)}, f32[800,200]{1,0:T(8,128)S(1)}, f32[200,49]{1,0:T(8,128)S(1)}) custom-call(s32[1]{0:T(128)} %bitcast.9.me, bf16[32,96,128]{2,1,0:T(8,128)(2,1)S(1)} %bitcast.87), custom_call_target="tpu_custom_call" | custom-call | tf_op jit(solution)/shard_map/unpack/pallas_call | solution.py:302
  (70 shorter events, 21.2 us)
Async XLA Ops:
  0.6 64.1 %copy-start = (bf16[200,800]{1,0:T(8,128)(2,1)S(1)}, bf16[200,800]{1,0:T(8,128)(2,1)}, u32[]{:S(2)}) copy-start(bf16[200,800]{1,0:T(8,128)(2,1)} %param.17) | copy-start | bytes 960004
  0.6 55.0 %copy-start.4 = (s32[32]{0:T(128)S(1)}, s32[32]{0:T(128)}, u32[]{:S(2)}) copy-start(s32[32]{0:T(128)} %owner.3) | copy-start | bytes 388
  0.7 40.0 %copy-start.9 = (f32[200]{0:T(256)S(1)}, f32[200]{0:T(256)}, u32[]{:S(2)}) copy-start(f32[200]{0:T(256)} %param.16) | copy-start | bytes 2404
  0.7 40.1 %copy-start.8 = (f32[200]{0:T(256)S(1)}, f32[200]{0:T(256)}, u32[]{:S(2)}) copy-start(f32[200]{0:T(256)} %param.19) | copy-start | bytes 2404
  0.7 40.3 %copy-start.5 = (bf16[1,1,200,8,128]{4,3,2,1,0:T(8,128)(2,1)S(1)}, bf16[1,1,200,8,128]{4,3,2,1,0:T(8,128)(2,1)}, u32[]{:S(2)}) copy-start(bf16[1,1,200,8,128]{4,3,2,1,0:T(8,128)(2,1)} %param.11) | copy-start | bytes 1228804
  2.9 25.1 %all-to-all-start = ((bf16[32,7,8,128]{3,2,1,0:T(8,128)(2,1)}), bf16[32,7,8,128]{3,2,1,0:T(8,128)(2,1)S(1)}, u32[]{:S(2)}, u32[]{:S(2)}) async-start(bf16[32,7,8,128]{3,2,1,0:T(8,128)(2,1)} %bitcast.3), calls=%async_computation | async-start | bytes 917504 | tf_op jit(solution)/shard_map/all_to_all | solution.py:358
  36.5 19.2 %all-to-all-start.1 = ((bf16[32,7,8,128]{3,2,1,0:T(8,128)(2,1)}), bf16[32,7,8,128]{3,2,1,0:T(8,128)(2,1)S(1)}, u32[]{:S(2)}, u32[]{:S(2)}) async-start(bf16[32,7,8,128]{3,2,1,0:T(8,128)(2,1)} %compose.1), calls=%async_computation.1 | async-start | bytes 917504 | tf_op jit(solution)/shard_map/all_to_all | solution.py:361
  84.3 2.4 %collective-permute-start = (f32[16,96,128]{2,1,0:T(8,128)S(1)}, f32[16,96,128]{2,1,0:T(8,128)S(1)}, u32[]{:S(2)}, u32[]{:S(2)}) collective-permute-start(f32[16,96,128]{2,1,0:T(8,128)S(1)} %get-tuple-element.22), channel_id=1, source_target_pairs={{0,1},{1,0},{2,3},{3,2},{4,5},{5,4},{6,7},{7,6},{8,9},{9,8},{10,11... | collective-permute-start | bytes 2359304 | tf_op jit(solution)/shard_map/ppermute | solution.py:318
  86.8 11.9 %collective-permute-start.3 = (f32[4,96,128]{2,1,0:T(8,128)S(1)}, f32[4,96,128]{2,1,0:T(8,128)S(1)}, u32[]{:S(2)}, u32[]{:S(2)}) collective-permute-start(f32[4,96,128]{2,1,0:T(8,128)S(1)} %get-tuple-element.34), channel_id=1, source_target_pairs={{0,6},{1,7},{2,4},{3,5},{4,2},{5,3},{6,0},{7,1},{8,14},{9,15},{10,... | collective-permute-start | bytes 589832 | tf_op jit(solution)/shard_map/ppermute | solution.py:318
  88.1 10.6 %collective-permute-start.2 = (f32[4,96,128]{2,1,0:T(8,128)S(1)}, f32[4,96,128]{2,1,0:T(8,128)S(1)}, u32[]{:S(2)}, u32[]{:S(2)}) collective-permute-start(f32[4,96,128]{2,1,0:T(8,128)S(1)} %get-tuple-element.35), channel_id=1, source_target_pairs={{0,4},{1,5},{2,6},{3,7},{4,0},{5,1},{6,2},{7,3},{8,12},{9,13},{10,... | collective-permute-start | bytes 589832 | tf_op jit(solution)/shard_map/ppermute | solution.py:318
  89.1 9.8 %collective-permute-start.1 = (f32[4,96,128]{2,1,0:T(8,128)S(1)}, f32[4,96,128]{2,1,0:T(8,128)S(1)}, u32[]{:S(2)}, u32[]{:S(2)}) collective-permute-start(f32[4,96,128]{2,1,0:T(8,128)S(1)} %get-tuple-element.36), channel_id=1, source_target_pairs={{0,2},{1,3},{2,0},{3,1},{4,6},{5,7},{6,4},{7,5},{8,10},{9,11},{10,... | collective-permute-start | bytes 589832 | tf_op jit(solution)/shard_map/ppermute | solution.py:318
  99.0 4.3 %collective-permute-start.6 = (f32[96,128]{1,0:T(8,128)S(1)}, f32[96,128]{1,0:T(8,128)S(1)}, u32[]{:S(2)}, u32[]{:S(2)}) collective-permute-start(f32[96,128]{1,0:T(8,128)S(1)} %get-tuple-element.39), channel_id=1, source_target_pairs={{0,192},{1,193},{2,194},{3,195},{4,196},{5,197},{6,198},{7,199},{8... | collective-permute-start | bytes 147464 | tf_op jit(solution)/shard_map/ppermute | solution.py:318
  101.9 4.4 %collective-permute-start.5 = (f32[96,128]{1,0:T(8,128)S(1)}, f32[96,128]{1,0:T(8,128)S(1)}, u32[]{:S(2)}, u32[]{:S(2)}) collective-permute-start(f32[96,128]{1,0:T(8,128)S(1)} %get-tuple-element.40), channel_id=1, source_target_pairs={{0,128},{1,129},{2,130},{3,131},{4,132},{5,133},{6,134},{7,135},{8... | collective-permute-start | bytes 147464 | tf_op jit(solution)/shard_map/ppermute | solution.py:318
  102.2 4.1 %collective-permute-start.4 = (f32[96,128]{1,0:T(8,128)S(1)}, f32[96,128]{1,0:T(8,128)S(1)}, u32[]{:S(2)}, u32[]{:S(2)}) collective-permute-start(f32[96,128]{1,0:T(8,128)S(1)} %get-tuple-element.41), channel_id=1, source_target_pairs={{0,64},{1,65},{2,66},{3,67},{4,68},{5,69},{6,70},{7,71},{8,72},{9,... | collective-permute-start | bytes 147464 | tf_op jit(solution)/shard_map/ppermute | solution.py:318
  106.3 3.0 %collective-permute-start.7 = (f32[96,128]{1,0:T(8,128)S(1)}, f32[96,128]{1,0:T(8,128)S(1)}, u32[]{:S(2)}, u32[]{:S(2)}) collective-permute-start(f32[96,128]{1,0:T(8,128)S(1)} %fusion.18), channel_id=1, source_target_pairs={{0,8},{1,9},{2,10},{3,11},{4,12},{5,13},{6,14},{7,15},{8,0},{9,1},... | collective-permute-start | bytes 147464 | tf_op jit(solution)/shard_map/ppermute | solution.py:318
  109.4 4.6 %collective-permute-start.8 = (f32[96,128]{1,0:T(8,128)S(1)}, f32[96,128]{1,0:T(8,128)S(1)}, u32[]{:S(2)}, u32[]{:S(2)}) collective-permute-start(f32[96,128]{1,0:T(8,128)S(1)} %add.69), channel_id=1, source_target_pairs={{0,16},{1,17},{2,18},{3,19},{4,20},{5,21},{6,22},{7,23},{8,24},{9,... | collective-permute-start | bytes 147464 | tf_op jit(solution)/shard_map/ppermute | solution.py:318
  114.0 6.9 %collective-permute-start.9 = (f32[96,128]{1,0:T(8,128)S(1)}, f32[96,128]{1,0:T(8,128)S(1)}, u32[]{:S(2)}, u32[]{:S(2)}) collective-permute-start(f32[96,128]{1,0:T(8,128)S(1)} %add.70), channel_id=1, source_target_pairs={{0,32},{1,33},{2,34},{3,35},{4,36},{5,37},{6,38},{7,39},{8,40},{9,... | collective-permute-start | bytes 147464 | tf_op jit(solution)/shard_map/ppermute | solution.py:318
  120.9 4.3 %collective-permute-start.12 = (bf16[96,128]{1,0:T(8,128)(2,1)S(1)}, bf16[96,128]{1,0:T(8,128)(2,1)S(1)}, u32[]{:S(2)}, u32[]{:S(2)}) collective-permute-start(bf16[96,128]{1,0:T(8,128)(2,1)S(1)} %add_convert_fusion), channel_id=1, source_target_pairs={{0,192},{1,193},{2,194},{3,195},{4,196},{5,197},{6,198},{7,199},{8... | collective-permute-start | bytes 73736 | tf_op jit(solution)/shard_map/ppermute | solution.py:318
  121.9 4.2 %collective-permute-start.11 = (bf16[96,128]{1,0:T(8,128)(2,1)S(1)}, bf16[96,128]{1,0:T(8,128)(2,1)S(1)}, u32[]{:S(2)}, u32[]{:S(2)}) collective-permute-start(bf16[96,128]{1,0:T(8,128)(2,1)S(1)} %add_convert_fusion), channel_id=1, source_target_pairs={{0,128},{1,129},{2,130},{3,131},{4,132},{5,133},{6,134},{7,135},{8... | collective-permute-start | bytes 73736 | tf_op jit(solution)/shard_map/ppermute | solution.py:318
  122.7 3.4 %collective-permute-start.10 = (bf16[96,128]{1,0:T(8,128)(2,1)S(1)}, bf16[96,128]{1,0:T(8,128)(2,1)S(1)}, u32[]{:S(2)}, u32[]{:S(2)}) collective-permute-start(bf16[96,128]{1,0:T(8,128)(2,1)S(1)} %add_convert_fusion), channel_id=1, source_target_pairs={{0,64},{1,65},{2,66},{3,67},{4,68},{5,69},{6,70},{7,71},{8,72},{9,... | collective-permute-start | bytes 73736 | tf_op jit(solution)/shard_map/ppermute | solution.py:318
  126.2 5.1 %collective-permute-start.14 = (bf16[4,96,128]{2,1,0:T(8,128)(2,1)S(1)}, bf16[4,96,128]{2,1,0:T(8,128)(2,1)S(1)}, u32[]{:S(2)}, u32[]{:S(2)}) collective-permute-start(bf16[4,96,128]{2,1,0:T(8,128)(2,1)S(1)} %get-tuple-element.43), channel_id=1, source_target_pairs={{0,4},{1,5},{2,6},{3,7},{4,0},{5,1},{6,2},{7,3},{8,12},{9,13},{10,... | collective-permute-start | bytes 294920 | tf_op jit(solution)/shard_map/ppermute | solution.py:318
  127.3 4.0 %collective-permute-start.13 = (bf16[4,96,128]{2,1,0:T(8,128)(2,1)S(1)}, bf16[4,96,128]{2,1,0:T(8,128)(2,1)S(1)}, u32[]{:S(2)}, u32[]{:S(2)}) collective-permute-start(bf16[4,96,128]{2,1,0:T(8,128)(2,1)S(1)} %get-tuple-element.43), channel_id=1, source_target_pairs={{0,2},{1,3},{2,0},{3,1},{4,6},{5,7},{6,4},{7,5},{8,10},{9,11},{10,... | collective-permute-start | bytes 294920 | tf_op jit(solution)/shard_map/ppermute | solution.py:318
  128.0 5.0 %collective-permute-start.15 = (bf16[4,96,128]{2,1,0:T(8,128)(2,1)S(1)}, bf16[4,96,128]{2,1,0:T(8,128)(2,1)S(1)}, u32[]{:S(2)}, u32[]{:S(2)}) collective-permute-start(bf16[4,96,128]{2,1,0:T(8,128)(2,1)S(1)} %get-tuple-element.43), channel_id=1, source_target_pairs={{0,6},{1,7},{2,4},{3,5},{4,2},{5,3},{6,0},{7,1},{8,14},{9,15},{10,... | collective-permute-start | bytes 294920 | tf_op jit(solution)/shard_map/ppermute | solution.py:318
  133.0 10.6 %collective-permute-start.16 = (bf16[4,4,96,128]{3,2,1,0:T(8,128)(2,1)S(1)}, bf16[4,4,96,128]{3,2,1,0:T(8,128)(2,1)S(1)}, u32[]{:S(2)}, u32[]{:S(2)}) collective-permute-start(bf16[4,4,96,128]{3,2,1,0:T(8,128)(2,1)S(1)} %get-tuple-element.38), channel_id=1, source_target_pairs={{0,1},{1,0},{2,3},{3,2},{4,5},{5,4},{6,7},{7,6},{8,9},{9,8},{10,11... | collective-permute-start | bytes 1179656 | tf_op jit(solution)/shard_map/ppermute | solution.py:318
  (6 other events, 66.5 us)

commit v2 on v1

v2 whole, which is shorter than its diff:
```python
import jax
import jax.numpy as jnp
from jax import lax
from jax.experimental import pallas as pl
from jax.experimental.pallas import tpu as pltpu
from jax.sharding import PartitionSpec as P

LEVELS = 19
TILES = 32
CH = 200
PARTS = 7
ROWS = 8
COLS = 128
EXT = 14
TAPS = 7
HID = 800
CELLS = ROWS * COLS
CHUNKS = 32
SUB = 11
TILES_IN = 175

root_half = 0.7071067811865476
gauss_norm = 0.3989422804014327
norm_epsilon = 1e-06
f32 = jnp.float32
bf16 = jnp.bfloat16
AXES = ("ens", "tile")
BIG = 24 << 20


def gelu_value(values):
    return 0.5 * values * (1.0 + lax.erf(values * root_half))


def gelu_slope(values):
    return (
        0.5 * (1.0 + lax.erf(values * root_half))
        + values * jnp.exp(-0.5 * values * values) * gauss_norm
    )


def link_at(links, tile_id, column):
    return jnp.where(tile_id >= 0, links[jnp.maximum(tile_id, 0), column], -1)


def compose_kernel(links, owner, x_ref, o_ref, inverse):
    shape = (PARTS, ROWS, COLS)
    row = lax.broadcasted_iota(jnp.int32, shape, 1)
    lane = lax.broadcasted_iota(jnp.int32, shape, 2)
    edge = (lane < 3) | (lane >= COLS - 3)
    east_side = lane < 64

    def note(k, _):
        inverse[owner[k]] = k
        return 0

    lax.fori_loop(0, TILES, note, 0)

    def load(tile_id):
        slot = jnp.where(tile_id >= 0, owner[jnp.maximum(tile_id, 0)], 0)
        block = x_ref[slot].astype(f32)
        return jnp.where(tile_id >= 0, block, 0.0)

    def north_of(tile_id):
        block = load(link_at(links, tile_id, 0))
        return jnp.where(link_at(links, tile_id, 4) == 1, pltpu.roll(block, 3, 1), block)

    def body(d, _):
        own = inverse[d]
        west = link_at(links, own, 2)
        east = link_at(links, own, 3)
        north_rows = north_of(own)
        south_rows = load(link_at(links, own, 1))
        sides = jnp.where(edge, jnp.where(east_side, load(east), load(west)), 0.0)
        north_side = (lane < 64) != (link_at(links, own, 4) == 1)
        north_corner = jnp.where(north_side, north_of(east), north_of(west))
        south_corner = jnp.where(
            east_side, load(link_at(links, east, 1)), load(link_at(links, west, 1))
        )
        corners = jnp.where(row < 3, north_corner, south_corner)
        corners = jnp.where(edge & ((row < 3) | (row > 4)), corners, 0.0)
        spread = pltpu.roll(
            sides + pltpu.roll(corners, 64, 2), 24, 2, stride=8, stride_axis=1
        )
        packed = jnp.sum(spread, axis=1, keepdims=True)
        block = jnp.where(row == 3, packed, jnp.where(row < 3, north_rows, south_rows))
        o_ref[d] = block.astype(bf16)
        return 0

    lax.fori_loop(0, TILES, body, 0, unroll=8)


def compose(links, owner, chunks):
    smem = pl.BlockSpec(memory_space=pltpu.SMEM)
    vmem = pl.BlockSpec(memory_space=pltpu.VMEM)
    return pl.pallas_call(
        compose_kernel,
        out_shape=jax.ShapeDtypeStruct((TILES, PARTS, ROWS, COLS), bf16),
        in_specs=[smem, smem, vmem],
        out_specs=vmem,
        scratch_shapes=[pltpu.SMEM((TILES,), jnp.int32)],
        compiler_params=pltpu.CompilerParams(vmem_limit_bytes=BIG),
        name="compose",
    )(links, owner, chunks)


def chosen(center, halo, col_off, lane):
    if col_off < 3:
        return jnp.where(lane >= COLS - 3 + col_off, halo, center)
    if col_off > 3:
        return jnp.where(lane < col_off - 3, halo, center)
    return center


def turned(values, col_off):
    return values if col_off == 3 else pltpu.roll(values, (3 - col_off) % COLS, 1)


def extended_rows(own_rows, ext, halo, at, col_off, lane):
    rows = [ext[r, at, :] for r in range(3)]
    rows += [own_rows[r, at, :] for r in range(ROWS)]
    rows += [ext[r, at, :] for r in range(3, 6)]
    return [chosen(x, halo[r, at, :], col_off, lane) for r, x in enumerate(rows)]


def prepare_kernel(m_ref, coef, own, wide, flat_ref, mine):
    mine[...] = m_ref[0:CH].astype(f32).reshape(CH * ROWS, COLS)
    for r in range(ROWS):
        values = mine[pl.ds(r, CH, stride=ROWS), :]
        own[r] = values
        flat_ref[:, COLS * r : COLS * r + COLS] = values.astype(bf16)
    for k in range(TAPS * TAPS):
        wide[k] = jnp.broadcast_to(coef[:, k : k + 1], (CH, COLS))


def prepare(payload, coef):
    vmem = pl.BlockSpec(memory_space=pltpu.VMEM)
    return pl.pallas_call(
        prepare_kernel,
        out_shape=[
            jax.ShapeDtypeStruct((ROWS, CH, COLS), f32),
            jax.ShapeDtypeStruct((TAPS * TAPS, CH, COLS), f32),
            jax.ShapeDtypeStruct((CH, CELLS), bf16),
        ],
        in_specs=[vmem, vmem],
        out_specs=[vmem] * 3,
        scratch_shapes=[pltpu.VMEM((CH * ROWS, COLS), f32)],
        compiler_params=pltpu.CompilerParams(vmem_limit_bytes=BIG),
        name="prepare",
    )(payload, coef)


def conv_kernel(
    links, owner, own_slot, own_rows, taps, r_ref, coef, cen_ref, norm_ref, inv_ref, ext, halo, rims, wide, arrived
):
    fetch = pltpu.make_async_copy(taps, wide, arrived)
    fetch.start()
    slot = own_slot[0]

    def find(k, best):
        return jnp.where(owner[k] == slot, k, best)

    own = lax.fori_loop(0, TILES, find, 0)
    fold = links[own, 4] == 1
    rims[...] = r_ref[0:CH].astype(f32).reshape(CH * ROWS, COLS)
    row = lax.broadcasted_iota(jnp.int32, (COLS, COLS), 0)
    col = lax.broadcasted_iota(jnp.int32, (COLS, COLS), 1)
    turn = (row == jnp.where(fold, COLS - 1 - col, col)).astype(f32).astype(bf16)
    edges = rims[pl.ds(3, CH, stride=ROWS), :]
    for r in range(11):
        halo[r] = edges if r == 0 else pltpu.roll(edges, COLS - 8 * r, 1)
    north = [rims[pl.ds(t, CH, stride=ROWS), :] for t in range(3)]
    corner = [pltpu.roll(edges, COLS - 8 * (11 + t), 1) for t in range(3)]
    for t in range(3):
        ext[t] = rims[pl.ds(5 + t, CH, stride=ROWS), :]
        for dest, source, first in ((ext, north, 3), (halo, corner, 11)):
            raw = jnp.where(fold, source[2 - t], source[t]).astype(bf16)
            dest[first + t] = jnp.dot(raw, turn, preferred_element_type=f32)
    lane = lax.broadcasted_iota(jnp.int32, (8, COLS), 1)
    fetch.wait()

    def block(i, sums):
        at = pl.ds(pl.multiple_of(8 * i, 8), 8)
        acc = [jnp.zeros((8, COLS), f32) for _ in range(ROWS)]
        for b in range(TAPS):
            moved = extended_rows(own_rows, ext, halo, at, b, lane)
            part = [None] * ROWS
            for a in range(TAPS):
                tap = wide[7 * a + b, at, :]
                for r in range(ROWS):
                    term = tap * moved[r + a]
                    part[r] = term if a == 0 else part[r] + term
            for r in range(ROWS):
                acc[r] = acc[r] + turned(part[r], b)
        for r in range(ROWS):
            cen_ref[at, COLS * r : COLS * r + COLS] = acc[r]
        return tuple(s + x for s, x in zip(sums, acc))

    sums = lax.fori_loop(0, CH // 8, block, tuple(jnp.zeros((8, COLS), f32) for _ in range(ROWS)))
    gain = jnp.broadcast_to(coef[:, 49:50], (CH, COLS))
    for r in range(ROWS):
        at = slice(COLS * r, COLS * r + COLS)
        mean = jnp.sum(sums[r], axis=0, keepdims=True) * (1.0 / CH)
        off = cen_ref[:, at] - mean
        var = jnp.sum(off * off, axis=0, keepdims=True) * (1.0 / CH)
        inv = 1.0 / jnp.sqrt(var + norm_epsilon)
        centred = off * inv
        cen_ref[:, at] = centred
        norm_ref[:, at] = (centred * gain).astype(bf16)
        inv_ref[r : r + 1, :] = inv


def forward_conv(links, owner, own_slot, own_rows, wide, rims, coef):
    smem = pl.BlockSpec(memory_space=pltpu.SMEM)
    vmem = pl.BlockSpec(memory_space=pltpu.VMEM)
    shapes = [
        ((CH, CELLS), f32),
        ((CH, CELLS), bf16),
        ((ROWS, COLS), f32),
        ((6, CH, COLS), f32),
        ((EXT, CH, COLS), f32),
    ]
    return pl.pallas_call(
        conv_kernel,
        out_shape=[jax.ShapeDtypeStruct(s, d) for s, d in shapes],
        in_specs=[smem, smem, smem, vmem, pl.BlockSpec(memory_space=pl.ANY), vmem, vmem],
        out_specs=[vmem] * len(shapes),
        scratch_shapes=[
            pltpu.VMEM((CH * ROWS, COLS), f32),
            pltpu.VMEM((TAPS * TAPS, CH, COLS), f32),
            pltpu.SemaphoreType.DMA,
        ],
        compiler_params=pltpu.CompilerParams(vmem_limit_bytes=BIG),
        name="forward_conv",
    )(links, owner, own_slot, own_rows, wide, rims, coef)


def grad_kernel(
    me, gn_ref, cen_ref, inv_ref, own_rows, ext, halo, coef, in_ref, out_ref, packed, gconv, terms_ref
):
    gain = jnp.broadcast_to(coef[:, 49:50], (CH, COLS))
    for r in range(ROWS):
        at = slice(COLS * r, COLS * r + COLS)
        scaled = gn_ref[:, at] * gain
        centred = cen_ref[:, at]
        mean = jnp.sum(scaled, axis=0, keepdims=True) * (1.0 / CH)
        along = jnp.sum(scaled * centred, axis=0, keepdims=True) * (1.0 / CH)
        gconv[:, at] = (scaled - mean - centred * along) * inv_ref[r : r + 1, :]
    lane = lax.broadcasted_iota(jnp.int32, (8, COLS), 1)

    def block(i, _):
        at = pl.ds(pl.multiple_of(8 * i, 8), 8)
        grads = [gconv[at, COLS * r : COLS * r + COLS] for r in range(ROWS)]
        for b in range(TAPS):
            moved = extended_rows(own_rows, ext, halo, at, b, lane)
            back = [turned(g, 6 - b) for g in grads]
            for a in range(TAPS):
                terms = back[0] * moved[a]
                for r in range(1, ROWS):
                    terms = terms + back[r] * moved[r + a]
                terms_ref[7 * a + b, at, :] = terms
        return 0

    lax.fori_loop(0, CH // 8, block, 0)
    ones = jnp.ones((COLS, COLS), bf16)
    wide_lane = lax.broadcasted_iota(jnp.int32, (CH, COLS), 1)
    found = jnp.zeros((CH, COLS), f32)
    for k in range(TAPS * TAPS):
        terms = terms_ref[k]
        high = terms.astype(bf16)
        low = (terms - high.astype(f32)).astype(bf16)
        total = jnp.dot(high, ones, preferred_element_type=f32)
        total = total + jnp.dot(low, ones, preferred_element_type=f32)
        found = jnp.where(wide_lane == 32 + k, total, found)
    place = [chunk ^ me[0] for chunk in range(CHUNKS)]
    blank = jnp.zeros((8, 96), f32)
    for t in range(CHUNKS * SUB):
        source, at = (in_ref, t) if t < TILES_IN else (out_ref, t - TILES_IN)
        i, l = at // 7, at % 7
        if i >= CH // 8:
            tile = jnp.zeros((8, COLS), f32)
        elif l < 6:
            tile = source[8 * i : 8 * i + 8, COLS * l : COLS * l + COLS]
        else:
            tile = jnp.concatenate([source[8 * i : 8 * i + 8, 6 * COLS : HID], blank], axis=1)
            if t < TILES_IN:
                tile = jnp.where(lane < 32, tile, found[8 * i : 8 * i + 8, :])
        at = 8 * (t % SUB)
        packed[place[t // SUB], at : at + 8, :] = tile


def backward_conv(me, gn, cen, inv, own_rows, ext, halo, coef, part_in, part_out):
    smem = pl.BlockSpec(memory_space=pltpu.SMEM)
    vmem = pl.BlockSpec(memory_space=pltpu.VMEM)
    return pl.pallas_call(
        grad_kernel,
        out_shape=jax.ShapeDtypeStruct((CHUNKS, 8 * SUB, COLS), f32),
        in_specs=[smem] + [vmem] * 9,
        out_specs=vmem,
        scratch_shapes=[
            pltpu.VMEM((CH, CELLS), f32),
            pltpu.VMEM((TAPS * TAPS, CH, COLS), f32),
        ],
        compiler_params=pltpu.CompilerParams(vmem_limit_bytes=BIG),
        name="backward_conv",
    )(me, gn, cen, inv, own_rows, ext, halo, coef, part_in, part_out)


def unpack_kernel(me, x_ref, in_ref, out_ref, k_ref, taps):
    share = 1.0 / (8 * TILES * CH * CELLS)
    for chunk in range(CHUNKS):
        values = x_ref[chunk ^ me[0]].astype(f32) * share
        for p in range(SUB):
            t = SUB * chunk + p
            dest, at = (in_ref, t) if t < TILES_IN else (out_ref, t - TILES_IN)
            i, l = at // 7, at % 7
            tile = values[8 * p : 8 * p + 8, :]
            if i >= CH // 8:
                continue
            if l < 6:
                dest[8 * i : 8 * i + 8, COLS * l : COLS * l + COLS] = tile
            else:
                dest[8 * i : 8 * i + 8, 6 * COLS : HID] = tile[:, 0:32]
                if t < TILES_IN:
                    taps[8 * i : 8 * i + 8, :] = tile
    taps[CH:256, :] = jnp.zeros((256 - CH, COLS), f32)
    k_ref[...] = jnp.transpose(taps[...])[32:81, 0:CH]


def unpack(me, gathered):
    vmem = pl.BlockSpec(memory_space=pltpu.VMEM)
    return pl.pallas_call(
        unpack_kernel,
        out_shape=[
            jax.ShapeDtypeStruct((CH, HID), f32),
            jax.ShapeDtypeStruct((CH, HID), f32),
            jax.ShapeDtypeStruct((49, CH), f32),
        ],
        in_specs=[pl.BlockSpec(memory_space=pltpu.SMEM), vmem],
        out_specs=[vmem] * 3,
        scratch_shapes=[pltpu.VMEM((256, COLS), f32)],
        compiler_params=pltpu.CompilerParams(vmem_limit_bytes=BIG),
        name="unpack",
    )(me, gathered)


def swap(values, bits):
    return lax.ppermute(values, AXES, [(i, i ^ bits) for i in range(256)])


def reduce_all(held):
    held = (held[:16] + swap(held[16:], 1)).reshape(4, 4, 8 * SUB, COLS)
    sent = [swap(held[k].astype(bf16), k << 1).astype(f32) for k in (1, 2, 3)]
    held = (held[0] + sent[0]) + (sent[1] + sent[2])
    held = (held[0] + swap(held[1], 64)) + (swap(held[2], 128) + swap(held[3], 192))
    held = (held + swap(held, 8)) + (swap(held, 16) + swap(held, 24))
    held = held + swap(held, 32)
    part = held.astype(bf16)
    part = jnp.stack([part] + [swap(part, k << 6) for k in (1, 2, 3)])
    part = jnp.stack([part] + [swap(part, k << 1) for k in (1, 2, 3)])
    part = jnp.stack([part, swap(part, 1)])
    return part.reshape(CHUNKS, 8 * SUB, COLS)


def local(
    fields,
    target,
    wet_levels,
    tile_links,
    tile_owner,
    kernel,
    norm_gain,
    weight_in,
    weight_out,
    layer_scale,
):
    tile_at = lax.axis_index("tile").astype(jnp.int32)
    ens_at = lax.axis_index("ens").astype(jnp.int32)
    own_slot = tile_at.reshape(1)
    me = ((tile_at & 1) * 16 + ((tile_at >> 1) & 3) * 4 + (ens_at >> 1)).reshape(1)
    level_of = jnp.arange(TILES * PARTS, dtype=jnp.int32) * LEVELS // CH
    wet_mask = wet_levels[0][None, :, :] > level_of[:, None, None]
    own_input = jnp.pad(fields[0, 0], ((0, TILES * PARTS - CH), (0, 0), (0, 0)))
    payload = jnp.where(wet_mask, own_input, jnp.zeros_like(own_input))
    coef = jnp.concatenate([kernel, norm_gain[:, None], layer_scale[:, None]], axis=1)

    own_rows, wide, flat_masked = prepare(payload, coef)
    chunks = lax.all_to_all(
        payload.reshape(TILES, PARTS, ROWS, COLS), "tile", 0, 0, tiled=True
    )
    rims = lax.all_to_all(compose(tile_links, tile_owner, chunks), "tile", 0, 0, tiled=True)
    rims = rims.reshape(TILES * PARTS, ROWS, COLS)
    centred, flat_norm, inv_std, ext, halo = forward_conv(
        tile_links, tile_owner, own_slot, own_rows, wide, rims, coef
    )

    scale_wide = layer_scale[:, None]
    hidden = jnp.einsum("ch,cp->hp", weight_in, flat_norm, preferred_element_type=f32)
    activated = gelu_value(hidden).astype(bf16)
    mlp_out = jnp.einsum("hc,hp->cp", weight_out, activated, preferred_element_type=f32)
    block_out = (flat_masked.astype(f32) + scale_wide * mlp_out).astype(bf16)
    flat_wet = wet_levels[0].reshape(1, CELLS) > level_of[:CH, None]
    misfit = jnp.where(
        flat_wet, block_out.astype(f32) - target[0, 0].reshape(CH, CELLS).astype(f32), 0.0
    )
    grad_mlp = (2.0 * scale_wide * misfit).astype(bf16)
    part_out = jnp.einsum("cp,hp->ch", grad_mlp, activated, preferred_element_type=f32)
    grad_act = jnp.einsum("hc,cp->hp", weight_out, grad_mlp, preferred_element_type=f32)
    grad_hidden = (grad_act * gelu_slope(hidden)).astype(bf16)
    part_in = jnp.einsum("cp,hp->ch", flat_norm, grad_hidden, preferred_element_type=f32)
    grad_normed = jnp.einsum("ch,hp->cp", weight_in, grad_hidden, preferred_element_type=f32)

    packed = backward_conv(
        me, grad_normed, centred, inv_std, own_rows, ext, halo, coef, part_in, part_out
    )
    grad_in, grad_out, grad_taps = unpack(me, reduce_all(packed))
    return block_out.reshape(1, 1, CH, ROWS, COLS), grad_in, grad_out.T, grad_taps.T


def solution(mesh):
    placed = (
        P("ens", "tile", None, None, None),
        P("ens", "tile", None, None, None),
        P("tile", None, None),
        P(),
        P(),
        P(),
        P(),
        P(),
        P(),
        P(),
    )
    return jax.shard_map(
        local,
        mesh=mesh,
        in_specs=placed,
        out_specs=(P("ens", "tile", None, None, None), P(), P(), P()),
        check_vma=False,
    )
```

time: 149 us -> 127 us (0.85)
  waiting for transfers between devices: 58.5 us -> 43.8 us
  Pallas kernels: 33.9 us -> 21.4 us
  local copies, waits for them, and re-layouts: 5.35 us -> 7.4 us
  starting transfers between devices: 42.5 us -> 44.5 us
    ppermute x17 -> x18, waiting for transfers between devices: 29.7 us -> 19.9 us  [swap(): return lax.ppermute(values, AXES, [(i, i ^ bits) for i in range(256)])]
    all_to_all x1, waiting for transfers between devices: 14.5 us -> 9.56 us  [local(): lax.all_to_all(compose(tile_links, tile_owner, chunks), 'tile', 0, 0, til...]
    pallas_call x1, Pallas kernels: 7.81 us -> 3.45 us  [compose(): pl.pallas_call(compose_kernel, out_shape=jax.ShapeDtypeStruct((TILES, PAR...]
    pallas_call x1 -> x2, Pallas kernels: 13.5 us -> 10 us  [the longest x1 7.38 us: backward_conv(): pl.pallas_call(grad_kernel, out_shape=jax.ShapeDtypeStruct((CHUNKS, 8 * S...]
    unnamed x27 -> x25, local copies, waits for them, and re-layouts: 4.26 us -> 7.08 us
    pallas_call x1, Pallas kernels: 9.04 us -> 6.66 us  [forward_conv(): pl.pallas_call(conv_kernel, out_shape=[jax.ShapeDtypeStruct(s, d) for s,...]
    pallas_call x1, Pallas kernels: 3.58 us -> 1.21 us  [unpack(): pl.pallas_call(unpack_kernel, out_shape=[jax.ShapeDtypeStruct((CH, HID),...]
    ppermute x17 -> x18, starting transfers between devices: 28.4 us -> 30.4 us  [swap(): return lax.ppermute(values, AXES, [(i, i ^ bits) for i in range(256)])]
  transfers between devices with their start and end apart: 19 -> 20, of which waited for: 16 -> 17; matrix products, arithmetic and copies ran while one was open for 1% -> 2% of each run, Pallas kernels for 0% -> 2%
where the time goes in v2:
time: 127 us
  starting transfers between devices  44.5 us (35%)
  waiting for transfers between devices  43.8 us (34%)
  Pallas kernels  21.4 us (17%)
  local copies, waits for them, and re-layouts  7.4 us (6%)
  matrix products  6.08 us (5%)
  other arithmetic  2.77 us (2%)
    ppermute x18, starting transfers between devices, swap(): return lax.ppermute(values, AXES, [(i, i ^ bits) for i in range(256)])  30.4 us
    ppermute x18, waiting for transfers between devices, swap(): return lax.ppermute(values, AXES, [(i, i ^ bits) for i in range(256)])  19.9 us
    all_to_all x1, waiting for transfers between devices, local(): lax.all_to_all(payload.reshape(TILES, PARTS, ROWS, COLS), 'tile', 0, 0, t...  14.3 us
    all_to_all x1, starting transfers between devices, local(): lax.all_to_all(payload.reshape(TILES, PARTS, ROWS, COLS), 'tile', 0, 0, t...  10 us
    all_to_all x1, waiting for transfers between devices, local(): lax.all_to_all(compose(tile_links, tile_owner, chunks), 'tile', 0, 0, til...  9.56 us
    pallas_call x1, Pallas kernels, backward_conv(): pl.pallas_call(grad_kernel, out_shape=jax.ShapeDtypeStruct((CHUNKS, 8 * S...  7.38 us
    unnamed x25, local copies, waits for them, and re-layouts  7.08 us
    pallas_call x1, Pallas kernels, forward_conv(): pl.pallas_call(conv_kernel, out_shape=[jax.ShapeDtypeStruct(s, d) for s,...  6.66 us
  transfers between devices with their start and end apart: 20, of which 17 were waited for; matrix products, arithmetic and copies ran while one was open for 2% of the time, Pallas kernels for 2%

profile of v2, /device:TPU:1, one launch (start us, length us, event | category | flops | bytes accessed | tf_op | source)
XLA Modules:
  0.0 126.8 jit_solution(5875583607027234347)
XLA Ops:
  0.7 2.2 %compare_select_fusion.m_ref = bf16[224,8,128]{2,1,0:T(8,128)(2,1)} fusion(bf16[200,8,128]{2,1,0:T(8,128)(2,1)} %bitcast.94, s32[8,128]{1,0:T(8,128)} %bitcast.103, s32[224]{0:T(256)S(1)} %and_select_fusion), kind=kLoop, calls=%fused_computation.18 | loop fusion | flops 458752 | bytes 873344 | tf_op jit(solution)/shard_map/jit(_where)/select_n | solution.py:384
  2.9 10.0 %all-to-all-start = ((bf16[32,7,8,128]{3,2,1,0:T(8,128)(2,1)}), bf16[32,7,8,128]{3,2,1,0:T(8,128)(2,1)S(1)}, u32[]{:S(2)}, u32[]{:S(2)}) async-start(bf16[32,7,8,128]{3,2,1,0:T(8,128)(2,1)} %bitcast.5), calls=%async_computation | async-start | bytes 917504 | tf_op jit(solution)/shard_map/all_to_all | solution.py:388
  13.7 14.3 %all-to-all-done.x_ref = bf16[32,7,8,128]{3,2,1,0:T(8,128)(2,1)S(1)} async-done(((bf16[32,7,8,128]{3,2,1,0:T(8,128)(2,1)}), bf16[32,7,8,128]{3,2,1,0:T(8,128)(2,1)S(1)}, u32[]{:S(2)}, u32[]{:S(2)}) %all-to-all-start) | async-done | bytes 458784 | tf_op jit(solution)/shard_map/all_to_all | solution.py:388
  28.7 3.4 %compose.1 = bf16[32,7,8,128]{3,2,1,0:T(8,128)(2,1)} custom-call(s32[32,5]{1,0:T(8,128)S(1)} %copy.21.links, s32[32]{0:T(128)S(1)} %copy-done.3, bf16[32,7,8,128]{3,2,1,0:T(8,128)(2,1)S(1)} %all-to-all-done.x_ref), custom_call_target="tpu_custom_call" | custom-call | tf_op jit(solution)/shard_map/compose/pallas_call | solution.py:96
  32.1 4.0 %all-to-all-start.1 = ((bf16[32,7,8,128]{3,2,1,0:T(8,128)(2,1)}), bf16[32,7,8,128]{3,2,1,0:T(8,128)(2,1)S(1)}, u32[]{:S(2)}, u32[]{:S(2)}) async-start(bf16[32,7,8,128]{3,2,1,0:T(8,128)(2,1)} %compose.1), calls=%async_computation.1 | async-start | bytes 917504 | tf_op jit(solution)/shard_map/all_to_all | solution.py:391
  36.8 2.7 %prepare.1 = (f32[8,200,128]{2,1,0:T(8,128)S(1)}, f32[49,200,128]{2,1,0:T(8,128)S(1)}, bf16[200,1024]{1,0:T(8,128)(2,1)S(1)}) custom-call(bf16[224,8,128]{2,1,0:T(8,128)(2,1)} %compare_select_fusion.m_ref, f32[200,51]{1,0:T(8,128)S(1)} %pad_maximum_fusion.2.coef), custom_call_target="tpu_custom_call" | custom-call | tf_op jit(solution)/shard_map/prepare/pallas_call | solution.py:138
  39.4 2.3 %copy-done.1 = f32[49,200,128]{2,1,0:T(8,128)} copy-done((f32[49,200,128]{2,1,0:T(8,128)}, f32[49,200,128]{2,1,0:T(8,128)S(1)}, u32[]{:S(2)}) %copy-start.1) | copy-done | bytes 5017624
  41.7 9.6 %all-to-all-done.1 = bf16[32,7,8,128]{3,2,1,0:T(8,128)(2,1)S(1)} async-done(((bf16[32,7,8,128]{3,2,1,0:T(8,128)(2,1)}), bf16[32,7,8,128]{3,2,1,0:T(8,128)(2,1)S(1)}, u32[]{:S(2)}, u32[]{:S(2)}) %all-to-all-start.1) | async-done | bytes 458784 | tf_op jit(solution)/shard_map/all_to_all | solution.py:391
  51.3 2.4 %copy-done.2 = f32[49,200,128]{2,1,0:T(8,128)S(1)} copy-done((f32[49,200,128]{2,1,0:T(8,128)S(1)}, f32[49,200,128]{2,1,0:T(8,128)}, u32[]{:S(2)}) %copy-start.2) | copy-done | bytes 5017624
  53.7 6.7 %forward_conv.1 = (f32[200,1024]{1,0:T(8,128)S(1)}, bf16[200,1024]{1,0:T(8,128)(2,1)S(1)}, f32[8,128]{1,0:T(8,128)S(1)}, f32[6,200,128]{2,1,0:T(8,128)S(1)}, f32[14,200,128]{2,1,0:T(8,128)S(1)}) custom-call(s32[32,5]{1,0:T(8,128)S(1)} %copy.21.links, s32[32]{0:T(128)S(1)} %copy-done.4, s32[1]{0:T(128)} %bitcast.4.own_slot, ...), custom_call_target="tpu_custom_call" | custom-call | tf_op jit(solution)/shard_map/forward_conv/pallas_call | solution.py:223
  63.5 1.7 %fusion.5 = bf16[800,1024]{1,0:T(8,128)(2,1)S(1)} fusion(f32[1024,800]{0,1:T(8,128)S(1)} %get-tuple-element.39, bf16[200,1024]{1,0:T(8,128)(2,1)S(1)} %get-tuple-element.40, bf16[800,200]{0,1:T(8,128)(2,1)S(1)} %copy-done.10), kind=kOutput, calls=%fused_computation.6 | convolution fusion | flops 335872000 | bytes 5644800 | tf_op jit(solution)/shard_map/hc,cp->hp/dot_general | solution.py:408
  66.5 7.4 %backward_conv.1 = f32[32,88,128]{2,1,0:T(8,128)S(1)} custom-call(s32[1]{0:T(128)} %bitcast.9.me, f32[200,1024]{1,0:T(8,128)S(1)} %convolution_bitcast_fusion.gn_ref, f32[200,1024]{1,0:T(8,128)S(1)} %get-tuple-element.19.cen_ref, f32[8,128]{1,0:T(8,128)S(1)} %get-tuple-element.20.inv_ref, f32[8,200,128]{2,1,0:T(8,128)S(1)} %get-tuple-element.16.own_rows, ...), custom_call_target="tpu_custom_call" | custom-call | tf_op jit(solution)/shard_map/backward_conv/pallas_call | solution.py:295
  74.1 2.2 %collective-permute-done = f32[16,88,128]{2,1,0:T(8,128)S(1)} collective-permute-done((f32[16,88,128]{2,1,0:T(8,128)S(1)}, f32[16,88,128]{2,1,0:T(8,128)S(1)}, u32[]{:S(2)}, u32[]{:S(2)}) %collective-permute-start) | collective-permute-done | bytes 720928 | tf_op jit(solution)/shard_map/ppermute | solution.py:348
  78.1 1.9 %collective-permute-start.2 = (bf16[4,88,128]{2,1,0:T(8,128)(2,1)S(1)}, bf16[4,88,128]{2,1,0:T(8,128)(2,1)S(1)}, u32[]{:S(2)}, u32[]{:S(2)}) collective-permute-start(bf16[4,88,128]{2,1,0:T(8,128)(2,1)S(1)} %get-tuple-element.32), channel_id=1, source_target_pairs={{0,4},{1,5},{2,6},{3,7},{4,0},{5,1},{6,2},{7,3},{8,12},{9,13},{10,... | collective-permute-start | bytes 270344 | tf_op jit(solution)/shard_map/ppermute | solution.py:348
  83.2 2.8 %collective-permute-start.6 = (f32[88,128]{1,0:T(8,128)S(1)}, f32[88,128]{1,0:T(8,128)S(1)}, u32[]{:S(2)}, u32[]{:S(2)}) collective-permute-start(f32[88,128]{1,0:T(8,128)S(1)} %get-tuple-element.33), channel_id=1, source_target_pairs={{0,192},{1,193},{2,194},{3,195},{4,196},{5,197},{6,198},{7,199},{8... | collective-permute-start | bytes 135176 | tf_op jit(solution)/shard_map/ppermute | solution.py:348
  87.4 3.1 %collective-permute-done.5 = f32[88,128]{1,0:T(8,128)S(1)} collective-permute-done((f32[88,128]{1,0:T(8,128)S(1)}, f32[88,128]{1,0:T(8,128)S(1)}, u32[]{:S(2)}, u32[]{:S(2)}) %collective-permute-start.5) | collective-permute-done | bytes 45088 | tf_op jit(solution)/shard_map/ppermute | solution.py:348
  92.3 1.9 %collective-permute-start.7 = (f32[88,128]{1,0:T(8,128)S(1)}, f32[88,128]{1,0:T(8,128)S(1)}, u32[]{:S(2)}, u32[]{:S(2)}) collective-permute-start(f32[88,128]{1,0:T(8,128)S(1)} %fusion.18), channel_id=1, source_target_pairs={{0,8},{1,9},{2,10},{3,11},{4,12},{5,13},{6,14},{7,15},{8,0},{9,1},... | collective-permute-start | bytes 135176 | tf_op jit(solution)/shard_map/ppermute | solution.py:348
  96.3 4.3 %collective-permute-start.10 = (f32[88,128]{1,0:T(8,128)S(1)}, f32[88,128]{1,0:T(8,128)S(1)}, u32[]{:S(2)}, u32[]{:S(2)}) collective-permute-start(f32[88,128]{1,0:T(8,128)S(1)} %add_add_fusion), channel_id=1, source_target_pairs={{0,32},{1,33},{2,34},{3,35},{4,36},{5,37},{6,38},{7,39},{8,40},{9,... | collective-permute-start | bytes 135176 | tf_op jit(solution)/shard_map/ppermute | solution.py:348
  100.6 2.7 %collective-permute-done.10 = f32[88,128]{1,0:T(8,128)S(1)} collective-permute-done((f32[88,128]{1,0:T(8,128)S(1)}, f32[88,128]{1,0:T(8,128)S(1)}, u32[]{:S(2)}, u32[]{:S(2)}) %collective-permute-start.10) | collective-permute-done | bytes 45088 | tf_op jit(solution)/shard_map/ppermute | solution.py:348
  105.1 1.5 %collective-permute-start.11 = (bf16[88,128]{1,0:T(8,128)(2,1)S(1)}, bf16[88,128]{1,0:T(8,128)(2,1)S(1)}, u32[]{:S(2)}, u32[]{:S(2)}) collective-permute-start(bf16[88,128]{1,0:T(8,128)(2,1)S(1)} %add_convert_fusion), channel_id=1, source_target_pairs={{0,64},{1,65},{2,66},{3,67},{4,68},{5,69},{6,70},{7,71},{8,72},{9,... | collective-permute-start | bytes 67592 | tf_op jit(solution)/shard_map/ppermute | solution.py:348
  108.4 1.8 %collective-permute-start.15 = (bf16[4,88,128]{2,1,0:T(8,128)(2,1)S(1)}, bf16[4,88,128]{2,1,0:T(8,128)(2,1)S(1)}, u32[]{:S(2)}, u32[]{:S(2)}) collective-permute-start(bf16[4,88,128]{2,1,0:T(8,128)(2,1)S(1)} %get-tuple-element.37), channel_id=1, source_target_pairs={{0,4},{1,5},{2,6},{3,7},{4,0},{5,1},{6,2},{7,3},{8,12},{9,13},{10,... | collective-permute-start | bytes 270344 | tf_op jit(solution)/shard_map/ppermute | solution.py:348
  111.8 1.6 %collective-permute-done.15 = bf16[4,88,128]{2,1,0:T(8,128)(2,1)S(1)} collective-permute-done((bf16[4,88,128]{2,1,0:T(8,128)(2,1)S(1)}, bf16[4,88,128]{2,1,0:T(8,128)(2,1)S(1)}, u32[]{:S(2)}, u32[]{:S(2)}) %collective-permute-start.15) | collective-permute-done | bytes 90144 | tf_op jit(solution)/shard_map/ppermute | solution.py:348
  113.8 1.6 %collective-permute-done.16 = bf16[4,88,128]{2,1,0:T(8,128)(2,1)S(1)} collective-permute-done((bf16[4,88,128]{2,1,0:T(8,128)(2,1)S(1)}, bf16[4,88,128]{2,1,0:T(8,128)(2,1)S(1)}, u32[]{:S(2)}, u32[]{:S(2)}) %collective-permute-start.16) | collective-permute-done | bytes 90144 | tf_op jit(solution)/shard_map/ppermute | solution.py:348
  115.5 8.7 %collective-permute-start.17 = (bf16[4,4,88,128]{3,2,1,0:T(8,128)(2,1)S(1)}, bf16[4,4,88,128]{3,2,1,0:T(8,128)(2,1)S(1)}, u32[]{:S(2)}, u32[]{:S(2)}) collective-permute-start(bf16[4,4,88,128]{3,2,1,0:T(8,128)(2,1)S(1)} %get-tuple-element.29), channel_id=1, source_target_pairs={{0,1},{1,0},{2,3},{3,2},{4,5},{5,4},{6,7},{7,6},{8,9},{9,8},{10,11... | collective-permute-start | bytes 1081352 | tf_op jit(solution)/shard_map/ppermute | solution.py:348
  (70 shorter events, 25.1 us)
Async XLA Ops:
  0.6 59.8 %copy-start = (bf16[200,800]{1,0:T(8,128)(2,1)S(1)}, bf16[200,800]{1,0:T(8,128)(2,1)}, u32[]{:S(2)}) copy-start(bf16[200,800]{1,0:T(8,128)(2,1)} %param.17) | copy-start | bytes 960004
  0.6 50.6 %copy-start.4 = (s32[32]{0:T(128)S(1)}, s32[32]{0:T(128)}, u32[]{:S(2)}) copy-start(s32[32]{0:T(128)} %owner.3) | copy-start | bytes 388
  0.7 35.7 %copy-start.8 = (f32[200]{0:T(256)S(1)}, f32[200]{0:T(256)}, u32[]{:S(2)}) copy-start(f32[200]{0:T(256)} %param.19) | copy-start | bytes 2404
  0.7 35.9 %copy-start.5 = (bf16[1,1,200,8,128]{4,3,2,1,0:T(8,128)(2,1)S(1)}, bf16[1,1,200,8,128]{4,3,2,1,0:T(8,128)(2,1)}, u32[]{:S(2)}) copy-start(bf16[1,1,200,8,128]{4,3,2,1,0:T(8,128)(2,1)} %param.11) | copy-start | bytes 1228804
  2.9 25.1 %all-to-all-start = ((bf16[32,7,8,128]{3,2,1,0:T(8,128)(2,1)}), bf16[32,7,8,128]{3,2,1,0:T(8,128)(2,1)S(1)}, u32[]{:S(2)}, u32[]{:S(2)}) async-start(bf16[32,7,8,128]{3,2,1,0:T(8,128)(2,1)} %bitcast.5), calls=%async_computation | async-start | bytes 917504 | tf_op jit(solution)/shard_map/all_to_all | solution.py:388
  32.1 19.2 %all-to-all-start.1 = ((bf16[32,7,8,128]{3,2,1,0:T(8,128)(2,1)}), bf16[32,7,8,128]{3,2,1,0:T(8,128)(2,1)S(1)}, u32[]{:S(2)}, u32[]{:S(2)}) async-start(bf16[32,7,8,128]{3,2,1,0:T(8,128)(2,1)} %compose.1), calls=%async_computation.1 | async-start | bytes 917504 | tf_op jit(solution)/shard_map/all_to_all | solution.py:391
  74.0 2.3 %collective-permute-start = (f32[16,88,128]{2,1,0:T(8,128)S(1)}, f32[16,88,128]{2,1,0:T(8,128)S(1)}, u32[]{:S(2)}, u32[]{:S(2)}) collective-permute-start(f32[16,88,128]{2,1,0:T(8,128)S(1)} %slice.52), channel_id=1, source_target_pairs={{0,1},{1,0},{2,3},{3,2},{4,5},{5,4},{6,7},{7,6},{8,9},{9,8},{10,11... | collective-permute-start | bytes 2162696 | tf_op jit(solution)/shard_map/ppermute | solution.py:348
  76.5 4.3 %collective-permute-start.1 = (bf16[4,88,128]{2,1,0:T(8,128)(2,1)S(1)}, bf16[4,88,128]{2,1,0:T(8,128)(2,1)S(1)}, u32[]{:S(2)}, u32[]{:S(2)}) collective-permute-start(bf16[4,88,128]{2,1,0:T(8,128)(2,1)S(1)} %get-tuple-element.30), channel_id=1, source_target_pairs={{0,2},{1,3},{2,0},{3,1},{4,6},{5,7},{6,4},{7,5},{8,10},{9,11},{10,... | collective-permute-start | bytes 270344 | tf_op jit(solution)/shard_map/ppermute | solution.py:348
  77.2 5.0 %collective-permute-start.3 = (bf16[4,88,128]{2,1,0:T(8,128)(2,1)S(1)}, bf16[4,88,128]{2,1,0:T(8,128)(2,1)S(1)}, u32[]{:S(2)}, u32[]{:S(2)}) collective-permute-start(bf16[4,88,128]{2,1,0:T(8,128)(2,1)S(1)} %get-tuple-element.31), channel_id=1, source_target_pairs={{0,6},{1,7},{2,4},{3,5},{4,2},{5,3},{6,0},{7,1},{8,14},{9,15},{10,... | collective-permute-start | bytes 270344 | tf_op jit(solution)/shard_map/ppermute | solution.py:348
  78.1 5.0 %collective-permute-start.2 = (bf16[4,88,128]{2,1,0:T(8,128)(2,1)S(1)}, bf16[4,88,128]{2,1,0:T(8,128)(2,1)S(1)}, u32[]{:S(2)}, u32[]{:S(2)}) collective-permute-start(bf16[4,88,128]{2,1,0:T(8,128)(2,1)S(1)} %get-tuple-element.32), channel_id=1, source_target_pairs={{0,4},{1,5},{2,6},{3,7},{4,0},{5,1},{6,2},{7,3},{8,12},{9,13},{10,... | collective-permute-start | bytes 270344 | tf_op jit(solution)/shard_map/ppermute | solution.py:348
  83.2 4.2 %collective-permute-start.6 = (f32[88,128]{1,0:T(8,128)S(1)}, f32[88,128]{1,0:T(8,128)S(1)}, u32[]{:S(2)}, u32[]{:S(2)}) collective-permute-start(f32[88,128]{1,0:T(8,128)S(1)} %get-tuple-element.33), channel_id=1, source_target_pairs={{0,192},{1,193},{2,194},{3,195},{4,196},{5,197},{6,198},{7,199},{8... | collective-permute-start | bytes 135176 | tf_op jit(solution)/shard_map/ppermute | solution.py:348
  86.0 4.5 %collective-permute-start.5 = (f32[88,128]{1,0:T(8,128)S(1)}, f32[88,128]{1,0:T(8,128)S(1)}, u32[]{:S(2)}, u32[]{:S(2)}) collective-permute-start(f32[88,128]{1,0:T(8,128)S(1)} %get-tuple-element.34), channel_id=1, source_target_pairs={{0,128},{1,129},{2,130},{3,131},{4,132},{5,133},{6,134},{7,135},{8... | collective-permute-start | bytes 135176 | tf_op jit(solution)/shard_map/ppermute | solution.py:348
  86.3 4.2 %collective-permute-start.4 = (f32[88,128]{1,0:T(8,128)S(1)}, f32[88,128]{1,0:T(8,128)S(1)}, u32[]{:S(2)}, u32[]{:S(2)}) collective-permute-start(f32[88,128]{1,0:T(8,128)S(1)} %get-tuple-element.35), channel_id=1, source_target_pairs={{0,64},{1,65},{2,66},{3,67},{4,68},{5,69},{6,70},{7,71},{8,72},{9,... | collective-permute-start | bytes 135176 | tf_op jit(solution)/shard_map/ppermute | solution.py:348
  90.5 4.8 %collective-permute-start.9 = (f32[88,128]{1,0:T(8,128)S(1)}, f32[88,128]{1,0:T(8,128)S(1)}, u32[]{:S(2)}, u32[]{:S(2)}) collective-permute-start(f32[88,128]{1,0:T(8,128)S(1)} %fusion.18), channel_id=1, source_target_pairs={{0,24},{1,25},{2,26},{3,27},{4,28},{5,29},{6,30},{7,31},{8,16},{9,... | collective-permute-start | bytes 135176 | tf_op jit(solution)/shard_map/ppermute | solution.py:348
  91.7 4.6 %collective-permute-start.8 = (f32[88,128]{1,0:T(8,128)S(1)}, f32[88,128]{1,0:T(8,128)S(1)}, u32[]{:S(2)}, u32[]{:S(2)}) collective-permute-start(f32[88,128]{1,0:T(8,128)S(1)} %fusion.18), channel_id=1, source_target_pairs={{0,16},{1,17},{2,18},{3,19},{4,20},{5,21},{6,22},{7,23},{8,24},{9,... | collective-permute-start | bytes 135176 | tf_op jit(solution)/shard_map/ppermute | solution.py:348
  92.3 4.0 %collective-permute-start.7 = (f32[88,128]{1,0:T(8,128)S(1)}, f32[88,128]{1,0:T(8,128)S(1)}, u32[]{:S(2)}, u32[]{:S(2)}) collective-permute-start(f32[88,128]{1,0:T(8,128)S(1)} %fusion.18), channel_id=1, source_target_pairs={{0,8},{1,9},{2,10},{3,11},{4,12},{5,13},{6,14},{7,15},{8,0},{9,1},... | collective-permute-start | bytes 135176 | tf_op jit(solution)/shard_map/ppermute | solution.py:348
  96.3 7.0 %collective-permute-start.10 = (f32[88,128]{1,0:T(8,128)S(1)}, f32[88,128]{1,0:T(8,128)S(1)}, u32[]{:S(2)}, u32[]{:S(2)}) collective-permute-start(f32[88,128]{1,0:T(8,128)S(1)} %add_add_fusion), channel_id=1, source_target_pairs={{0,32},{1,33},{2,34},{3,35},{4,36},{5,37},{6,38},{7,39},{8,40},{9,... | collective-permute-start | bytes 135176 | tf_op jit(solution)/shard_map/ppermute | solution.py:348
  103.3 4.2 %collective-permute-start.13 = (bf16[88,128]{1,0:T(8,128)(2,1)S(1)}, bf16[88,128]{1,0:T(8,128)(2,1)S(1)}, u32[]{:S(2)}, u32[]{:S(2)}) collective-permute-start(bf16[88,128]{1,0:T(8,128)(2,1)S(1)} %add_convert_fusion), channel_id=1, source_target_pairs={{0,192},{1,193},{2,194},{3,195},{4,196},{5,197},{6,198},{7,199},{8... | collective-permute-start | bytes 67592 | tf_op jit(solution)/shard_map/ppermute | solution.py:348
  103.9 4.5 %collective-permute-start.12 = (bf16[88,128]{1,0:T(8,128)(2,1)S(1)}, bf16[88,128]{1,0:T(8,128)(2,1)S(1)}, u32[]{:S(2)}, u32[]{:S(2)}) collective-permute-start(bf16[88,128]{1,0:T(8,128)(2,1)S(1)} %add_convert_fusion), channel_id=1, source_target_pairs={{0,128},{1,129},{2,130},{3,131},{4,132},{5,133},{6,134},{7,135},{8... | collective-permute-start | bytes 67592 | tf_op jit(solution)/shard_map/ppermute | solution.py:348
  105.1 3.3 %collective-permute-start.11 = (bf16[88,128]{1,0:T(8,128)(2,1)S(1)}, bf16[88,128]{1,0:T(8,128)(2,1)S(1)}, u32[]{:S(2)}, u32[]{:S(2)}) collective-permute-start(bf16[88,128]{1,0:T(8,128)(2,1)S(1)} %add_convert_fusion), channel_id=1, source_target_pairs={{0,64},{1,65},{2,66},{3,67},{4,68},{5,69},{6,70},{7,71},{8,72},{9,... | collective-permute-start | bytes 67592 | tf_op jit(solution)/shard_map/ppermute | solution.py:348
  108.4 5.0 %collective-permute-start.15 = (bf16[4,88,128]{2,1,0:T(8,128)(2,1)S(1)}, bf16[4,88,128]{2,1,0:T(8,128)(2,1)S(1)}, u32[]{:S(2)}, u32[]{:S(2)}) collective-permute-start(bf16[4,88,128]{2,1,0:T(8,128)(2,1)S(1)} %get-tuple-element.37), channel_id=1, source_target_pairs={{0,4},{1,5},{2,6},{3,7},{4,0},{5,1},{6,2},{7,3},{8,12},{9,13},{10,... | collective-permute-start | bytes 270344 | tf_op jit(solution)/shard_map/ppermute | solution.py:348
  110.2 3.6 %collective-permute-start.14 = (bf16[4,88,128]{2,1,0:T(8,128)(2,1)S(1)}, bf16[4,88,128]{2,1,0:T(8,128)(2,1)S(1)}, u32[]{:S(2)}, u32[]{:S(2)}) collective-permute-start(bf16[4,88,128]{2,1,0:T(8,128)(2,1)S(1)} %get-tuple-element.37), channel_id=1, source_target_pairs={{0,2},{1,3},{2,0},{3,1},{4,6},{5,7},{6,4},{7,5},{8,10},{9,11},{10,... | collective-permute-start | bytes 270344 | tf_op jit(solution)/shard_map/ppermute | solution.py:348
  110.7 4.8 %collective-permute-start.16 = (bf16[4,88,128]{2,1,0:T(8,128)(2,1)S(1)}, bf16[4,88,128]{2,1,0:T(8,128)(2,1)S(1)}, u32[]{:S(2)}, u32[]{:S(2)}) collective-permute-start(bf16[4,88,128]{2,1,0:T(8,128)(2,1)S(1)} %get-tuple-element.37), channel_id=1, source_target_pairs={{0,6},{1,7},{2,4},{3,5},{4,2},{5,3},{6,0},{7,1},{8,14},{9,15},{10,... | collective-permute-start | bytes 270344 | tf_op jit(solution)/shard_map/ppermute | solution.py:348
  115.5 10.0 %collective-permute-start.17 = (bf16[4,4,88,128]{3,2,1,0:T(8,128)(2,1)S(1)}, bf16[4,4,88,128]{3,2,1,0:T(8,128)(2,1)S(1)}, u32[]{:S(2)}, u32[]{:S(2)}) collective-permute-start(bf16[4,4,88,128]{3,2,1,0:T(8,128)(2,1)S(1)} %get-tuple-element.29), channel_id=1, source_target_pairs={{0,1},{1,0},{2,3},{3,2},{4,5},{5,4},{6,7},{7,6},{8,9},{9,8},{10,11... | collective-permute-start | bytes 1081352 | tf_op jit(solution)/shard_map/ppermute | solution.py:348
  (7 other events, 79.6 us)

commit v3 on v2

--- a/solution.py
+++ b/solution.py
@@ -3,6 +3,7 @@
 from jax import lax
 from jax.experimental import pallas as pl
 from jax.experimental.pallas import tpu as pltpu
+from jax.sharding import Mesh
 from jax.sharding import PartitionSpec as P
 
 LEVELS = 19
@@ -24,7 +25,7 @@
 norm_epsilon = 1e-06
 f32 = jnp.float32
 bf16 = jnp.bfloat16
-AXES = ("ens", "tile")
+TILE = ("zl", "x", "core")
 BIG = 24 << 20
 
 
@@ -39,11 +40,11 @@
     )
 
 
-def link_at(links, tile_id, column):
-    return jnp.where(tile_id >= 0, links[jnp.maximum(tile_id, 0), column], -1)
-
-
-def compose_kernel(links, owner, x_ref, o_ref, inverse):
+def link_at(table, tile_id, column):
+    return jnp.where(tile_id >= 0, table[jnp.maximum(tile_id, 0), column], -1)
+
+
+def compose_kernel(table, x_ref, o_ref, inverse):
     shape = (PARTS, ROWS, COLS)
     row = lax.broadcasted_iota(jnp.int32, shape, 1)
     lane = lax.broadcasted_iota(jnp.int32, shape, 2)
@@ -51,31 +52,31 @@
     east_side = lane < 64
 
     def note(k, _):
-        inverse[owner[k]] = k
+        inverse[table[k, 5]] = k
         return 0
 
     lax.fori_loop(0, TILES, note, 0)
 
     def load(tile_id):
-        slot = jnp.where(tile_id >= 0, owner[jnp.maximum(tile_id, 0)], 0)
+        slot = jnp.maximum(link_at(table, tile_id, 5), 0)
         block = x_ref[slot].astype(f32)
         return jnp.where(tile_id >= 0, block, 0.0)
 
     def north_of(tile_id):
-        block = load(link_at(links, tile_id, 0))
-        return jnp.where(link_at(links, tile_id, 4) == 1, pltpu.roll(block, 3, 1), block)
+        block = load(link_at(table, tile_id, 0))
+        return jnp.where(link_at(table, tile_id, 4) == 1, pltpu.roll(block, 3, 1), block)
 
     def body(d, _):
         own = inverse[d]
-        west = link_at(links, own, 2)
-        east = link_at(links, own, 3)
+        west = link_at(table, own, 2)
+        east = link_at(table, own, 3)
         north_rows = north_of(own)
-        south_rows = load(link_at(links, own, 1))
+        south_rows = load(link_at(table, own, 1))
         sides = jnp.where(edge, jnp.where(east_side, load(east), load(west)), 0.0)
-        north_side = (lane < 64) != (link_at(links, own, 4) == 1)
+        north_side = (lane < 64) != (link_at(table, own, 4) == 1)
         north_corner = jnp.where(north_side, north_of(east), north_of(west))
         south_corner = jnp.where(
-            east_side, load(link_at(links, east, 1)), load(link_at(links, west, 1))
+            east_side, load(link_at(table, east, 1)), load(link_at(table, west, 1))
         )
         corners = jnp.where(row < 3, north_corner, south_corner)
         corners = jnp.where(edge & ((row < 3) | (row > 4)), corners, 0.0)
@@ -90,18 +91,18 @@
     lax.fori_loop(0, TILES, body, 0, unroll=8)
 
 
-def compose(links, owner, chunks):
+def compose(table, chunks):
     smem = pl.BlockSpec(memory_space=pltpu.SMEM)
     vmem = pl.BlockSpec(memory_space=pltpu.VMEM)
     return pl.pallas_call(
         compose_kernel,
         out_shape=jax.ShapeDtypeStruct((TILES, PARTS, ROWS, COLS), bf16),
-        in_specs=[smem, smem, vmem],
+        in_specs=[smem, vmem],
         out_specs=vmem,
         scratch_shapes=[pltpu.SMEM((TILES,), jnp.int32)],
         compiler_params=pltpu.CompilerParams(vmem_limit_bytes=BIG),
         name="compose",
-    )(links, owner, chunks)
+    )(table, chunks)
 
 
 def chosen(center, halo, col_off, lane):
@@ -123,49 +124,98 @@
     return [chosen(x, halo[r, at, :], col_off, lane) for r, x in enumerate(rows)]
 
 
-def prepare_kernel(m_ref, coef, own, wide, flat_ref, mine):
+def prepare_kernel(table, own_slot, m_ref, coef, own, taps, flat_ref, turn_ref, fold_ref, mine, wide, sent):
+    for k in range(TAPS * TAPS):
+        wide[k] = jnp.broadcast_to(coef[:, k : k + 1], (CH, COLS))
+    store = pltpu.make_async_copy(wide, taps, sent)
+    store.start()
     mine[...] = m_ref[0:CH].astype(f32).reshape(CH * ROWS, COLS)
     for r in range(ROWS):
         values = mine[pl.ds(r, CH, stride=ROWS), :]
         own[r] = values
         flat_ref[:, COLS * r : COLS * r + COLS] = values.astype(bf16)
-    for k in range(TAPS * TAPS):
-        wide[k] = jnp.broadcast_to(coef[:, k : k + 1], (CH, COLS))
-
-
-def prepare(payload, coef):
-    vmem = pl.BlockSpec(memory_space=pltpu.VMEM)
+    slot = own_slot[0]
+
+    def find(k, best):
+        return jnp.where(table[k, 5] == slot, k, best)
+
+    fold = table[lax.fori_loop(0, TILES, find, 0), 4] == 1
+    row = lax.broadcasted_iota(jnp.int32, (COLS, COLS), 0)
+    col = lax.broadcasted_iota(jnp.int32, (COLS, COLS), 1)
+    turn_ref[...] = (row == jnp.where(fold, COLS - 1 - col, col)).astype(f32).astype(bf16)
+    fold_ref[...] = jnp.broadcast_to(jnp.where(fold, 1, 0), (8, COLS))
+    store.wait()
+
+
+def prepare(table, own_slot, payload, coef):
+    smem = pl.BlockSpec(memory_space=pltpu.SMEM)
+    vmem = pl.BlockSpec(memory_space=pltpu.VMEM)
+    wide = (TAPS * TAPS, CH, COLS)
     return pl.pallas_call(
         prepare_kernel,
         out_shape=[
             jax.ShapeDtypeStruct((ROWS, CH, COLS), f32),
-            jax.ShapeDtypeStruct((TAPS * TAPS, CH, COLS), f32),
+            jax.ShapeDtypeStruct(wide, f32),
             jax.ShapeDtypeStruct((CH, CELLS), bf16),
-        ],
-        in_specs=[vmem, vmem],
-        out_specs=[vmem] * 3,
-        scratch_shapes=[pltpu.VMEM((CH * ROWS, COLS), f32)],
+            jax.ShapeDtypeStruct((COLS, COLS), bf16),
+            jax.ShapeDtypeStruct((8, COLS), jnp.int32),
+        ],
+        in_specs=[smem, smem, vmem, vmem],
+        out_specs=[vmem, pl.BlockSpec(memory_space=pltpu.HBM), vmem, vmem, vmem],
+        scratch_shapes=[
+            pltpu.VMEM((CH * ROWS, COLS), f32),
+            pltpu.VMEM(wide, f32),
+            pltpu.SemaphoreType.DMA,
+        ],
         compiler_params=pltpu.CompilerParams(vmem_limit_bytes=BIG),
         name="prepare",
-    )(payload, coef)
+    )(table, own_slot, payload, coef)
+
+
+def mask_kernel(fields, wet_levels, o_ref, held, wet_ref, arrived):
+    cuts = (0, 56, 104, 152, CH)
+    levels = pltpu.make_async_copy(wet_levels, wet_ref, arrived.at[4])
+    levels.start()
+    copies = []
+    for n in range(4):
+        span = pl.ds(cuts[n], cuts[n + 1] - cuts[n])
+        copies.append(pltpu.make_async_copy(fields.at[span], held.at[span], arrived.at[n]))
+        copies[n].start()
+    levels.wait()
+    wet = wet_ref[...].astype(f32) * CH
+    for n in range(4):
+        copies[n].wait()
+        for c in range(cuts[n], cuts[n + 1]):
+            value = held[c].astype(f32)
+            o_ref[c] = jnp.where(wet > LEVELS * c, value, 0.0).astype(bf16)
+    o_ref[CH:] = jnp.zeros((TILES * PARTS - CH, ROWS, COLS), bf16)
+
+
+def mask_fields(fields, wet_levels):
+    vmem = pl.BlockSpec(memory_space=pltpu.VMEM)
+    return pl.pallas_call(
+        mask_kernel,
+        out_shape=jax.ShapeDtypeStruct((TILES * PARTS, ROWS, COLS), bf16),
+        in_specs=[pl.BlockSpec(memory_space=pltpu.HBM)] * 2,
+        out_specs=vmem,
+        scratch_shapes=[
+            pltpu.VMEM((CH, ROWS, COLS), bf16),
+            pltpu.VMEM((ROWS, COLS), jnp.int32),
+            pltpu.SemaphoreType.DMA((5,)),
+        ],
+        compiler_params=pltpu.CompilerParams(vmem_limit_bytes=BIG),
+        name="mask_fields",
+    )(*(pltpu.with_memory_space_constraint(x, pltpu.HBM) for x in (fields, wet_levels)))
 
 
 def conv_kernel(
-    links, owner, own_slot, own_rows, taps, r_ref, coef, cen_ref, norm_ref, inv_ref, ext, halo, rims, wide, arrived
+    own_rows, taps, r_ref, coef, turn_ref, fold_ref, cen_ref, norm_ref, inv_ref, ext, halo, rims, wide, arrived
 ):
     fetch = pltpu.make_async_copy(taps, wide, arrived)
     fetch.start()
-    slot = own_slot[0]
-
-    def find(k, best):
-        return jnp.where(owner[k] == slot, k, best)
-
-    own = lax.fori_loop(0, TILES, find, 0)
-    fold = links[own, 4] == 1
+    fold = jnp.broadcast_to(fold_ref[0:1, :], (CH, COLS)) == 1
     rims[...] = r_ref[0:CH].astype(f32).reshape(CH * ROWS, COLS)
-    row = lax.broadcasted_iota(jnp.int32, (COLS, COLS), 0)
-    col = lax.broadcasted_iota(jnp.int32, (COLS, COLS), 1)
-    turn = (row == jnp.where(fold, COLS - 1 - col, col)).astype(f32).astype(bf16)
+    turn = turn_ref[...]
     edges = rims[pl.ds(3, CH, stride=ROWS), :]
     for r in range(11):
         halo[r] = edges if r == 0 else pltpu.roll(edges, COLS - 8 * r, 1)
@@ -210,8 +260,7 @@
         inv_ref[r : r + 1, :] = inv
 
 
-def forward_conv(links, owner, own_slot, own_rows, wide, rims, coef):
-    smem = pl.BlockSpec(memory_space=pltpu.SMEM)
+def forward_conv(own_rows, wide, rims, coef, turn, fold):
     vmem = pl.BlockSpec(memory_space=pltpu.VMEM)
     shapes = [
         ((CH, CELLS), f32),
@@ -223,7 +272,7 @@
     return pl.pallas_call(
         conv_kernel,
         out_shape=[jax.ShapeDtypeStruct(s, d) for s, d in shapes],
-        in_specs=[smem, smem, smem, vmem, pl.BlockSpec(memory_space=pl.ANY), vmem, vmem],
+        in_specs=[vmem, pl.BlockSpec(memory_space=pltpu.HBM), vmem, vmem, vmem, vmem],
         out_specs=[vmem] * len(shapes),
         scratch_shapes=[
             pltpu.VMEM((CH * ROWS, COLS), f32),
@@ -232,7 +281,7 @@
         ],
         compiler_params=pltpu.CompilerParams(vmem_limit_bytes=BIG),
         name="forward_conv",
-    )(links, owner, own_slot, own_rows, wide, rims, coef)
+    )(own_rows, pltpu.with_memory_space_constraint(wide, pltpu.HBM), rims, coef, turn, fold)
 
 
 def grad_kernel(
@@ -272,7 +321,7 @@
         total = jnp.dot(high, ones, preferred_element_type=f32)
         total = total + jnp.dot(low, ones, preferred_element_type=f32)
         found = jnp.where(wide_lane == 32 + k, total, found)
-    place = [chunk ^ me[0] for chunk in range(CHUNKS)]
+    place = [chunk ^ (16 * me[0]) for chunk in range(CHUNKS)]
     blank = jnp.zeros((8, 96), f32)
     for t in range(CHUNKS * SUB):
         source, at = (in_ref, t) if t < TILES_IN else (out_ref, t - TILES_IN)
@@ -306,10 +355,11 @@
     )(me, gn, cen, inv, own_rows, ext, halo, coef, part_in, part_out)
 
 
-def unpack_kernel(me, x_ref, in_ref, out_ref, k_ref, taps):
+def unpack_kernel(me, own_half, other_half, in_ref, out_ref, k_ref, taps):
     share = 1.0 / (8 * TILES * CH * CELLS)
     for chunk in range(CHUNKS):
-        values = x_ref[chunk ^ me[0]].astype(f32) * share
+        mine = me[0] == chunk // 16
+        values = jnp.where(mine, own_half[chunk % 16], other_half[chunk % 16]).astype(f32) * share
         for p in range(SUB):
             t = SUB * chunk + p
             dest, at = (in_ref, t) if t < TILES_IN else (out_ref, t - TILES_IN)
@@ -327,7 +377,7 @@
     k_ref[...] = jnp.transpose(taps[...])[32:81, 0:CH]
 
 
-def unpack(me, gathered):
+def unpack(me, own_half, other_half):
     vmem = pl.BlockSpec(memory_space=pltpu.VMEM)
     return pl.pallas_call(
         unpack_kernel,
@@ -336,30 +386,28 @@
             jax.ShapeDtypeStruct((CH, HID), f32),
             jax.ShapeDtypeStruct((49, CH), f32),
         ],
-        in_specs=[pl.BlockSpec(memory_space=pltpu.SMEM), vmem],
+        in_specs=[pl.BlockSpec(memory_space=pltpu.SMEM), vmem, vmem],
         out_specs=[vmem] * 3,
         scratch_shapes=[pltpu.VMEM((256, COLS), f32)],
         compiler_params=pltpu.CompilerParams(vmem_limit_bytes=BIG),
         name="unpack",
-    )(me, gathered)
-
-
-def swap(values, bits):
-    return lax.ppermute(values, AXES, [(i, i ^ bits) for i in range(256)])
+    )(me, own_half, other_half)
+
+
+def swap(values, axis, bits):
+    size = lax.axis_size(axis)
+    return lax.ppermute(values, axis, [(i, i ^ bits) for i in range(size)])
 
 
 def reduce_all(held):
-    held = (held[:16] + swap(held[16:], 1)).reshape(4, 4, 8 * SUB, COLS)
-    sent = [swap(held[k].astype(bf16), k << 1).astype(f32) for k in (1, 2, 3)]
-    held = (held[0] + sent[0]) + (sent[1] + sent[2])
-    held = (held[0] + swap(held[1], 64)) + (swap(held[2], 128) + swap(held[3], 192))
-    held = (held + swap(held, 8)) + (swap(held, 16) + swap(held, 24))
-    held = held + swap(held, 32)
-    part = held.astype(bf16)
-    part = jnp.stack([part] + [swap(part, k << 6) for k in (1, 2, 3)])
-    part = jnp.stack([part] + [swap(part, k << 1) for k in (1, 2, 3)])
-    part = jnp.stack([part, swap(part, 1)])
-    return part.reshape(CHUNKS, 8 * SUB, COLS)
+    held = held[:16] + swap(held[16:], "core", 1)
+    parts = lax.all_to_all(held.astype(bf16), ("y", "x"), 0, 0, tiled=True)
+    held = jnp.sum(parts.astype(f32), axis=0)
+    held = (held + swap(held, "zl", 1)) + (swap(held, "zl", 2) + swap(held, "zl", 3))
+    held = held + swap(held, "zh", 1)
+    copies = jnp.broadcast_to(held.astype(bf16)[None], (16, 8 * SUB, COLS))
+    half = lax.all_to_all(copies, ("y", "x"), 0, 0, tiled=True)
+    return half, swap(half, "core", 1)
 
 
 def local(
@@ -374,32 +422,25 @@
     weight_out,
     layer_scale,
 ):
-    tile_at = lax.axis_index("tile").astype(jnp.int32)
-    ens_at = lax.axis_index("ens").astype(jnp.int32)
-    own_slot = tile_at.reshape(1)
-    me = ((tile_at & 1) * 16 + ((tile_at >> 1) & 3) * 4 + (ens_at >> 1)).reshape(1)
-    level_of = jnp.arange(TILES * PARTS, dtype=jnp.int32) * LEVELS // CH
-    wet_mask = wet_levels[0][None, :, :] > level_of[:, None, None]
-    own_input = jnp.pad(fields[0, 0], ((0, TILES * PARTS - CH), (0, 0), (0, 0)))
-    payload = jnp.where(wet_mask, own_input, jnp.zeros_like(own_input))
+    own_slot = lax.axis_index(TILE).astype(jnp.int32).reshape(1)
+    me = lax.axis_index("core").astype(jnp.int32).reshape(1)
+    table = jnp.concatenate([tile_links, tile_owner[:, None]], axis=1)
+    level_of = jnp.arange(CH, dtype=jnp.int32) * LEVELS // CH
+    payload = mask_fields(fields[0, 0], wet_levels[0])
     coef = jnp.concatenate([kernel, norm_gain[:, None], layer_scale[:, None]], axis=1)
 
-    own_rows, wide, flat_masked = prepare(payload, coef)
-    chunks = lax.all_to_all(
-        payload.reshape(TILES, PARTS, ROWS, COLS), "tile", 0, 0, tiled=True
-    )
-    rims = lax.all_to_all(compose(tile_links, tile_owner, chunks), "tile", 0, 0, tiled=True)
+    own_rows, wide, flat_masked, turn, fold = prepare(table, own_slot, payload, coef)
+    chunks = lax.all_to_all(payload.reshape(TILES, PARTS, ROWS, COLS), TILE, 0, 0, tiled=True)
+    rims = lax.all_to_all(compose(table, chunks), TILE, 0, 0, tiled=True)
     rims = rims.reshape(TILES * PARTS, ROWS, COLS)
-    centred, flat_norm, inv_std, ext, halo = forward_conv(
-        tile_links, tile_owner, own_slot, own_rows, wide, rims, coef
-    )
+    centred, flat_norm, inv_std, ext, halo = forward_conv(own_rows, wide, rims, coef, turn, fold)
 
     scale_wide = layer_scale[:, None]
     hidden = jnp.einsum("ch,cp->hp", weight_in, flat_norm, preferred_element_type=f32)
     activated = gelu_value(hidden).astype(bf16)
     mlp_out = jnp.einsum("hc,hp->cp", weight_out, activated, preferred_element_type=f32)
     block_out = (flat_masked.astype(f32) + scale_wide * mlp_out).astype(bf16)
-    flat_wet = wet_levels[0].reshape(1, CELLS) > level_of[:CH, None]
+    flat_wet = wet_levels[0].reshape(1, CELLS) > level_of[:, None]
     misfit = jnp.where(
         flat_wet, block_out.astype(f32) - target[0, 0].reshape(CH, CELLS).astype(f32), 0.0
     )
@@ -413,27 +454,18 @@
     packed = backward_conv(
         me, grad_normed, centred, inv_std, own_rows, ext, halo, coef, part_in, part_out
     )
-    grad_in, grad_out, grad_taps = unpack(me, reduce_all(packed))
+    grad_in, grad_out, grad_taps = unpack(me, *reduce_all(packed))
     return block_out.reshape(1, 1, CH, ROWS, COLS), grad_in, grad_out.T, grad_taps.T
 
 
 def solution(mesh):
-    placed = (
-        P("ens", "tile", None, None, None),
-        P("ens", "tile", None, None, None),
-        P("tile", None, None),
-        P(),
-        P(),
-        P(),
-        P(),
-        P(),
-        P(),
-        P(),
-    )
+    fine = Mesh(mesh.devices.reshape(4, 2, 4, 4, 2), ("y", "zh", "zl", "x", "core"))
+    big = P(("y", "zh"), TILE, None, None, None)
+    placed = (big, big, P(TILE, None, None)) + (P(),) * 7
     return jax.shard_map(
         local,
-        mesh=mesh,
+        mesh=fine,
         in_specs=placed,
-        out_specs=(P("ens", "tile", None, None, None), P(), P(), P()),
+        out_specs=(big, P(), P(), P()),
         check_vma=False,
     )

time: 127 us -> 121 us (0.953)
  blocking collectives: 0 us -> 25.1 us
  starting transfers between devices: 44.5 us -> 27.7 us
  waiting for transfers between devices: 43.8 us -> 31 us
  local copies, waits for them, and re-layouts: 7.4 us -> 3.62 us
  Pallas kernels: 21.4 us -> 24.9 us
  other arithmetic: 2.77 us -> 1.11 us
    all_to_all x0 -> x2, blocking collectives: none -> 25.1 us  [the longest x1 14.3 us: reduce_all(): parts = lax.all_to_all(held.astype(bf16), ('y', 'x'), 0, 0, tiled=True)]
    ppermute x18 -> x6, starting transfers between devices: 30.4 us -> 13.6 us  [swap(): return lax.ppermute(values, axis, [(i, i ^ bits) for i in range(size)])]
    ppermute x18 -> x6, waiting for transfers between devices: 19.9 us -> 7.99 us  [swap(): return lax.ppermute(values, axis, [(i, i ^ bits) for i in range(size)])]
    unnamed x25 -> x18, local copies, waits for them, and re-layouts: 7.08 us -> 3.2 us
    select_n x2 -> x1, other arithmetic: 2.16 us -> 0.01 us  [local(): level_of = jnp.arange(CH, dtype=jnp.int32) * LEVELS // CH]
    pallas_call x0 -> x1, Pallas kernels: none -> 1.97 us  [mask_fields(): pl.pallas_call(mask_kernel, out_shape=jax.ShapeDtypeStruct((TILES * PARTS...]
  transfers between devices with their start and end apart: 20 -> 8, of which waited for: 17 -> 7; matrix products, arithmetic and copies ran while one was open for 2% -> 2% of each run, Pallas kernels for 2% -> 3%
where the time goes in v3:
time: 121 us; the launch traced here: 120 us
  waiting for transfers between devices  31 us (26%)
  starting transfers between devices  27.7 us (23%)
  blocking collectives  25.1 us (21%)
  Pallas kernels  24.9 us (21%)
  matrix products  6.1 us (5%)
  local copies, waits for them, and re-layouts  3.62 us (3%)
    all_to_all x1, waiting for transfers between devices, local(): lax.all_to_all(payload.reshape(TILES, PARTS, ROWS, COLS), TILE, 0, 0, til...  14.3 us
    all_to_all x1, blocking collectives, reduce_all(): parts = lax.all_to_all(held.astype(bf16), ('y', 'x'), 0, 0, tiled=True)  14.3 us
    ppermute x6, starting transfers between devices, swap(): return lax.ppermute(values, axis, [(i, i ^ bits) for i in range(size)])  13.6 us
    all_to_all x1, blocking collectives, reduce_all(): half = lax.all_to_all(copies, ('y', 'x'), 0, 0, tiled=True)  10.8 us
    all_to_all x1, starting transfers between devices, local(): lax.all_to_all(payload.reshape(TILES, PARTS, ROWS, COLS), TILE, 0, 0, til...  10 us
    all_to_all x1, waiting for transfers between devices, local(): rims = lax.all_to_all(compose(table, chunks), TILE, 0, 0, tiled=True)  8.71 us
    ppermute x6, waiting for transfers between devices, swap(): return lax.ppermute(values, axis, [(i, i ^ bits) for i in range(size)])  7.99 us
    pallas_call x1, Pallas kernels, backward_conv(): pl.pallas_call(grad_kernel, out_shape=jax.ShapeDtypeStruct((CHUNKS, 8 * S...  7.38 us
  transfers between devices with their start and end apart: 8, of which 7 were waited for; matrix products, arithmetic and copies ran while one was open for 2% of the time, Pallas kernels for 3%

profile of v3, /device:TPU:1, one launch (start us, length us, event | category | flops | bytes accessed | tf_op | source)
XLA Modules:
  0.0 120.5 jit_solution(391930475978719623)
XLA Ops:
  0.7 2.0 %mask_fields.1.m_ref = bf16[224,8,128]{2,1,0:T(8,128)(2,1)} custom-call(bf16[200,8,128]{2,1,0:T(8,128)(2,1)} %bitcast.68, s32[8,128]{1,0:T(8,128)} %bitcast.69), custom_call_target="tpu_custom_call" | custom-call | tf_op jit(solution)/shard_map/mask_fields/pallas_call | solution.py:196
  2.7 10.0 %all-to-all-start = ((bf16[32,7,8,128]{3,2,1,0:T(8,128)(2,1)}), bf16[32,7,8,128]{3,2,1,0:T(8,128)(2,1)S(1)}, u32[]{:S(2)}, u32[]{:S(2)}) async-start(bf16[32,7,8,128]{3,2,1,0:T(8,128)(2,1)} %bitcast.6), calls=%async_computation | async-start | bytes 917504 | tf_op jit(solution)/shard_map/all_to_all | solution.py:433
  13.5 14.3 %all-to-all-done.x_ref = bf16[32,7,8,128]{3,2,1,0:T(8,128)(2,1)S(1)} async-done(((bf16[32,7,8,128]{3,2,1,0:T(8,128)(2,1)}), bf16[32,7,8,128]{3,2,1,0:T(8,128)(2,1)S(1)}, u32[]{:S(2)}, u32[]{:S(2)}) %all-to-all-start) | async-done | bytes 458784 | tf_op jit(solution)/shard_map/all_to_all | solution.py:433
  27.8 3.6 %compose.1 = bf16[32,7,8,128]{3,2,1,0:T(8,128)(2,1)} custom-call(s32[32,6]{1,0:T(8,128)S(1)} %copy.25.table, bf16[32,7,8,128]{3,2,1,0:T(8,128)(2,1)S(1)} %all-to-all-done.x_ref), custom_call_target="tpu_custom_call" | custom-call | tf_op jit(solution)/shard_map/compose/pallas_call | solution.py:97
  31.4 4.0 %all-to-all-start.1 = ((bf16[32,7,8,128]{3,2,1,0:T(8,128)(2,1)}), bf16[32,7,8,128]{3,2,1,0:T(8,128)(2,1)S(1)}, u32[]{:S(2)}, u32[]{:S(2)}) async-start(bf16[32,7,8,128]{3,2,1,0:T(8,128)(2,1)} %compose.1), calls=%async_computation.1 | async-start | bytes 917504 | tf_op jit(solution)/shard_map/all_to_all | solution.py:434
  36.1 3.5 %prepare.1 = (f32[8,200,128]{2,1,0:T(8,128)S(1)}, f32[49,200,128]{2,1,0:T(8,128)S(1)}, bf16[200,1024]{1,0:T(8,128)(2,1)S(1)}, bf16[128,128]{1,0:T(8,128)(2,1)S(1)}, s32[8,128]{1,0:T(8,128)S(1)}) custom-call(s32[32,6]{1,0:T(8,128)S(1)} %copy.25.table, s32[1]{0:T(128)} %bitcast.1.own_slot, bf16[224,8,128]{2,1,0:T(8,128)(2,1)} %mask_fields.1.m_ref, ...), custom_call_target="tpu_custom_call" | custom-call | tf_op jit(solution)/shard_map/prepare/pallas_call | solution.py:154
  39.6 2.2 %copy-done.1 = f32[49,200,128]{2,1,0:T(8,128)} copy-done((f32[49,200,128]{2,1,0:T(8,128)}, f32[49,200,128]{2,1,0:T(8,128)S(1)}, u32[]{:S(2)}) %copy-start.1) | copy-done | bytes 5017624
  41.9 8.7 %all-to-all-done.1 = bf16[32,7,8,128]{3,2,1,0:T(8,128)(2,1)S(1)} async-done(((bf16[32,7,8,128]{3,2,1,0:T(8,128)(2,1)}), bf16[32,7,8,128]{3,2,1,0:T(8,128)(2,1)S(1)}, u32[]{:S(2)}, u32[]{:S(2)}) %all-to-all-start.1) | async-done | bytes 458784 | tf_op jit(solution)/shard_map/all_to_all | solution.py:434
  50.6 7.2 %forward_conv.1 = (f32[200,1024]{1,0:T(8,128)S(1)}, bf16[200,1024]{1,0:T(8,128)(2,1)S(1)}, f32[8,128]{1,0:T(8,128)S(1)}, f32[6,200,128]{2,1,0:T(8,128)S(1)}, f32[14,200,128]{2,1,0:T(8,128)S(1)}) custom-call(f32[8,200,128]{2,1,0:T(8,128)S(1)} %get-tuple-element.18.own_rows, f32[49,200,128]{2,1,0:T(8,128)} %copy-done.1, bf16[224,8,128]{2,1,0:T(8,128)(2,1)S(1)} %bitcast.64, ...), custom_call_target="tpu_custom_call" | custom-call | tf_op jit(solution)/shard_map/forward_conv/pallas_call | solution.py:272
  57.8 1.5 %fusion.7 = (bf16[800,1024]{1,0:T(8,128)(2,1)S(1)}, f32[1024,800]{0,1:T(8,128)S(1)}) fusion(bf16[200,1024]{1,0:T(8,128)(2,1)S(1)} %get-tuple-element.22, bf16[200,800]{1,0:T(8,128)(2,1)S(1)} %copy-done), kind=kOutput, calls=%fused_computation.10 | convolution fusion | flops 331776000 | bytes 5644800 | tf_op jit(solution)/shard_map/ch,cp->hp/dot_general | solution.py:439
  60.9 1.7 %fusion.5 = bf16[800,1024]{1,0:T(8,128)(2,1)S(1)} fusion(f32[1024,800]{0,1:T(8,128)S(1)} %get-tuple-element.31, bf16[200,1024]{1,0:T(8,128)(2,1)S(1)} %get-tuple-element.32, bf16[800,200]{0,1:T(8,128)(2,1)S(1)} %copy-done.7), kind=kOutput, calls=%fused_computation.6 | convolution fusion | flops 335872000 | bytes 5644800 | tf_op jit(solution)/shard_map/hc,cp->hp/dot_general | solution.py:449
  62.6 0.8 fusion.17.in_ref
  64.0 7.4 %backward_conv.1 = f32[32,88,128]{2,1,0:T(8,128)S(1)} custom-call(s32[1]{0:T(128)} %bitcast.10.me, f32[200,1024]{1,0:T(8,128)S(1)} %convolution_bitcast_fusion.gn_ref, f32[200,1024]{1,0:T(8,128)S(1)} %get-tuple-element.23.cen_ref, f32[8,128]{1,0:T(8,128)S(1)} %get-tuple-element.24.inv_ref, f32[8,200,128]{2,1,0:T(8,128)S(1)} %get-tuple-element.18.own_rows, ...), custom_call_target="tpu_custom_call" | custom-call | tf_op jit(solution)/shard_map/backward_conv/pallas_call | solution.py:344
  71.5 2.2 %collective-permute-done = f32[16,88,128]{2,1,0:T(8,128)S(1)} collective-permute-done((f32[16,88,128]{2,1,0:T(8,128)S(1)}, f32[16,88,128]{2,1,0:T(8,128)S(1)}, u32[]{:S(2)}, u32[]{:S(2)}) %collective-permute-start) | collective-permute-done | bytes 720928 | tf_op jit(solution)/shard_map/ppermute | solution.py:399
  73.8 14.3 %all_to_all.20 = bf16[16,88,128]{2,1,0:T(8,128)(2,1)S(1)} all-to-all(bf16[16,88,128]{2,1,0:T(8,128)(2,1)S(1)} %fusion.16), channel_id=1, replica_groups=mesh['y'=4,'zh'=2,'zl'=4,'x'=4,'core'=2] {'y','x'}, dimensions={0} | all-to-all | bytes 720896 | tf_op jit(solution)/shard_map/all_to_all | solution.py:404
  88.4 1.5 %collective-permute-start.2 = (f32[88,128]{1,0:T(8,128)S(1)}, f32[88,128]{1,0:T(8,128)S(1)}, u32[]{:S(2)}, u32[]{:S(2)}) collective-permute-start(f32[88,128]{1,0:T(8,128)S(1)} %convert_reduce_fusion), channel_id=1, source_target_pairs={{0,16},{8,24},{16,0},{24,8},{1,17},{9,25},{17,1},{25,9},{2,18},{10... | collective-permute-start | bytes 135176 | tf_op jit(solution)/shard_map/ppermute | solution.py:399
  89.9 2.1 %collective-permute-start.3 = (f32[88,128]{1,0:T(8,128)S(1)}, f32[88,128]{1,0:T(8,128)S(1)}, u32[]{:S(2)}, u32[]{:S(2)}) collective-permute-start(f32[88,128]{1,0:T(8,128)S(1)} %convert_reduce_fusion), channel_id=1, source_target_pairs={{0,24},{8,16},{16,8},{24,0},{1,25},{9,17},{17,9},{25,1},{2,26},{10... | collective-permute-start | bytes 135176 | tf_op jit(solution)/shard_map/ppermute | solution.py:399
  92.3 2.4 %collective-permute-done.3 = f32[88,128]{1,0:T(8,128)S(1)} collective-permute-done((f32[88,128]{1,0:T(8,128)S(1)}, f32[88,128]{1,0:T(8,128)S(1)}, u32[]{:S(2)}, u32[]{:S(2)}) %collective-permute-start.3) | collective-permute-done | bytes 45088 | tf_op jit(solution)/shard_map/ppermute | solution.py:399
  94.7 4.3 %collective-permute-start.4 = (f32[88,128]{1,0:T(8,128)S(1)}, f32[88,128]{1,0:T(8,128)S(1)}, u32[]{:S(2)}, u32[]{:S(2)}) collective-permute-start(f32[88,128]{1,0:T(8,128)S(1)} %add_add_fusion), channel_id=1, source_target_pairs={{0,32},{32,0},{1,33},{33,1},{2,34},{34,2},{3,35},{35,3},{4,36},{36... | collective-permute-start | bytes 135176 | tf_op jit(solution)/shard_map/ppermute | solution.py:399
  99.0 2.6 %collective-permute-done.4 = f32[88,128]{1,0:T(8,128)S(1)} collective-permute-done((f32[88,128]{1,0:T(8,128)S(1)}, f32[88,128]{1,0:T(8,128)S(1)}, u32[]{:S(2)}, u32[]{:S(2)}) %collective-permute-start.4) | collective-permute-done | bytes 45088 | tf_op jit(solution)/shard_map/ppermute | solution.py:399
  101.7 10.8 %all_to_all.21.own_half = bf16[16,88,128]{2,1,0:T(8,128)(2,1)S(1)} all-to-all(bf16[16,88,128]{2,1,0:T(8,128)(2,1)S(1)} %broadcast_in_dim.25), channel_id=1, replica_groups=mesh['y'=4,'zh'=2,'zl'=4,'x'=4,'core'=2] {'y','x'}, dimensions={0} | all-to-all | bytes 720896 | tf_op jit(solution)/shard_map/all_to_all | solution.py:409
  112.5 5.4 %collective-permute-start.5 = (bf16[16,88,128]{2,1,0:T(8,128)(2,1)S(1)}, bf16[16,88,128]{2,1,0:T(8,128)(2,1)S(1)}, u32[]{:S(2)}, u32[]{:S(2)}) collective-permute-start(bf16[16,88,128]{2,1,0:T(8,128)(2,1)S(1)} %all_to_all.21.own_half), channel_id=1, source_target_pairs={{0,1},{1,0},{2,3},{3,2},{4,5},{5,4},{6,7},{7,6},{8,9},{9,8},{10,11... | collective-permute-start | bytes 1081352 | tf_op jit(solution)/shard_map/ppermute | solution.py:399
  117.9 0.8 copy.27
  119.2 1.2 %unpack.1 = (f32[200,800]{1,0:T(8,128)}, f32[200,800]{1,0:T(8,128)}, f32[49,200]{1,0:T(8,128)}) custom-call(s32[1]{0:T(128)} %bitcast.10.me, bf16[16,88,128]{2,1,0:T(8,128)(2,1)S(1)} %all_to_all.21.own_half, bf16[16,88,128]{2,1,0:T(8,128)(2,1)S(1)} %collective-permute-done.5.other_half), custom_call_target="tpu_custom_call" | custom-call | tf_op jit(solution)/shard_map/unpack/pallas_call | solution.py:382
  (38 shorter events, 5.0 us)
Async XLA Ops:
  0.6 57.2 %copy-start = (bf16[200,800]{1,0:T(8,128)(2,1)S(1)}, bf16[200,800]{1,0:T(8,128)(2,1)}, u32[]{:S(2)}) copy-start(bf16[200,800]{1,0:T(8,128)(2,1)} %param.17) | copy-start | bytes 960004
  0.6 34.8 %copy-start.3 = (f32[200,49]{0,1:T(8,128)S(1)}, f32[200,49]{0,1:T(8,128)}, u32[]{:S(2)}) copy-start(f32[200,49]{0,1:T(8,128)} %param.15) | copy-start | bytes 117604
  0.7 34.9 %copy-start.6 = (f32[200]{0:T(256)S(1)}, f32[200]{0:T(256)}, u32[]{:S(2)}) copy-start(f32[200]{0:T(256)} %param.16) | copy-start | bytes 2404
  0.7 35.1 %copy-start.5 = (f32[200]{0:T(256)S(1)}, f32[200]{0:T(256)}, u32[]{:S(2)}) copy-start(f32[200]{0:T(256)} %param.19) | copy-start | bytes 2404
  0.7 35.2 %copy-start.2 = (bf16[1,1,200,8,128]{4,3,2,1,0:T(8,128)(2,1)S(1)}, bf16[1,1,200,8,128]{4,3,2,1,0:T(8,128)(2,1)}, u32[]{:S(2)}) copy-start(bf16[1,1,200,8,128]{4,3,2,1,0:T(8,128)(2,1)} %param.11) | copy-start | bytes 1228804
  2.7 25.2 %all-to-all-start = ((bf16[32,7,8,128]{3,2,1,0:T(8,128)(2,1)}), bf16[32,7,8,128]{3,2,1,0:T(8,128)(2,1)S(1)}, u32[]{:S(2)}, u32[]{:S(2)}) async-start(bf16[32,7,8,128]{3,2,1,0:T(8,128)(2,1)} %bitcast.6), calls=%async_computation | async-start | bytes 917504 | tf_op jit(solution)/shard_map/all_to_all | solution.py:433
  31.4 19.2 %all-to-all-start.1 = ((bf16[32,7,8,128]{3,2,1,0:T(8,128)(2,1)}), bf16[32,7,8,128]{3,2,1,0:T(8,128)(2,1)S(1)}, u32[]{:S(2)}, u32[]{:S(2)}) async-start(bf16[32,7,8,128]{3,2,1,0:T(8,128)(2,1)} %compose.1), calls=%async_computation.1 | async-start | bytes 917504 | tf_op jit(solution)/shard_map/all_to_all | solution.py:434
  39.6 2.2 %copy-start.1 = (f32[49,200,128]{2,1,0:T(8,128)}, f32[49,200,128]{2,1,0:T(8,128)S(1)}, u32[]{:S(2)}) copy-start(f32[49,200,128]{2,1,0:T(8,128)S(1)} %get-tuple-element.19.taps) | copy-start | bytes 15052804
  57.8 1.6 %copy-start.4 = (s32[1,8,128]{2,1,0:T(8,128)S(1)}, s32[1,8,128]{2,1,0:T(8,128)}, u32[]{:S(2)}) copy-start(s32[1,8,128]{2,1,0:T(8,128)} %param.12) | copy-start | bytes 12292
  57.8 1.6 %copy-start.7 = (bf16[800,200]{0,1:T(8,128)(2,1)S(1)}, bf16[800,200]{0,1:T(8,128)(2,1)}, u32[]{:S(2)}) copy-start(bf16[800,200]{0,1:T(8,128)(2,1)} %param.18) | copy-start | bytes 960004
  71.4 2.3 %collective-permute-start = (f32[16,88,128]{2,1,0:T(8,128)S(1)}, f32[16,88,128]{2,1,0:T(8,128)S(1)}, u32[]{:S(2)}, u32[]{:S(2)}) collective-permute-start(f32[16,88,128]{2,1,0:T(8,128)S(1)} %slice.9), channel_id=1, source_target_pairs={{0,1},{1,0},{2,3},{3,2},{4,5},{5,4},{6,7},{7,6},{8,9},{9,8},{10,11... | collective-permute-start | bytes 2162696 | tf_op jit(solution)/shard_map/ppermute | solution.py:399
  88.2 3.8 %collective-permute-start.1 = (f32[88,128]{1,0:T(8,128)S(1)}, f32[88,128]{1,0:T(8,128)S(1)}, u32[]{:S(2)}, u32[]{:S(2)}) collective-permute-start(f32[88,128]{1,0:T(8,128)S(1)} %convert_reduce_fusion), channel_id=1, source_target_pairs={{0,8},{8,0},{16,24},{24,16},{1,9},{9,1},{17,25},{25,17},{2,10},{10... | collective-permute-start | bytes 135176 | tf_op jit(solution)/shard_map/ppermute | solution.py:399
  88.4 3.9 %collective-permute-start.2 = (f32[88,128]{1,0:T(8,128)S(1)}, f32[88,128]{1,0:T(8,128)S(1)}, u32[]{:S(2)}, u32[]{:S(2)}) collective-permute-start(f32[88,128]{1,0:T(8,128)S(1)} %convert_reduce_fusion), channel_id=1, source_target_pairs={{0,16},{8,24},{16,0},{24,8},{1,17},{9,25},{17,1},{25,9},{2,18},{10... | collective-permute-start | bytes 135176 | tf_op jit(solution)/shard_map/ppermute | solution.py:399
  89.9 4.8 %collective-permute-start.3 = (f32[88,128]{1,0:T(8,128)S(1)}, f32[88,128]{1,0:T(8,128)S(1)}, u32[]{:S(2)}, u32[]{:S(2)}) collective-permute-start(f32[88,128]{1,0:T(8,128)S(1)} %convert_reduce_fusion), channel_id=1, source_target_pairs={{0,24},{8,16},{16,8},{24,0},{1,25},{9,17},{17,9},{25,1},{2,26},{10... | collective-permute-start | bytes 135176 | tf_op jit(solution)/shard_map/ppermute | solution.py:399
  94.7 6.9 %collective-permute-start.4 = (f32[88,128]{1,0:T(8,128)S(1)}, f32[88,128]{1,0:T(8,128)S(1)}, u32[]{:S(2)}, u32[]{:S(2)}) collective-permute-start(f32[88,128]{1,0:T(8,128)S(1)} %add_add_fusion), channel_id=1, source_target_pairs={{0,32},{32,0},{1,33},{33,1},{2,34},{34,2},{3,35},{35,3},{4,36},{36... | collective-permute-start | bytes 135176 | tf_op jit(solution)/shard_map/ppermute | solution.py:399
  112.5 6.7 %collective-permute-start.5 = (bf16[16,88,128]{2,1,0:T(8,128)(2,1)S(1)}, bf16[16,88,128]{2,1,0:T(8,128)(2,1)S(1)}, u32[]{:S(2)}, u32[]{:S(2)}) collective-permute-start(bf16[16,88,128]{2,1,0:T(8,128)(2,1)S(1)} %all_to_all.21.own_half), channel_id=1, source_target_pairs={{0,1},{1,0},{2,3},{3,2},{4,5},{5,4},{6,7},{7,6},{8,9},{9,8},{10,11... | collective-permute-start | bytes 1081352 | tf_op jit(solution)/shard_map/ppermute | solution.py:399

commit v4 on v3

--- a/solution.py
+++ b/solution.py
@@ -26,6 +26,7 @@
 f32 = jnp.float32
 bf16 = jnp.bfloat16
 TILE = ("zl", "x", "core")
+ROUTE = ("core", "x", "zl")
 BIG = 24 << 20
 
 
@@ -182,12 +183,12 @@
         copies.append(pltpu.make_async_copy(fields.at[span], held.at[span], arrived.at[n]))
         copies[n].start()
     levels.wait()
-    wet = wet_ref[...].astype(f32) * CH
+    wet = wet_ref[...].astype(f32).astype(bf16)
+    dry = jnp.zeros((ROWS, COLS), bf16)
     for n in range(4):
         copies[n].wait()
         for c in range(cuts[n], cuts[n + 1]):
-            value = held[c].astype(f32)
-            o_ref[c] = jnp.where(wet > LEVELS * c, value, 0.0).astype(bf16)
+            o_ref[c] = jnp.where(wet > bf16(LEVELS * c // CH), held[c], dry)
     o_ref[CH:] = jnp.zeros((TILES * PARTS - CH, ROWS, COLS), bf16)
 
 
@@ -285,7 +286,7 @@
 
 
 def grad_kernel(
-    me, gn_ref, cen_ref, inv_ref, own_rows, ext, halo, coef, in_ref, out_ref, packed, gconv, terms_ref
+    me, gn_ref, cen_ref, inv_ref, own_rows, ext, halo, coef, in_ref, out_ref, keep, send, gconv, terms_ref
 ):
     gain = jnp.broadcast_to(coef[:, 49:50], (CH, COLS))
     for r in range(ROWS):
@@ -311,31 +312,35 @@
         return 0
 
     lax.fori_loop(0, CH // 8, block, 0)
-    ones = jnp.ones((COLS, COLS), bf16)
+    ones = jnp.ones((2 * COLS, COLS), bf16)
     wide_lane = lax.broadcasted_iota(jnp.int32, (CH, COLS), 1)
     found = jnp.zeros((CH, COLS), f32)
     for k in range(TAPS * TAPS):
         terms = terms_ref[k]
         high = terms.astype(bf16)
         low = (terms - high.astype(f32)).astype(bf16)
-        total = jnp.dot(high, ones, preferred_element_type=f32)
-        total = total + jnp.dot(low, ones, preferred_element_type=f32)
+        both = jnp.concatenate([high, low], axis=1)
+        total = jnp.dot(both, ones, preferred_element_type=f32)
         found = jnp.where(wide_lane == 32 + k, total, found)
-    place = [chunk ^ (16 * me[0]) for chunk in range(CHUNKS)]
     blank = jnp.zeros((8, 96), f32)
-    for t in range(CHUNKS * SUB):
-        source, at = (in_ref, t) if t < TILES_IN else (out_ref, t - TILES_IN)
-        i, l = at // 7, at % 7
-        if i >= CH // 8:
-            tile = jnp.zeros((8, COLS), f32)
-        elif l < 6:
-            tile = source[8 * i : 8 * i + 8, COLS * l : COLS * l + COLS]
-        else:
-            tile = jnp.concatenate([source[8 * i : 8 * i + 8, 6 * COLS : HID], blank], axis=1)
-            if t < TILES_IN:
-                tile = jnp.where(lane < 32, tile, found[8 * i : 8 * i + 8, :])
-        at = 8 * (t % SUB)
-        packed[place[t // SUB], at : at + 8, :] = tile
+
+    def pack(halves):
+        for t in range(CHUNKS * SUB):
+            source, at = (in_ref, t) if t < TILES_IN else (out_ref, t - TILES_IN)
+            i, l = at // 7, at % 7
+            if i >= CH // 8:
+                tile = jnp.zeros((8, COLS), f32)
+            elif l < 6:
+                tile = source[8 * i : 8 * i + 8, COLS * l : COLS * l + COLS]
+            else:
+                tile = jnp.concatenate([source[8 * i : 8 * i + 8, 6 * COLS : HID], blank], axis=1)
+                if t < TILES_IN:
+                    tile = jnp.where(lane < 32, tile, found[8 * i : 8 * i + 8, :])
+            chunk, at = t // SUB, 8 * (t % SUB)
+            halves[chunk // 16][chunk % 16, at : at + 8, :] = tile
+
+    pl.when(me[0] == 0)(lambda: pack((keep, send)))
+    pl.when(me[0] == 1)(lambda: pack((send, keep)))
 
 
 def backward_conv(me, gn, cen, inv, own_rows, ext, halo, coef, part_in, part_out):
@@ -343,9 +348,9 @@
     vmem = pl.BlockSpec(memory_space=pltpu.VMEM)
     return pl.pallas_call(
         grad_kernel,
-        out_shape=jax.ShapeDtypeStruct((CHUNKS, 8 * SUB, COLS), f32),
+        out_shape=[jax.ShapeDtypeStruct((CHUNKS // 2, 8 * SUB, COLS), f32)] * 2,
         in_specs=[smem] + [vmem] * 9,
-        out_specs=vmem,
+        out_specs=[vmem] * 2,
         scratch_shapes=[
             pltpu.VMEM((CH, CELLS), f32),
             pltpu.VMEM((TAPS * TAPS, CH, COLS), f32),
@@ -357,22 +362,26 @@
 
 def unpack_kernel(me, own_half, other_half, in_ref, out_ref, k_ref, taps):
     share = 1.0 / (8 * TILES * CH * CELLS)
-    for chunk in range(CHUNKS):
-        mine = me[0] == chunk // 16
-        values = jnp.where(mine, own_half[chunk % 16], other_half[chunk % 16]).astype(f32) * share
-        for p in range(SUB):
-            t = SUB * chunk + p
-            dest, at = (in_ref, t) if t < TILES_IN else (out_ref, t - TILES_IN)
-            i, l = at // 7, at % 7
-            tile = values[8 * p : 8 * p + 8, :]
-            if i >= CH // 8:
-                continue
-            if l < 6:
-                dest[8 * i : 8 * i + 8, COLS * l : COLS * l + COLS] = tile
-            else:
-                dest[8 * i : 8 * i + 8, 6 * COLS : HID] = tile[:, 0:32]
-                if t < TILES_IN:
-                    taps[8 * i : 8 * i + 8, :] = tile
+
+    def spread(halves):
+        for chunk in range(CHUNKS):
+            values = halves[chunk // 16][chunk % 16].astype(f32) * share
+            for p in range(SUB):
+                t = SUB * chunk + p
+                dest, at = (in_ref, t) if t < TILES_IN else (out_ref, t - TILES_IN)
+                i, l = at // 7, at % 7
+                tile = values[8 * p : 8 * p + 8, :]
+                if i >= CH // 8:
+                    continue
+                if l < 6:
+                    dest[8 * i : 8 * i + 8, COLS * l : COLS * l + COLS] = tile
+                else:
+                    dest[8 * i : 8 * i + 8, 6 * COLS : HID] = tile[:, 0:32]
+                    if t < TILES_IN:
+                        taps[8 * i : 8 * i + 8, :] = tile
+
+    pl.when(me[0] == 0)(lambda: spread((own_half, other_half)))
+    pl.when(me[0] == 1)(lambda: spread((other_half, own_half)))
     taps[CH:256, :] = jnp.zeros((256 - CH, COLS), f32)
     k_ref[...] = jnp.transpose(taps[...])[32:81, 0:CH]
 
@@ -399,14 +408,14 @@
     return lax.ppermute(values, axis, [(i, i ^ bits) for i in range(size)])
 
 
-def reduce_all(held):
-    held = held[:16] + swap(held[16:], "core", 1)
-    parts = lax.all_to_all(held.astype(bf16), ("y", "x"), 0, 0, tiled=True)
+def reduce_all(keep, send):
+    held = keep + swap(send, "core", 1)
+    parts = lax.all_to_all(held.astype(bf16), ("x", "y"), 0, 0, tiled=True)
     held = jnp.sum(parts.astype(f32), axis=0)
     held = (held + swap(held, "zl", 1)) + (swap(held, "zl", 2) + swap(held, "zl", 3))
     held = held + swap(held, "zh", 1)
     copies = jnp.broadcast_to(held.astype(bf16)[None], (16, 8 * SUB, COLS))
-    half = lax.all_to_all(copies, ("y", "x"), 0, 0, tiled=True)
+    half = lax.all_to_all(copies, ("x", "y"), 0, 0, tiled=True)
     return half, swap(half, "core", 1)
 
 
@@ -422,16 +431,17 @@
     weight_out,
     layer_scale,
 ):
-    own_slot = lax.axis_index(TILE).astype(jnp.int32).reshape(1)
+    own_slot = lax.axis_index(ROUTE).astype(jnp.int32).reshape(1)
     me = lax.axis_index("core").astype(jnp.int32).reshape(1)
-    table = jnp.concatenate([tile_links, tile_owner[:, None]], axis=1)
+    place = (tile_owner & 1) * 16 + ((tile_owner >> 1) & 3) * 4 + (tile_owner >> 3)
+    table = jnp.concatenate([tile_links, place[:, None]], axis=1)
     level_of = jnp.arange(CH, dtype=jnp.int32) * LEVELS // CH
     payload = mask_fields(fields[0, 0], wet_levels[0])
     coef = jnp.concatenate([kernel, norm_gain[:, None], layer_scale[:, None]], axis=1)
 
     own_rows, wide, flat_masked, turn, fold = prepare(table, own_slot, payload, coef)
-    chunks = lax.all_to_all(payload.reshape(TILES, PARTS, ROWS, COLS), TILE, 0, 0, tiled=True)
-    rims = lax.all_to_all(compose(table, chunks), TILE, 0, 0, tiled=True)
+    chunks = lax.all_to_all(payload.reshape(TILES, PARTS, ROWS, COLS), ROUTE, 0, 0, tiled=True)
+    rims = lax.all_to_all(compose(table, chunks), ROUTE, 0, 0, tiled=True)
     rims = rims.reshape(TILES * PARTS, ROWS, COLS)
     centred, flat_norm, inv_std, ext, halo = forward_conv(own_rows, wide, rims, coef, turn, fold)
 
@@ -451,10 +461,10 @@
     part_in = jnp.einsum("cp,hp->ch", flat_norm, grad_hidden, preferred_element_type=f32)
     grad_normed = jnp.einsum("ch,hp->cp", weight_in, grad_hidden, preferred_element_type=f32)
 
-    packed = backward_conv(
+    keep, send = backward_conv(
         me, grad_normed, centred, inv_std, own_rows, ext, halo, coef, part_in, part_out
     )
-    grad_in, grad_out, grad_taps = unpack(me, *reduce_all(packed))
+    grad_in, grad_out, grad_taps = unpack(me, *reduce_all(keep, send))
     return block_out.reshape(1, 1, CH, ROWS, COLS), grad_in, grad_out.T, grad_taps.T
 
 

time: 121 us -> 120 us (level)
  waiting for transfers between devices: 31 us -> 27.8 us
  starting transfers between devices: 27.7 us -> 30 us
  Pallas kernels: 24.9 us -> 23.6 us
    all_to_all x2, waiting for transfers between devices: 23 us -> 20.5 us  [the longest x1 12.7 us: local(): lax.all_to_all(payload.reshape(TILES, PARTS, ROWS, COLS), ROUTE, 0, 0, ti...]
    ppermute x6, starting transfers between devices: 13.6 us -> 14.9 us  [swap(): return lax.ppermute(values, axis, [(i, i ^ bits) for i in range(size)])]
    pallas_call x1, Pallas kernels: 7.38 us -> 6.07 us  [backward_conv(): pl.pallas_call(grad_kernel, out_shape=[jax.ShapeDtypeStruct((CHUNKS // 2,...]
where the time goes in v4:
time: 120 us; the launch traced here: 119 us
  starting transfers between devices  30 us (25%)
  waiting for transfers between devices  27.8 us (23%)
  blocking collectives  25.4 us (21%)
  Pallas kernels  23.6 us (20%)
  matrix products  6.09 us (5%)
  local copies, waits for them, and re-layouts  3.57 us (3%)
  other arithmetic  1.76 us (1%)
    ppermute x6, starting transfers between devices, swap(): return lax.ppermute(values, axis, [(i, i ^ bits) for i in range(size)])  14.9 us
    all_to_all x1, blocking collectives, reduce_all(): parts = lax.all_to_all(held.astype(bf16), ('x', 'y'), 0, 0, tiled=True)  14.2 us
    all_to_all x1, waiting for transfers between devices, local(): lax.all_to_all(payload.reshape(TILES, PARTS, ROWS, COLS), ROUTE, 0, 0, ti...  12.7 us
    all_to_all x1, blocking collectives, reduce_all(): half = lax.all_to_all(copies, ('x', 'y'), 0, 0, tiled=True)  11.2 us
    all_to_all x1, starting transfers between devices, local(): lax.all_to_all(payload.reshape(TILES, PARTS, ROWS, COLS), ROUTE, 0, 0, ti...  10 us
    all_to_all x1, waiting for transfers between devices, local(): rims = lax.all_to_all(compose(table, chunks), ROUTE, 0, 0, tiled=True)  7.76 us
    ppermute x6, waiting for transfers between devices, swap(): return lax.ppermute(values, axis, [(i, i ^ bits) for i in range(size)])  7.3 us
    pallas_call x1, Pallas kernels, forward_conv(): pl.pallas_call(conv_kernel, out_shape=[jax.ShapeDtypeStruct(s, d) for s,...  7.19 us
  transfers between devices with their start and end apart: 8, of which 7 were waited for; matrix products, arithmetic and copies ran while one was open for 2% of the time, Pallas kernels for 3%

profile of v4, /device:TPU:1, one launch (start us, length us, event | category | flops | bytes accessed | tf_op | source)
XLA Modules:
  0.0 119.0 jit_solution(15250906822338604348)
XLA Ops:
  0.7 2.0 %mask_fields.1.m_ref = bf16[224,8,128]{2,1,0:T(8,128)(2,1)} custom-call(bf16[200,8,128]{2,1,0:T(8,128)(2,1)} %bitcast.69, s32[8,128]{1,0:T(8,128)} %bitcast.70), custom_call_target="tpu_custom_call" | custom-call | tf_op jit(solution)/shard_map/mask_fields/pallas_call | solution.py:197
  2.7 10.0 %all-to-all-start = ((bf16[32,7,8,128]{3,2,1,0:T(8,128)(2,1)}), bf16[32,7,8,128]{3,2,1,0:T(8,128)(2,1)S(1)}, u32[]{:S(2)}, u32[]{:S(2)}) async-start(bf16[32,7,8,128]{3,2,1,0:T(8,128)(2,1)} %bitcast.6), calls=%async_computation | async-start | bytes 917504 | tf_op jit(solution)/shard_map/all_to_all | solution.py:443
  14.2 12.7 %all-to-all-done.x_ref = bf16[32,7,8,128]{3,2,1,0:T(8,128)(2,1)S(1)} async-done(((bf16[32,7,8,128]{3,2,1,0:T(8,128)(2,1)}), bf16[32,7,8,128]{3,2,1,0:T(8,128)(2,1)S(1)}, u32[]{:S(2)}, u32[]{:S(2)}) %all-to-all-start) | async-done | bytes 458784 | tf_op jit(solution)/shard_map/all_to_all | solution.py:443
  26.9 3.6 %compose.1 = bf16[32,7,8,128]{3,2,1,0:T(8,128)(2,1)} custom-call(s32[32,6]{1,0:T(8,128)S(1)} %copy.25.table, bf16[32,7,8,128]{3,2,1,0:T(8,128)(2,1)S(1)} %all-to-all-done.x_ref), custom_call_target="tpu_custom_call" | custom-call | tf_op jit(solution)/shard_map/compose/pallas_call | solution.py:98
  30.5 5.0 %all-to-all-start.1 = ((bf16[32,7,8,128]{3,2,1,0:T(8,128)(2,1)}), bf16[32,7,8,128]{3,2,1,0:T(8,128)(2,1)S(1)}, u32[]{:S(2)}, u32[]{:S(2)}) async-start(bf16[32,7,8,128]{3,2,1,0:T(8,128)(2,1)} %compose.1), calls=%async_computation.1 | async-start | bytes 917504 | tf_op jit(solution)/shard_map/all_to_all | solution.py:444
  36.1 3.5 %prepare.1 = (f32[8,200,128]{2,1,0:T(8,128)S(1)}, f32[49,200,128]{2,1,0:T(8,128)S(1)}, bf16[200,1024]{1,0:T(8,128)(2,1)S(1)}, bf16[128,128]{1,0:T(8,128)(2,1)S(1)}, s32[8,128]{1,0:T(8,128)S(1)}) custom-call(s32[32,6]{1,0:T(8,128)S(1)} %copy.25.table, s32[1]{0:T(128)} %bitcast.1.own_slot, bf16[224,8,128]{2,1,0:T(8,128)(2,1)} %mask_fields.1.m_ref, ...), custom_call_target="tpu_custom_call" | custom-call | tf_op jit(solution)/shard_map/prepare/pallas_call | solution.py:155
  39.7 2.2 %copy-done.1 = f32[49,200,128]{2,1,0:T(8,128)} copy-done((f32[49,200,128]{2,1,0:T(8,128)}, f32[49,200,128]{2,1,0:T(8,128)S(1)}, u32[]{:S(2)}) %copy-start.1) | copy-done | bytes 5017624
  41.9 7.8 %all-to-all-done.1 = bf16[32,7,8,128]{3,2,1,0:T(8,128)(2,1)S(1)} async-done(((bf16[32,7,8,128]{3,2,1,0:T(8,128)(2,1)}), bf16[32,7,8,128]{3,2,1,0:T(8,128)(2,1)S(1)}, u32[]{:S(2)}, u32[]{:S(2)}) %all-to-all-start.1) | async-done | bytes 458784 | tf_op jit(solution)/shard_map/all_to_all | solution.py:444
  49.7 7.2 %forward_conv.1 = (f32[200,1024]{1,0:T(8,128)S(1)}, bf16[200,1024]{1,0:T(8,128)(2,1)S(1)}, f32[8,128]{1,0:T(8,128)S(1)}, f32[6,200,128]{2,1,0:T(8,128)S(1)}, f32[14,200,128]{2,1,0:T(8,128)S(1)}) custom-call(f32[8,200,128]{2,1,0:T(8,128)S(1)} %get-tuple-element.20.own_rows, f32[49,200,128]{2,1,0:T(8,128)} %copy-done.1, bf16[224,8,128]{2,1,0:T(8,128)(2,1)S(1)} %bitcast.65, ...), custom_call_target="tpu_custom_call" | custom-call | tf_op jit(solution)/shard_map/forward_conv/pallas_call | solution.py:273
  56.9 1.5 %fusion.7 = (bf16[800,1024]{1,0:T(8,128)(2,1)S(1)}, f32[1024,800]{0,1:T(8,128)S(1)}) fusion(bf16[200,1024]{1,0:T(8,128)(2,1)S(1)} %get-tuple-element.24, bf16[200,800]{1,0:T(8,128)(2,1)S(1)} %copy-done), kind=kOutput, calls=%fused_computation.10 | convolution fusion | flops 331776000 | bytes 5644800 | tf_op jit(solution)/shard_map/ch,cp->hp/dot_general | solution.py:449
  60.0 1.7 %fusion.5 = bf16[800,1024]{1,0:T(8,128)(2,1)S(1)} fusion(f32[1024,800]{0,1:T(8,128)S(1)} %get-tuple-element.35, bf16[200,1024]{1,0:T(8,128)(2,1)S(1)} %get-tuple-element.36, bf16[800,200]{0,1:T(8,128)(2,1)S(1)} %copy-done.7), kind=kOutput, calls=%fused_computation.6 | convolution fusion | flops 335872000 | bytes 5644800 | tf_op jit(solution)/shard_map/hc,cp->hp/dot_general | solution.py:459
  63.1 6.1 %backward_conv.1 = (f32[16,88,128]{2,1,0:T(8,128)S(1)}, f32[16,88,128]{2,1,0:T(8,128)S(1)}) custom-call(s32[1]{0:T(128)} %bitcast.10.me, f32[200,1024]{1,0:T(8,128)S(1)} %convolution_bitcast_fusion.gn_ref, f32[200,1024]{1,0:T(8,128)S(1)} %get-tuple-element.25.cen_ref, f32[8,128]{1,0:T(8,128)S(1)} %get-tuple-element.26.inv_ref, ...), custom_call_target="tpu_custom_call" | custom-call | tf_op jit(solution)/shard_map/backward_conv/pallas_call | solution.py:349
  69.2 1.4 %collective-permute-start = (f32[16,88,128]{2,1,0:T(8,128)S(1)}, f32[16,88,128]{2,1,0:T(8,128)S(1)}, u32[]{:S(2)}, u32[]{:S(2)}) collective-permute-start(f32[16,88,128]{2,1,0:T(8,128)S(1)} %get-tuple-element.30), channel_id=1, source_target_pairs={{0,1},{1,0},{2,3},{3,2},{4,5},{5,4},{6,7},{7,6},{8,9},{9,8},{10,11... | collective-permute-start | bytes 2162696 | tf_op jit(solution)/shard_map/ppermute | solution.py:408
  70.6 1.8 %collective-permute-done = f32[16,88,128]{2,1,0:T(8,128)S(1)} collective-permute-done((f32[16,88,128]{2,1,0:T(8,128)S(1)}, f32[16,88,128]{2,1,0:T(8,128)S(1)}, u32[]{:S(2)}, u32[]{:S(2)}) %collective-permute-start) | collective-permute-done | bytes 720928 | tf_op jit(solution)/shard_map/ppermute | solution.py:408
  72.5 14.2 %all_to_all.20 = bf16[16,88,128]{2,1,0:T(8,128)(2,1)S(1)} all-to-all(bf16[16,88,128]{2,1,0:T(8,128)(2,1)S(1)} %add_convert_fusion), channel_id=1, replica_groups=mesh['y'=4,'zh'=2,'zl'=4,'x'=4,'core'=2] {'x','y'}, dimensions={0} | all-to-all | bytes 720896 | tf_op jit(solution)/shard_map/all_to_all | solution.py:413
  86.8 1.2 %collective-permute-start.2 = (f32[88,128]{1,0:T(8,128)S(1)}, f32[88,128]{1,0:T(8,128)S(1)}, u32[]{:S(2)}, u32[]{:S(2)}) collective-permute-start(f32[88,128]{1,0:T(8,128)S(1)} %convert_reduce_fusion), channel_id=1, source_target_pairs={{0,16},{8,24},{16,0},{24,8},{1,17},{9,25},{17,1},{25,9},{2,18},{10... | collective-permute-start | bytes 135176 | tf_op jit(solution)/shard_map/ppermute | solution.py:408
  88.0 2.3 %collective-permute-start.3 = (f32[88,128]{1,0:T(8,128)S(1)}, f32[88,128]{1,0:T(8,128)S(1)}, u32[]{:S(2)}, u32[]{:S(2)}) collective-permute-start(f32[88,128]{1,0:T(8,128)S(1)} %convert_reduce_fusion), channel_id=1, source_target_pairs={{0,24},{8,16},{16,8},{24,0},{1,25},{9,17},{17,9},{25,1},{2,26},{10... | collective-permute-start | bytes 135176 | tf_op jit(solution)/shard_map/ppermute | solution.py:408
  90.7 2.1 %collective-permute-done.3 = f32[88,128]{1,0:T(8,128)S(1)} collective-permute-done((f32[88,128]{1,0:T(8,128)S(1)}, f32[88,128]{1,0:T(8,128)S(1)}, u32[]{:S(2)}, u32[]{:S(2)}) %collective-permute-start.3) | collective-permute-done | bytes 45088 | tf_op jit(solution)/shard_map/ppermute | solution.py:408
  92.8 4.3 %collective-permute-start.4 = (f32[88,128]{1,0:T(8,128)S(1)}, f32[88,128]{1,0:T(8,128)S(1)}, u32[]{:S(2)}, u32[]{:S(2)}) collective-permute-start(f32[88,128]{1,0:T(8,128)S(1)} %add_add_fusion), channel_id=1, source_target_pairs={{0,32},{32,0},{1,33},{33,1},{2,34},{34,2},{3,35},{35,3},{4,36},{36... | collective-permute-start | bytes 135176 | tf_op jit(solution)/shard_map/ppermute | solution.py:408
  97.1 2.6 %collective-permute-done.4 = f32[88,128]{1,0:T(8,128)S(1)} collective-permute-done((f32[88,128]{1,0:T(8,128)S(1)}, f32[88,128]{1,0:T(8,128)S(1)}, u32[]{:S(2)}, u32[]{:S(2)}) %collective-permute-start.4) | collective-permute-done | bytes 45088 | tf_op jit(solution)/shard_map/ppermute | solution.py:408
  99.7 11.2 %all_to_all.21.own_half = bf16[16,88,128]{2,1,0:T(8,128)(2,1)S(1)} all-to-all(bf16[16,88,128]{2,1,0:T(8,128)(2,1)S(1)} %broadcast_in_dim.25), channel_id=1, replica_groups=mesh['y'=4,'zh'=2,'zl'=4,'x'=4,'core'=2] {'x','y'}, dimensions={0} | all-to-all | bytes 720896 | tf_op jit(solution)/shard_map/all_to_all | solution.py:418
  110.9 5.6 %collective-permute-start.5 = (bf16[16,88,128]{2,1,0:T(8,128)(2,1)S(1)}, bf16[16,88,128]{2,1,0:T(8,128)(2,1)S(1)}, u32[]{:S(2)}, u32[]{:S(2)}) collective-permute-start(bf16[16,88,128]{2,1,0:T(8,128)(2,1)S(1)} %all_to_all.21.own_half), channel_id=1, source_target_pairs={{0,1},{1,0},{2,3},{3,2},{4,5},{5,4},{6,7},{7,6},{8,9},{9,8},{10,11... | collective-permute-start | bytes 1081352 | tf_op jit(solution)/shard_map/ppermute | solution.py:408
  116.5 0.8 copy.27
  117.8 1.2 %unpack.1 = (f32[200,800]{1,0:T(8,128)}, f32[200,800]{1,0:T(8,128)}, f32[49,200]{1,0:T(8,128)}) custom-call(s32[1]{0:T(128)} %bitcast.10.me, bf16[16,88,128]{2,1,0:T(8,128)(2,1)S(1)} %all_to_all.21.own_half, bf16[16,88,128]{2,1,0:T(8,128)(2,1)S(1)} %collective-permute-done.5.other_half), custom_call_target="tpu_custom_call" | custom-call | tf_op jit(solution)/shard_map/unpack/pallas_call | solution.py:391
  (38 shorter events, 6.1 us)
Async XLA Ops:
  0.6 56.3 %copy-start = (bf16[200,800]{1,0:T(8,128)(2,1)S(1)}, bf16[200,800]{1,0:T(8,128)(2,1)}, u32[]{:S(2)}) copy-start(bf16[200,800]{1,0:T(8,128)(2,1)} %param.17) | copy-start | bytes 960004
  0.6 34.9 %copy-start.3 = (f32[200,49]{0,1:T(8,128)S(1)}, f32[200,49]{0,1:T(8,128)}, u32[]{:S(2)}) copy-start(f32[200,49]{0,1:T(8,128)} %param.15) | copy-start | bytes 117604
  0.7 35.0 %copy-start.6 = (f32[200]{0:T(256)S(1)}, f32[200]{0:T(256)}, u32[]{:S(2)}) copy-start(f32[200]{0:T(256)} %param.16) | copy-start | bytes 2404
  0.7 35.1 %copy-start.5 = (f32[200]{0:T(256)S(1)}, f32[200]{0:T(256)}, u32[]{:S(2)}) copy-start(f32[200]{0:T(256)} %param.19) | copy-start | bytes 2404
  0.7 35.2 %copy-start.2 = (bf16[1,1,200,8,128]{4,3,2,1,0:T(8,128)(2,1)S(1)}, bf16[1,1,200,8,128]{4,3,2,1,0:T(8,128)(2,1)}, u32[]{:S(2)}) copy-start(bf16[1,1,200,8,128]{4,3,2,1,0:T(8,128)(2,1)} %param.11) | copy-start | bytes 1228804
  2.7 24.2 %all-to-all-start = ((bf16[32,7,8,128]{3,2,1,0:T(8,128)(2,1)}), bf16[32,7,8,128]{3,2,1,0:T(8,128)(2,1)S(1)}, u32[]{:S(2)}, u32[]{:S(2)}) async-start(bf16[32,7,8,128]{3,2,1,0:T(8,128)(2,1)} %bitcast.6), calls=%async_computation | async-start | bytes 917504 | tf_op jit(solution)/shard_map/all_to_all | solution.py:443
  30.5 19.2 %all-to-all-start.1 = ((bf16[32,7,8,128]{3,2,1,0:T(8,128)(2,1)}), bf16[32,7,8,128]{3,2,1,0:T(8,128)(2,1)S(1)}, u32[]{:S(2)}, u32[]{:S(2)}) async-start(bf16[32,7,8,128]{3,2,1,0:T(8,128)(2,1)} %compose.1), calls=%async_computation.1 | async-start | bytes 917504 | tf_op jit(solution)/shard_map/all_to_all | solution.py:444
  39.7 2.2 %copy-start.1 = (f32[49,200,128]{2,1,0:T(8,128)}, f32[49,200,128]{2,1,0:T(8,128)S(1)}, u32[]{:S(2)}) copy-start(f32[49,200,128]{2,1,0:T(8,128)S(1)} %get-tuple-element.21.taps) | copy-start | bytes 15052804
  56.9 1.6 %copy-start.4 = (s32[1,8,128]{2,1,0:T(8,128)S(1)}, s32[1,8,128]{2,1,0:T(8,128)}, u32[]{:S(2)}) copy-start(s32[1,8,128]{2,1,0:T(8,128)} %param.12) | copy-start | bytes 12292
  56.9 1.6 %copy-start.7 = (bf16[800,200]{0,1:T(8,128)(2,1)S(1)}, bf16[800,200]{0,1:T(8,128)(2,1)}, u32[]{:S(2)}) copy-start(bf16[800,200]{0,1:T(8,128)(2,1)} %param.18) | copy-start | bytes 960004
  69.2 3.2 %collective-permute-start = (f32[16,88,128]{2,1,0:T(8,128)S(1)}, f32[16,88,128]{2,1,0:T(8,128)S(1)}, u32[]{:S(2)}, u32[]{:S(2)}) collective-permute-start(f32[16,88,128]{2,1,0:T(8,128)S(1)} %get-tuple-element.30), channel_id=1, source_target_pairs={{0,1},{1,0},{2,3},{3,2},{4,5},{5,4},{6,7},{7,6},{8,9},{9,8},{10,11... | collective-permute-start | bytes 2162696 | tf_op jit(solution)/shard_map/ppermute | solution.py:408
  86.7 3.6 %collective-permute-start.1 = (f32[88,128]{1,0:T(8,128)S(1)}, f32[88,128]{1,0:T(8,128)S(1)}, u32[]{:S(2)}, u32[]{:S(2)}) collective-permute-start(f32[88,128]{1,0:T(8,128)S(1)} %convert_reduce_fusion), channel_id=1, source_target_pairs={{0,8},{8,0},{16,24},{24,16},{1,9},{9,1},{17,25},{25,17},{2,10},{10... | collective-permute-start | bytes 135176 | tf_op jit(solution)/shard_map/ppermute | solution.py:408
  86.8 3.9 %collective-permute-start.2 = (f32[88,128]{1,0:T(8,128)S(1)}, f32[88,128]{1,0:T(8,128)S(1)}, u32[]{:S(2)}, u32[]{:S(2)}) collective-permute-start(f32[88,128]{1,0:T(8,128)S(1)} %convert_reduce_fusion), channel_id=1, source_target_pairs={{0,16},{8,24},{16,0},{24,8},{1,17},{9,25},{17,1},{25,9},{2,18},{10... | collective-permute-start | bytes 135176 | tf_op jit(solution)/shard_map/ppermute | solution.py:408
  88.0 4.7 %collective-permute-start.3 = (f32[88,128]{1,0:T(8,128)S(1)}, f32[88,128]{1,0:T(8,128)S(1)}, u32[]{:S(2)}, u32[]{:S(2)}) collective-permute-start(f32[88,128]{1,0:T(8,128)S(1)} %convert_reduce_fusion), channel_id=1, source_target_pairs={{0,24},{8,16},{16,8},{24,0},{1,25},{9,17},{17,9},{25,1},{2,26},{10... | collective-permute-start | bytes 135176 | tf_op jit(solution)/shard_map/ppermute | solution.py:408
  92.8 6.9 %collective-permute-start.4 = (f32[88,128]{1,0:T(8,128)S(1)}, f32[88,128]{1,0:T(8,128)S(1)}, u32[]{:S(2)}, u32[]{:S(2)}) collective-permute-start(f32[88,128]{1,0:T(8,128)S(1)} %add_add_fusion), channel_id=1, source_target_pairs={{0,32},{32,0},{1,33},{33,1},{2,34},{34,2},{3,35},{35,3},{4,36},{36... | collective-permute-start | bytes 135176 | tf_op jit(solution)/shard_map/ppermute | solution.py:408
  110.9 6.9 %collective-permute-start.5 = (bf16[16,88,128]{2,1,0:T(8,128)(2,1)S(1)}, bf16[16,88,128]{2,1,0:T(8,128)(2,1)S(1)}, u32[]{:S(2)}, u32[]{:S(2)}) collective-permute-start(bf16[16,88,128]{2,1,0:T(8,128)(2,1)S(1)} %all_to_all.21.own_half), channel_id=1, source_target_pairs={{0,1},{1,0},{2,3},{3,2},{4,5},{5,4},{6,7},{7,6},{8,9},{9,8},{10,11... | collective-permute-start | bytes 1081352 | tf_op jit(solution)/shard_map/ppermute | solution.py:408

commit v5 on v4

--- a/solution.py
+++ b/solution.py
@@ -126,8 +126,14 @@
 
 
 def prepare_kernel(table, own_slot, m_ref, coef, own, taps, flat_ref, turn_ref, fold_ref, mine, wide, sent):
-    for k in range(TAPS * TAPS):
-        wide[k] = jnp.broadcast_to(coef[:, k : k + 1], (CH, COLS))
+
+    def widen(i, _):
+        taps_of = coef[pl.ds(pl.multiple_of(8 * i, 8), 8), :]
+        for k in range(TAPS * TAPS):
+            wide[i, k] = jnp.broadcast_to(taps_of[:, k : k + 1], (8, COLS))
+        return 0
+
+    lax.fori_loop(0, CH // 8, widen, 0, unroll=5)
     store = pltpu.make_async_copy(wide, taps, sent)
     store.start()
     mine[...] = m_ref[0:CH].astype(f32).reshape(CH * ROWS, COLS)
@@ -151,7 +157,7 @@
 def prepare(table, own_slot, payload, coef):
     smem = pl.BlockSpec(memory_space=pltpu.SMEM)
     vmem = pl.BlockSpec(memory_space=pltpu.VMEM)
-    wide = (TAPS * TAPS, CH, COLS)
+    wide = (CH // 8, TAPS * TAPS, 8, COLS)
     return pl.pallas_call(
         prepare_kernel,
         out_shape=[
@@ -212,8 +218,11 @@
 def conv_kernel(
     own_rows, taps, r_ref, coef, turn_ref, fold_ref, cen_ref, norm_ref, inv_ref, ext, halo, rims, wide, arrived
 ):
-    fetch = pltpu.make_async_copy(taps, wide, arrived)
-    fetch.start()
+    fetches = []
+    for p in range(5):
+        span = pl.ds(5 * p, 5)
+        fetches.append(pltpu.make_async_copy(taps.at[span], wide.at[span], arrived.at[p]))
+        fetches[p].start()
     fold = jnp.broadcast_to(fold_ref[0:1, :], (CH, COLS)) == 1
     rims[...] = r_ref[0:CH].astype(f32).reshape(CH * ROWS, COLS)
     turn = turn_ref[...]
@@ -228,7 +237,6 @@
             raw = jnp.where(fold, source[2 - t], source[t]).astype(bf16)
             dest[first + t] = jnp.dot(raw, turn, preferred_element_type=f32)
     lane = lax.broadcasted_iota(jnp.int32, (8, COLS), 1)
-    fetch.wait()
 
     def block(i, sums):
         at = pl.ds(pl.multiple_of(8 * i, 8), 8)
@@ -237,7 +245,7 @@
             moved = extended_rows(own_rows, ext, halo, at, b, lane)
             part = [None] * ROWS
             for a in range(TAPS):
-                tap = wide[7 * a + b, at, :]
+                tap = wide[i, 7 * a + b]
                 for r in range(ROWS):
                     term = tap * moved[r + a]
                     part[r] = term if a == 0 else part[r] + term
@@ -247,7 +255,10 @@
             cen_ref[at, COLS * r : COLS * r + COLS] = acc[r]
         return tuple(s + x for s, x in zip(sums, acc))
 
-    sums = lax.fori_loop(0, CH // 8, block, tuple(jnp.zeros((8, COLS), f32) for _ in range(ROWS)))
+    sums = tuple(jnp.zeros((8, COLS), f32) for _ in range(ROWS))
+    for p in range(5):
+        fetches[p].wait()
+        sums = lax.fori_loop(5 * p, 5 * p + 5, block, sums)
     gain = jnp.broadcast_to(coef[:, 49:50], (CH, COLS))
     for r in range(ROWS):
         at = slice(COLS * r, COLS * r + COLS)
@@ -277,8 +288,8 @@
         out_specs=[vmem] * len(shapes),
         scratch_shapes=[
             pltpu.VMEM((CH * ROWS, COLS), f32),
-            pltpu.VMEM((TAPS * TAPS, CH, COLS), f32),
-            pltpu.SemaphoreType.DMA,
+            pltpu.VMEM((CH // 8, TAPS * TAPS, 8, COLS), f32),
+            pltpu.SemaphoreType.DMA((5,)),
         ],
         compiler_params=pltpu.CompilerParams(vmem_limit_bytes=BIG),
         name="forward_conv",
@@ -412,8 +423,9 @@
     held = keep + swap(send, "core", 1)
     parts = lax.all_to_all(held.astype(bf16), ("x", "y"), 0, 0, tiled=True)
     held = jnp.sum(parts.astype(f32), axis=0)
-    held = (held + swap(held, "zl", 1)) + (swap(held, "zl", 2) + swap(held, "zl", 3))
-    held = held + swap(held, "zh", 1)
+    copies = jnp.broadcast_to(held.astype(bf16)[None], (8, 8 * SUB, COLS))
+    parts = lax.all_to_all(copies, ("zl", "zh"), 0, 0, tiled=True)
+    held = jnp.sum(parts.astype(f32), axis=0)
     copies = jnp.broadcast_to(held.astype(bf16)[None], (16, 8 * SUB, COLS))
     half = lax.all_to_all(copies, ("x", "y"), 0, 0, tiled=True)
     return half, swap(half, "core", 1)

time: 120 us -> 116 us (0.967)
  blocking collectives: 25.4 us -> 37.4 us
  starting transfers between devices: 30 us -> 20.9 us
  waiting for transfers between devices: 27.8 us -> 21.7 us
    all_to_all x0 -> x1, blocking collectives: none -> 12.1 us  [reduce_all(): parts = lax.all_to_all(copies, ('zl', 'zh'), 0, 0, tiled=True)]
    ppermute x6 -> x2, starting transfers between devices: 14.9 us -> 5.82 us  [swap(): return lax.ppermute(values, axis, [(i, i ^ bits) for i in range(size)])]
    ppermute x6 -> x2, waiting for transfers between devices: 7.3 us -> 2.3 us  [swap(): return lax.ppermute(values, axis, [(i, i ^ bits) for i in range(size)])]
  transfers between devices with their start and end apart: 8 -> 4, of which waited for: 7 -> 4; matrix products, arithmetic and copies ran while one was open for 2% -> 2% of each run, Pallas kernels for 3% -> 4%
where the time goes in v5:
time: 116 us
  blocking collectives  37.4 us (32%)
  Pallas kernels  23.5 us (20%)
  waiting for transfers between devices  21.7 us (19%)
  starting transfers between devices  20.9 us (18%)
  matrix products  6.09 us (5%)
  local copies, waits for them, and re-layouts  3.6 us (3%)
  other arithmetic  1.77 us (2%)
    all_to_all x1, blocking collectives, reduce_all(): parts = lax.all_to_all(held.astype(bf16), ('x', 'y'), 0, 0, tiled=True)  14.2 us
    all_to_all x1, waiting for transfers between devices, local(): lax.all_to_all(payload.reshape(TILES, PARTS, ROWS, COLS), ROUTE, 0, 0, ti...  12.7 us
    all_to_all x1, blocking collectives, reduce_all(): parts = lax.all_to_all(copies, ('zl', 'zh'), 0, 0, tiled=True)  12.1 us
    all_to_all x1, blocking collectives, reduce_all(): half = lax.all_to_all(copies, ('x', 'y'), 0, 0, tiled=True)  11.1 us
    all_to_all x1, starting transfers between devices, local(): lax.all_to_all(payload.reshape(TILES, PARTS, ROWS, COLS), ROUTE, 0, 0, ti...  10 us
    all_to_all x1, waiting for transfers between devices, local(): rims = lax.all_to_all(compose(table, chunks), ROUTE, 0, 0, tiled=True)  6.71 us
    pallas_call x1, Pallas kernels, forward_conv(): pl.pallas_call(conv_kernel, out_shape=[jax.ShapeDtypeStruct(s, d) for s,...  6.13 us
    pallas_call x1, Pallas kernels, backward_conv(): pl.pallas_call(grad_kernel, out_shape=[jax.ShapeDtypeStruct((CHUNKS // 2,...  6.07 us
  transfers between devices with their start and end apart: 4, of which 4 were waited for; matrix products, arithmetic and copies ran while one was open for 2% of the time, Pallas kernels for 4%

profile of v5, /device:TPU:1, one launch (start us, length us, event | category | flops | bytes accessed | tf_op | source)
XLA Modules:
  0.0 116.0 jit_solution(4147658343974167537)
XLA Ops:
  0.7 2.0 %mask_fields.1.m_ref = bf16[224,8,128]{2,1,0:T(8,128)(2,1)} custom-call(bf16[200,8,128]{2,1,0:T(8,128)(2,1)} %bitcast.69, s32[8,128]{1,0:T(8,128)} %bitcast.70), custom_call_target="tpu_custom_call" | custom-call | tf_op jit(solution)/shard_map/mask_fields/pallas_call | solution.py:203
  2.7 10.0 %all-to-all-start = ((bf16[32,7,8,128]{3,2,1,0:T(8,128)(2,1)}), bf16[32,7,8,128]{3,2,1,0:T(8,128)(2,1)S(1)}, u32[]{:S(2)}, u32[]{:S(2)}) async-start(bf16[32,7,8,128]{3,2,1,0:T(8,128)(2,1)} %bitcast.6), calls=%async_computation | async-start | bytes 917504 | tf_op jit(solution)/shard_map/all_to_all | solution.py:455
  13.4 0.7 pad_add_fusion
  14.2 12.7 %all-to-all-done.x_ref = bf16[32,7,8,128]{3,2,1,0:T(8,128)(2,1)S(1)} async-done(((bf16[32,7,8,128]{3,2,1,0:T(8,128)(2,1)}), bf16[32,7,8,128]{3,2,1,0:T(8,128)(2,1)S(1)}, u32[]{:S(2)}, u32[]{:S(2)}) %all-to-all-start) | async-done | bytes 458784 | tf_op jit(solution)/shard_map/all_to_all | solution.py:455
  26.9 3.6 %compose.1 = bf16[32,7,8,128]{3,2,1,0:T(8,128)(2,1)} custom-call(s32[32,6]{1,0:T(8,128)S(1)} %copy.30.table, bf16[32,7,8,128]{3,2,1,0:T(8,128)(2,1)S(1)} %all-to-all-done.x_ref), custom_call_target="tpu_custom_call" | custom-call | tf_op jit(solution)/shard_map/compose/pallas_call | solution.py:98
  30.5 5.0 %all-to-all-start.1 = ((bf16[32,7,8,128]{3,2,1,0:T(8,128)(2,1)}), bf16[32,7,8,128]{3,2,1,0:T(8,128)(2,1)S(1)}, u32[]{:S(2)}, u32[]{:S(2)}) async-start(bf16[32,7,8,128]{3,2,1,0:T(8,128)(2,1)} %compose.1), calls=%async_computation.1 | async-start | bytes 917504 | tf_op jit(solution)/shard_map/all_to_all | solution.py:456
  36.1 4.6 %prepare.1 = (f32[8,200,128]{2,1,0:T(8,128)S(1)}, f32[25,49,8,128]{3,2,1,0:T(8,128)S(1)}, bf16[200,1024]{1,0:T(8,128)(2,1)S(1)}, bf16[128,128]{1,0:T(8,128)(2,1)S(1)}, s32[8,128]{1,0:T(8,128)S(1)}) custom-call(s32[32,6]{1,0:T(8,128)S(1)} %copy.30.table, s32[1]{0:T(128)} %bitcast.1.own_slot, bf16[224,8,128]{2,1,0:T(8,128)(2,1)} %mask_fields.1.m_ref, ...), custom_call_target="tpu_custom_call" | custom-call | tf_op jit(solution)/shard_map/prepare/pallas_call | solution.py:161
  40.7 2.2 %copy-done.1 = f32[25,49,8,128]{3,2,1,0:T(8,128)} copy-done((f32[25,49,8,128]{3,2,1,0:T(8,128)}, f32[25,49,8,128]{3,2,1,0:T(8,128)S(1)}, u32[]{:S(2)}) %copy-start.1) | copy-done | bytes 5017624
  43.0 6.7 %all-to-all-done.1 = bf16[32,7,8,128]{3,2,1,0:T(8,128)(2,1)S(1)} async-done(((bf16[32,7,8,128]{3,2,1,0:T(8,128)(2,1)}), bf16[32,7,8,128]{3,2,1,0:T(8,128)(2,1)S(1)}, u32[]{:S(2)}, u32[]{:S(2)}) %all-to-all-start.1) | async-done | bytes 458784 | tf_op jit(solution)/shard_map/all_to_all | solution.py:456
  49.7 6.1 %forward_conv.1 = (f32[200,1024]{1,0:T(8,128)S(1)}, bf16[200,1024]{1,0:T(8,128)(2,1)S(1)}, f32[8,128]{1,0:T(8,128)S(1)}, f32[6,200,128]{2,1,0:T(8,128)S(1)}, f32[14,200,128]{2,1,0:T(8,128)S(1)}) custom-call(f32[8,200,128]{2,1,0:T(8,128)S(1)} %get-tuple-element.20.own_rows, f32[25,49,8,128]{3,2,1,0:T(8,128)} %copy-done.1, bf16[224,8,128]{2,1,0:T(8,128)(2,1)S(1)} %bitcast.65, ...), custom_call_target="tpu_custom_call" | custom-call | tf_op jit(solution)/shard_map/forward_conv/pallas_call | solution.py:284
  55.9 1.5 %fusion.7 = (bf16[800,1024]{1,0:T(8,128)(2,1)S(1)}, f32[1024,800]{0,1:T(8,128)S(1)}) fusion(bf16[200,1024]{1,0:T(8,128)(2,1)S(1)} %get-tuple-element.24, bf16[200,800]{1,0:T(8,128)(2,1)S(1)} %copy-done), kind=kOutput, calls=%fused_computation.10 | convolution fusion | flops 331776000 | bytes 5644800 | tf_op jit(solution)/shard_map/ch,cp->hp/dot_general | solution.py:461
  57.4 0.8 fusion.15
  58.2 0.8 fusion.17.out_ref
  58.9 1.7 %fusion.5 = bf16[800,1024]{1,0:T(8,128)(2,1)S(1)} fusion(f32[1024,800]{0,1:T(8,128)S(1)} %get-tuple-element.35, bf16[200,1024]{1,0:T(8,128)(2,1)S(1)} %get-tuple-element.36, bf16[800,200]{0,1:T(8,128)(2,1)S(1)} %copy-done.7), kind=kOutput, calls=%fused_computation.6 | convolution fusion | flops 335872000 | bytes 5644800 | tf_op jit(solution)/shard_map/hc,cp->hp/dot_general | solution.py:471
  60.6 0.8 fusion.16.in_ref
  62.0 6.1 %backward_conv.1 = (f32[16,88,128]{2,1,0:T(8,128)S(1)}, f32[16,88,128]{2,1,0:T(8,128)S(1)}) custom-call(s32[1]{0:T(128)} %bitcast.10.me, f32[200,1024]{1,0:T(8,128)S(1)} %convolution_bitcast_fusion.gn_ref, f32[200,1024]{1,0:T(8,128)S(1)} %get-tuple-element.25.cen_ref, f32[8,128]{1,0:T(8,128)S(1)} %get-tuple-element.26.inv_ref, ...), custom_call_target="tpu_custom_call" | custom-call | tf_op jit(solution)/shard_map/backward_conv/pallas_call | solution.py:360
  68.1 1.4 %collective-permute-start = (f32[16,88,128]{2,1,0:T(8,128)S(1)}, f32[16,88,128]{2,1,0:T(8,128)S(1)}, u32[]{:S(2)}, u32[]{:S(2)}) collective-permute-start(f32[16,88,128]{2,1,0:T(8,128)S(1)} %get-tuple-element.30), channel_id=1, source_target_pairs={{0,1},{1,0},{2,3},{3,2},{4,5},{5,4},{6,7},{7,6},{8,9},{9,8},{10,11... | collective-permute-start | bytes 2162696 | tf_op jit(solution)/shard_map/ppermute | solution.py:419
  69.5 1.8 %collective-permute-done = f32[16,88,128]{2,1,0:T(8,128)S(1)} collective-permute-done((f32[16,88,128]{2,1,0:T(8,128)S(1)}, f32[16,88,128]{2,1,0:T(8,128)S(1)}, u32[]{:S(2)}, u32[]{:S(2)}) %collective-permute-start) | collective-permute-done | bytes 720928 | tf_op jit(solution)/shard_map/ppermute | solution.py:419
  71.4 14.2 %all_to_all.25 = bf16[16,88,128]{2,1,0:T(8,128)(2,1)S(1)} all-to-all(bf16[16,88,128]{2,1,0:T(8,128)(2,1)S(1)} %add_convert_fusion), channel_id=1, replica_groups=mesh['y'=4,'zh'=2,'zl'=4,'x'=4,'core'=2] {'x','y'}, dimensions={0} | all-to-all | bytes 720896 | tf_op jit(solution)/shard_map/all_to_all | solution.py:424
  85.7 12.1 %all_to_all.26 = bf16[8,88,128]{2,1,0:T(8,128)(2,1)S(1)} all-to-all(bf16[8,88,128]{2,1,0:T(8,128)(2,1)S(1)} %broadcast_in_dim.31), channel_id=1, replica_groups=mesh['y'=4,'zh'=2,'zl'=4,'x'=4,'core'=2] {'zl','zh'}, dimensions={0} | all-to-all | bytes 360448 | tf_op jit(solution)/shard_map/all_to_all | solution.py:427
  97.9 11.1 %all_to_all.27.own_half = bf16[16,88,128]{2,1,0:T(8,128)(2,1)S(1)} all-to-all(bf16[16,88,128]{2,1,0:T(8,128)(2,1)S(1)} %broadcast_in_dim.32), channel_id=1, replica_groups=mesh['y'=4,'zh'=2,'zl'=4,'x'=4,'core'=2] {'x','y'}, dimensions={0} | all-to-all | bytes 720896 | tf_op jit(solution)/shard_map/all_to_all | solution.py:430
  109.1 4.4 %collective-permute-start.1 = (bf16[16,88,128]{2,1,0:T(8,128)(2,1)S(1)}, bf16[16,88,128]{2,1,0:T(8,128)(2,1)S(1)}, u32[]{:S(2)}, u32[]{:S(2)}) collective-permute-start(bf16[16,88,128]{2,1,0:T(8,128)(2,1)S(1)} %all_to_all.27.own_half), channel_id=1, source_target_pairs={{0,1},{1,0},{2,3},{3,2},{4,5},{5,4},{6,7},{7,6},{8,9},{9,8},{10,11... | collective-permute-start | bytes 1081352 | tf_op jit(solution)/shard_map/ppermute | solution.py:419
  113.5 0.8 copy.32
  114.8 1.2 %unpack.1 = (f32[200,800]{1,0:T(8,128)}, f32[200,800]{1,0:T(8,128)}, f32[49,200]{1,0:T(8,128)}) custom-call(s32[1]{0:T(128)} %bitcast.10.me, bf16[16,88,128]{2,1,0:T(8,128)(2,1)S(1)} %all_to_all.27.own_half, bf16[16,88,128]{2,1,0:T(8,128)(2,1)S(1)} %collective-permute-done.1.other_half), custom_call_target="tpu_custom_call" | custom-call | tf_op jit(solution)/shard_map/unpack/pallas_call | solution.py:402
  (31 shorter events, 2.7 us)
Async XLA Ops:
  0.6 55.2 %copy-start = (bf16[200,800]{1,0:T(8,128)(2,1)S(1)}, bf16[200,800]{1,0:T(8,128)(2,1)}, u32[]{:S(2)}) copy-start(bf16[200,800]{1,0:T(8,128)(2,1)} %param.17) | copy-start | bytes 960004
  0.6 34.9 %copy-start.3 = (f32[200,49]{0,1:T(8,128)S(1)}, f32[200,49]{0,1:T(8,128)}, u32[]{:S(2)}) copy-start(f32[200,49]{0,1:T(8,128)} %param.15) | copy-start | bytes 117604
  0.7 35.0 %copy-start.6 = (f32[200]{0:T(256)S(1)}, f32[200]{0:T(256)}, u32[]{:S(2)}) copy-start(f32[200]{0:T(256)} %param.16) | copy-start | bytes 2404
  0.7 35.1 %copy-start.5 = (f32[200]{0:T(256)S(1)}, f32[200]{0:T(256)}, u32[]{:S(2)}) copy-start(f32[200]{0:T(256)} %param.19) | copy-start | bytes 2404
  0.7 35.2 %copy-start.2 = (bf16[1,1,200,8,128]{4,3,2,1,0:T(8,128)(2,1)S(1)}, bf16[1,1,200,8,128]{4,3,2,1,0:T(8,128)(2,1)}, u32[]{:S(2)}) copy-start(bf16[1,1,200,8,128]{4,3,2,1,0:T(8,128)(2,1)} %param.11) | copy-start | bytes 1228804
  2.7 24.2 %all-to-all-start = ((bf16[32,7,8,128]{3,2,1,0:T(8,128)(2,1)}), bf16[32,7,8,128]{3,2,1,0:T(8,128)(2,1)S(1)}, u32[]{:S(2)}, u32[]{:S(2)}) async-start(bf16[32,7,8,128]{3,2,1,0:T(8,128)(2,1)} %bitcast.6), calls=%async_computation | async-start | bytes 917504 | tf_op jit(solution)/shard_map/all_to_all | solution.py:455
  30.5 19.2 %all-to-all-start.1 = ((bf16[32,7,8,128]{3,2,1,0:T(8,128)(2,1)}), bf16[32,7,8,128]{3,2,1,0:T(8,128)(2,1)S(1)}, u32[]{:S(2)}, u32[]{:S(2)}) async-start(bf16[32,7,8,128]{3,2,1,0:T(8,128)(2,1)} %compose.1), calls=%async_computation.1 | async-start | bytes 917504 | tf_op jit(solution)/shard_map/all_to_all | solution.py:456
  40.7 2.2 %copy-start.1 = (f32[25,49,8,128]{3,2,1,0:T(8,128)}, f32[25,49,8,128]{3,2,1,0:T(8,128)S(1)}, u32[]{:S(2)}) copy-start(f32[25,49,8,128]{3,2,1,0:T(8,128)S(1)} %get-tuple-element.21.taps) | copy-start | bytes 15052804
  55.8 1.6 %copy-start.4 = (s32[1,8,128]{2,1,0:T(8,128)S(1)}, s32[1,8,128]{2,1,0:T(8,128)}, u32[]{:S(2)}) copy-start(s32[1,8,128]{2,1,0:T(8,128)} %param.12) | copy-start | bytes 12292
  55.8 1.6 %copy-start.7 = (bf16[800,200]{0,1:T(8,128)(2,1)S(1)}, bf16[800,200]{0,1:T(8,128)(2,1)}, u32[]{:S(2)}) copy-start(bf16[800,200]{0,1:T(8,128)(2,1)} %param.18) | copy-start | bytes 960004
  68.1 3.2 %collective-permute-start = (f32[16,88,128]{2,1,0:T(8,128)S(1)}, f32[16,88,128]{2,1,0:T(8,128)S(1)}, u32[]{:S(2)}, u32[]{:S(2)}) collective-permute-start(f32[16,88,128]{2,1,0:T(8,128)S(1)} %get-tuple-element.30), channel_id=1, source_target_pairs={{0,1},{1,0},{2,3},{3,2},{4,5},{5,4},{6,7},{7,6},{8,9},{9,8},{10,11... | collective-permute-start | bytes 2162696 | tf_op jit(solution)/shard_map/ppermute | solution.py:419
  109.1 5.7 %collective-permute-start.1 = (bf16[16,88,128]{2,1,0:T(8,128)(2,1)S(1)}, bf16[16,88,128]{2,1,0:T(8,128)(2,1)S(1)}, u32[]{:S(2)}, u32[]{:S(2)}) collective-permute-start(bf16[16,88,128]{2,1,0:T(8,128)(2,1)S(1)} %all_to_all.27.own_half), channel_id=1, source_target_pairs={{0,1},{1,0},{2,3},{3,2},{4,5},{5,4},{6,7},{7,6},{8,9},{9,8},{10,11... | collective-permute-start | bytes 1081352 | tf_op jit(solution)/shard_map/ppermute | solution.py:419

commit v6 on v5

--- a/solution.py
+++ b/solution.py
@@ -323,15 +323,11 @@
         return 0
 
     lax.fori_loop(0, CH // 8, block, 0)
-    ones = jnp.ones((2 * COLS, COLS), bf16)
+    ones = jnp.ones((COLS, COLS), bf16)
     wide_lane = lax.broadcasted_iota(jnp.int32, (CH, COLS), 1)
     found = jnp.zeros((CH, COLS), f32)
     for k in range(TAPS * TAPS):
-        terms = terms_ref[k]
-        high = terms.astype(bf16)
-        low = (terms - high.astype(f32)).astype(bf16)
-        both = jnp.concatenate([high, low], axis=1)
-        total = jnp.dot(both, ones, preferred_element_type=f32)
+        total = jnp.dot(terms_ref[k].astype(bf16), ones, preferred_element_type=f32)
         found = jnp.where(wide_lane == 32 + k, total, found)
     blank = jnp.zeros((8, 96), f32)
 

time: 116 us -> 116 us (level)
  no operation moved by 1% of the time
where the time goes in v6:
time: 116 us
  blocking collectives  37.4 us (32%)
  Pallas kernels  23.5 us (20%)
  waiting for transfers between devices  21.7 us (19%)
  starting transfers between devices  20.9 us (18%)
  matrix products  6.09 us (5%)
  local copies, waits for them, and re-layouts  3.6 us (3%)
  other arithmetic  1.77 us (2%)
    all_to_all x1, blocking collectives, reduce_all(): parts = lax.all_to_all(held.astype(bf16), ('x', 'y'), 0, 0, tiled=True)  14.2 us
    all_to_all x1, waiting for transfers between devices, local(): lax.all_to_all(payload.reshape(TILES, PARTS, ROWS, COLS), ROUTE, 0, 0, ti...  12.7 us
    all_to_all x1, blocking collectives, reduce_all(): parts = lax.all_to_all(copies, ('zl', 'zh'), 0, 0, tiled=True)  12.1 us
    all_to_all x1, blocking collectives, reduce_all(): half = lax.all_to_all(copies, ('x', 'y'), 0, 0, tiled=True)  11.1 us
    all_to_all x1, starting transfers between devices, local(): lax.all_to_all(payload.reshape(TILES, PARTS, ROWS, COLS), ROUTE, 0, 0, ti...  10 us
    all_to_all x1, waiting for transfers between devices, local(): rims = lax.all_to_all(compose(table, chunks), ROUTE, 0, 0, tiled=True)  6.71 us
    pallas_call x1, Pallas kernels, forward_conv(): pl.pallas_call(conv_kernel, out_shape=[jax.ShapeDtypeStruct(s, d) for s,...  6.13 us
    pallas_call x1, Pallas kernels, backward_conv(): pl.pallas_call(grad_kernel, out_shape=[jax.ShapeDtypeStruct((CHUNKS // 2,...  6.06 us
  transfers between devices with their start and end apart: 4, of which 4 were waited for; matrix products, arithmetic and copies ran while one was open for 2% of the time, Pallas kernels for 4%

profile of v6, /device:TPU:1, one launch (start us, length us, event | category | flops | bytes accessed | tf_op | source)
XLA Modules:
  0.0 116.0 jit_solution(16165900606992104571)
XLA Ops:
  0.7 2.0 %mask_fields.1.m_ref = bf16[224,8,128]{2,1,0:T(8,128)(2,1)} custom-call(bf16[200,8,128]{2,1,0:T(8,128)(2,1)} %bitcast.69, s32[8,128]{1,0:T(8,128)} %bitcast.70), custom_call_target="tpu_custom_call" | custom-call | tf_op jit(solution)/shard_map/mask_fields/pallas_call | solution.py:203
  2.7 10.0 %all-to-all-start = ((bf16[32,7,8,128]{3,2,1,0:T(8,128)(2,1)}), bf16[32,7,8,128]{3,2,1,0:T(8,128)(2,1)S(1)}, u32[]{:S(2)}, u32[]{:S(2)}) async-start(bf16[32,7,8,128]{3,2,1,0:T(8,128)(2,1)} %bitcast.6), calls=%async_computation | async-start | bytes 917504 | tf_op jit(solution)/shard_map/all_to_all | solution.py:451
  13.4 0.7 pad_add_fusion
  14.2 12.7 %all-to-all-done.x_ref = bf16[32,7,8,128]{3,2,1,0:T(8,128)(2,1)S(1)} async-done(((bf16[32,7,8,128]{3,2,1,0:T(8,128)(2,1)}), bf16[32,7,8,128]{3,2,1,0:T(8,128)(2,1)S(1)}, u32[]{:S(2)}, u32[]{:S(2)}) %all-to-all-start) | async-done | bytes 458784 | tf_op jit(solution)/shard_map/all_to_all | solution.py:451
  26.9 3.6 %compose.1 = bf16[32,7,8,128]{3,2,1,0:T(8,128)(2,1)} custom-call(s32[32,6]{1,0:T(8,128)S(1)} %copy.30.table, bf16[32,7,8,128]{3,2,1,0:T(8,128)(2,1)S(1)} %all-to-all-done.x_ref), custom_call_target="tpu_custom_call" | custom-call | tf_op jit(solution)/shard_map/compose/pallas_call | solution.py:98
  30.5 5.0 %all-to-all-start.1 = ((bf16[32,7,8,128]{3,2,1,0:T(8,128)(2,1)}), bf16[32,7,8,128]{3,2,1,0:T(8,128)(2,1)S(1)}, u32[]{:S(2)}, u32[]{:S(2)}) async-start(bf16[32,7,8,128]{3,2,1,0:T(8,128)(2,1)} %compose.1), calls=%async_computation.1 | async-start | bytes 917504 | tf_op jit(solution)/shard_map/all_to_all | solution.py:452
  36.1 4.6 %prepare.1 = (f32[8,200,128]{2,1,0:T(8,128)S(1)}, f32[25,49,8,128]{3,2,1,0:T(8,128)S(1)}, bf16[200,1024]{1,0:T(8,128)(2,1)S(1)}, bf16[128,128]{1,0:T(8,128)(2,1)S(1)}, s32[8,128]{1,0:T(8,128)S(1)}) custom-call(s32[32,6]{1,0:T(8,128)S(1)} %copy.30.table, s32[1]{0:T(128)} %bitcast.1.own_slot, bf16[224,8,128]{2,1,0:T(8,128)(2,1)} %mask_fields.1.m_ref, ...), custom_call_target="tpu_custom_call" | custom-call | tf_op jit(solution)/shard_map/prepare/pallas_call | solution.py:161
  40.7 2.2 %copy-done.1 = f32[25,49,8,128]{3,2,1,0:T(8,128)} copy-done((f32[25,49,8,128]{3,2,1,0:T(8,128)}, f32[25,49,8,128]{3,2,1,0:T(8,128)S(1)}, u32[]{:S(2)}) %copy-start.1) | copy-done | bytes 5017624
  43.0 6.7 %all-to-all-done.1 = bf16[32,7,8,128]{3,2,1,0:T(8,128)(2,1)S(1)} async-done(((bf16[32,7,8,128]{3,2,1,0:T(8,128)(2,1)}), bf16[32,7,8,128]{3,2,1,0:T(8,128)(2,1)S(1)}, u32[]{:S(2)}, u32[]{:S(2)}) %all-to-all-start.1) | async-done | bytes 458784 | tf_op jit(solution)/shard_map/all_to_all | solution.py:452
  49.7 6.1 %forward_conv.1 = (f32[200,1024]{1,0:T(8,128)S(1)}, bf16[200,1024]{1,0:T(8,128)(2,1)S(1)}, f32[8,128]{1,0:T(8,128)S(1)}, f32[6,200,128]{2,1,0:T(8,128)S(1)}, f32[14,200,128]{2,1,0:T(8,128)S(1)}) custom-call(f32[8,200,128]{2,1,0:T(8,128)S(1)} %get-tuple-element.20.own_rows, f32[25,49,8,128]{3,2,1,0:T(8,128)} %copy-done.1, bf16[224,8,128]{2,1,0:T(8,128)(2,1)S(1)} %bitcast.65, ...), custom_call_target="tpu_custom_call" | custom-call | tf_op jit(solution)/shard_map/forward_conv/pallas_call | solution.py:284
  55.9 1.5 %fusion.7 = (bf16[800,1024]{1,0:T(8,128)(2,1)S(1)}, f32[1024,800]{0,1:T(8,128)S(1)}) fusion(bf16[200,1024]{1,0:T(8,128)(2,1)S(1)} %get-tuple-element.24, bf16[200,800]{1,0:T(8,128)(2,1)S(1)} %copy-done), kind=kOutput, calls=%fused_computation.10 | convolution fusion | flops 331776000 | bytes 5644800 | tf_op jit(solution)/shard_map/ch,cp->hp/dot_general | solution.py:457
  57.4 0.8 fusion.15
  58.2 0.8 fusion.17.out_ref
  58.9 1.7 %fusion.5 = bf16[800,1024]{1,0:T(8,128)(2,1)S(1)} fusion(f32[1024,800]{0,1:T(8,128)S(1)} %get-tuple-element.35, bf16[200,1024]{1,0:T(8,128)(2,1)S(1)} %get-tuple-element.36, bf16[800,200]{0,1:T(8,128)(2,1)S(1)} %copy-done.7), kind=kOutput, calls=%fused_computation.6 | convolution fusion | flops 335872000 | bytes 5644800 | tf_op jit(solution)/shard_map/hc,cp->hp/dot_general | solution.py:467
  60.6 0.8 fusion.16.in_ref
  62.0 6.1 %backward_conv.1 = (f32[16,88,128]{2,1,0:T(8,128)S(1)}, f32[16,88,128]{2,1,0:T(8,128)S(1)}) custom-call(s32[1]{0:T(128)} %bitcast.10.me, f32[200,1024]{1,0:T(8,128)S(1)} %convolution_bitcast_fusion.gn_ref, f32[200,1024]{1,0:T(8,128)S(1)} %get-tuple-element.25.cen_ref, f32[8,128]{1,0:T(8,128)S(1)} %get-tuple-element.26.inv_ref, ...), custom_call_target="tpu_custom_call" | custom-call | tf_op jit(solution)/shard_map/backward_conv/pallas_call | solution.py:356
  68.1 1.4 %collective-permute-start = (f32[16,88,128]{2,1,0:T(8,128)S(1)}, f32[16,88,128]{2,1,0:T(8,128)S(1)}, u32[]{:S(2)}, u32[]{:S(2)}) collective-permute-start(f32[16,88,128]{2,1,0:T(8,128)S(1)} %get-tuple-element.30), channel_id=1, source_target_pairs={{0,1},{1,0},{2,3},{3,2},{4,5},{5,4},{6,7},{7,6},{8,9},{9,8},{10,11... | collective-permute-start | bytes 2162696 | tf_op jit(solution)/shard_map/ppermute | solution.py:415
  69.5 1.8 %collective-permute-done = f32[16,88,128]{2,1,0:T(8,128)S(1)} collective-permute-done((f32[16,88,128]{2,1,0:T(8,128)S(1)}, f32[16,88,128]{2,1,0:T(8,128)S(1)}, u32[]{:S(2)}, u32[]{:S(2)}) %collective-permute-start) | collective-permute-done | bytes 720928 | tf_op jit(solution)/shard_map/ppermute | solution.py:415
  71.4 14.2 %all_to_all.25 = bf16[16,88,128]{2,1,0:T(8,128)(2,1)S(1)} all-to-all(bf16[16,88,128]{2,1,0:T(8,128)(2,1)S(1)} %add_convert_fusion), channel_id=1, replica_groups=mesh['y'=4,'zh'=2,'zl'=4,'x'=4,'core'=2] {'x','y'}, dimensions={0} | all-to-all | bytes 720896 | tf_op jit(solution)/shard_map/all_to_all | solution.py:420
  85.7 12.1 %all_to_all.26 = bf16[8,88,128]{2,1,0:T(8,128)(2,1)S(1)} all-to-all(bf16[8,88,128]{2,1,0:T(8,128)(2,1)S(1)} %broadcast_in_dim.31), channel_id=1, replica_groups=mesh['y'=4,'zh'=2,'zl'=4,'x'=4,'core'=2] {'zl','zh'}, dimensions={0} | all-to-all | bytes 360448 | tf_op jit(solution)/shard_map/all_to_all | solution.py:423
  97.9 11.1 %all_to_all.27.own_half = bf16[16,88,128]{2,1,0:T(8,128)(2,1)S(1)} all-to-all(bf16[16,88,128]{2,1,0:T(8,128)(2,1)S(1)} %broadcast_in_dim.32), channel_id=1, replica_groups=mesh['y'=4,'zh'=2,'zl'=4,'x'=4,'core'=2] {'x','y'}, dimensions={0} | all-to-all | bytes 720896 | tf_op jit(solution)/shard_map/all_to_all | solution.py:426
  109.0 4.4 %collective-permute-start.1 = (bf16[16,88,128]{2,1,0:T(8,128)(2,1)S(1)}, bf16[16,88,128]{2,1,0:T(8,128)(2,1)S(1)}, u32[]{:S(2)}, u32[]{:S(2)}) collective-permute-start(bf16[16,88,128]{2,1,0:T(8,128)(2,1)S(1)} %all_to_all.27.own_half), channel_id=1, source_target_pairs={{0,1},{1,0},{2,3},{3,2},{4,5},{5,4},{6,7},{7,6},{8,9},{9,8},{10,11... | collective-permute-start | bytes 1081352 | tf_op jit(solution)/shard_map/ppermute | solution.py:415
  113.5 0.8 copy.32
  114.8 1.2 %unpack.1 = (f32[200,800]{1,0:T(8,128)}, f32[200,800]{1,0:T(8,128)}, f32[49,200]{1,0:T(8,128)}) custom-call(s32[1]{0:T(128)} %bitcast.10.me, bf16[16,88,128]{2,1,0:T(8,128)(2,1)S(1)} %all_to_all.27.own_half, bf16[16,88,128]{2,1,0:T(8,128)(2,1)S(1)} %collective-permute-done.1.other_half), custom_call_target="tpu_custom_call" | custom-call | tf_op jit(solution)/shard_map/unpack/pallas_call | solution.py:398
  (31 shorter events, 2.7 us)
Async XLA Ops:
  0.6 55.2 %copy-start = (bf16[200,800]{1,0:T(8,128)(2,1)S(1)}, bf16[200,800]{1,0:T(8,128)(2,1)}, u32[]{:S(2)}) copy-start(bf16[200,800]{1,0:T(8,128)(2,1)} %param.17) | copy-start | bytes 960004
  0.6 34.9 %copy-start.3 = (f32[200,49]{0,1:T(8,128)S(1)}, f32[200,49]{0,1:T(8,128)}, u32[]{:S(2)}) copy-start(f32[200,49]{0,1:T(8,128)} %param.15) | copy-start | bytes 117604
  0.7 35.0 %copy-start.6 = (f32[200]{0:T(256)S(1)}, f32[200]{0:T(256)}, u32[]{:S(2)}) copy-start(f32[200]{0:T(256)} %param.16) | copy-start | bytes 2404
  0.7 35.1 %copy-start.5 = (f32[200]{0:T(256)S(1)}, f32[200]{0:T(256)}, u32[]{:S(2)}) copy-start(f32[200]{0:T(256)} %param.19) | copy-start | bytes 2404
  0.7 35.2 %copy-start.2 = (bf16[1,1,200,8,128]{4,3,2,1,0:T(8,128)(2,1)S(1)}, bf16[1,1,200,8,128]{4,3,2,1,0:T(8,128)(2,1)}, u32[]{:S(2)}) copy-start(bf16[1,1,200,8,128]{4,3,2,1,0:T(8,128)(2,1)} %param.11) | copy-start | bytes 1228804
  2.7 24.2 %all-to-all-start = ((bf16[32,7,8,128]{3,2,1,0:T(8,128)(2,1)}), bf16[32,7,8,128]{3,2,1,0:T(8,128)(2,1)S(1)}, u32[]{:S(2)}, u32[]{:S(2)}) async-start(bf16[32,7,8,128]{3,2,1,0:T(8,128)(2,1)} %bitcast.6), calls=%async_computation | async-start | bytes 917504 | tf_op jit(solution)/shard_map/all_to_all | solution.py:451
  30.5 19.2 %all-to-all-start.1 = ((bf16[32,7,8,128]{3,2,1,0:T(8,128)(2,1)}), bf16[32,7,8,128]{3,2,1,0:T(8,128)(2,1)S(1)}, u32[]{:S(2)}, u32[]{:S(2)}) async-start(bf16[32,7,8,128]{3,2,1,0:T(8,128)(2,1)} %compose.1), calls=%async_computation.1 | async-start | bytes 917504 | tf_op jit(solution)/shard_map/all_to_all | solution.py:452
  40.7 2.2 %copy-start.1 = (f32[25,49,8,128]{3,2,1,0:T(8,128)}, f32[25,49,8,128]{3,2,1,0:T(8,128)S(1)}, u32[]{:S(2)}) copy-start(f32[25,49,8,128]{3,2,1,0:T(8,128)S(1)} %get-tuple-element.21.taps) | copy-start | bytes 15052804
  55.8 1.6 %copy-start.4 = (s32[1,8,128]{2,1,0:T(8,128)S(1)}, s32[1,8,128]{2,1,0:T(8,128)}, u32[]{:S(2)}) copy-start(s32[1,8,128]{2,1,0:T(8,128)} %param.12) | copy-start | bytes 12292
  55.8 1.6 %copy-start.7 = (bf16[800,200]{0,1:T(8,128)(2,1)S(1)}, bf16[800,200]{0,1:T(8,128)(2,1)}, u32[]{:S(2)}) copy-start(bf16[800,200]{0,1:T(8,128)(2,1)} %param.18) | copy-start | bytes 960004
  68.1 3.2 %collective-permute-start = (f32[16,88,128]{2,1,0:T(8,128)S(1)}, f32[16,88,128]{2,1,0:T(8,128)S(1)}, u32[]{:S(2)}, u32[]{:S(2)}) collective-permute-start(f32[16,88,128]{2,1,0:T(8,128)S(1)} %get-tuple-element.30), channel_id=1, source_target_pairs={{0,1},{1,0},{2,3},{3,2},{4,5},{5,4},{6,7},{7,6},{8,9},{9,8},{10,11... | collective-permute-start | bytes 2162696 | tf_op jit(solution)/shard_map/ppermute | solution.py:415
  109.0 5.7 %collective-permute-start.1 = (bf16[16,88,128]{2,1,0:T(8,128)(2,1)S(1)}, bf16[16,88,128]{2,1,0:T(8,128)(2,1)S(1)}, u32[]{:S(2)}, u32[]{:S(2)}) collective-permute-start(bf16[16,88,128]{2,1,0:T(8,128)(2,1)S(1)} %all_to_all.27.own_half), channel_id=1, source_target_pairs={{0,1},{1,0},{2,3},{3,2},{4,5},{5,4},{6,7},{7,6},{8,9},{9,8},{10,11... | collective-permute-start | bytes 1081352 | tf_op jit(solution)/shard_map/ppermute | solution.py:415
